TPU v7x, 512 devices: a whole 4x4x16 slice. The times are simulated.
512 devices in a mesh: tm: 16 (over x, y), space: 32 (over z, core).
Axes of the slice: x: 4, y: 4, z: 16, core: 2. Of those that a mesh axis runs over, the one named last changes fastest.
Arguments:
- start_values: float32 [16, 256, 128, 128], P('tm', 'space'), may hold values from -6 to 6
- regions: int32 [256, 128, 128], P('space'), may hold values from 0 to 3
- resistivity: float32 [4], replicated, may hold values from 0.1 to 1
Outputs:
- slice_ends: float32 [16, 256, 128, 128], P('tm', 'space')
All inputs are finite; a program needn't handle non-finite values.
Results may differ from a plain program's by a relative error of at most 0.0003.
Values sent between devices are 32-bit elements; how exact they have to be, the bound alone decides.
No kernel may reach another device: no remote copies, remote signals or barrier semaphores. Data moves between devices by JAX's collectives and lax.ppermute only.
A program may use at most 64 MiB of HBM per device.

v0:
```python
import jax
import jax.numpy as jnp
from jax import lax
from jax.sharding import PartitionSpec as P

STEPS = 8


fine_step = 0.008


def padded(block, sides, width):
    for axis, dim in sides:
        count = lax.axis_size(axis)
        forward = [(i, i + 1) for i in range(count - 1)]
        backward = [(target, source) for source, target in forward]
        low = lax.ppermute(
            lax.slice_in_dim(block, block.shape[dim] - width, None, axis=dim), axis, forward
        )
        high = lax.ppermute(lax.slice_in_dim(block, 0, width, axis=dim), axis, backward)
        block = jnp.concatenate([low, block, high], axis=dim)
    return block


def passed_along(value, axis, steps):
    count = lax.axis_size(axis)
    initial, last = (max(0, -steps), min(count, count - steps))
    return lax.ppermute(value, axis, [(source, source + steps) for source in range(initial, last)])


def lookup(regions, resistivity):
    result = jnp.zeros(regions.shape, jnp.float32)
    for region in range(resistivity.shape[0]):
        result = result + jnp.where(regions == region, resistivity[region], jnp.float32(0.0))
    return result


def conduct(field_pad, resist_pad, step_size):
    squared = field_pad * field_pad
    coeff = resist_pad * (1.0 + squared / (1.0 + squared))
    center = field_pad[1:-1, 1:-1, 1:-1]
    coeff_mid = coeff[1:-1, 1:-1, 1:-1]
    flux_sum = jnp.zeros_like(center)
    for axis_dim in range(3):
        for offset in (0, 2):
            index_list = [slice(1, -1)] * 3
            index_list[axis_dim] = slice(offset, offset + center.shape[axis_dim])
            neighbor = field_pad[tuple(index_list)]
            neighbor_coeff = coeff[tuple(index_list)]
            flux_sum = flux_sum + 0.5 * (coeff_mid + neighbor_coeff) * (neighbor - center)
    return center + step_size * flux_sum


def pad_slab(field):
    return jnp.pad(field, ((0, 0), (1, 1), (1, 1)))


def per_device(start_values, regions, resistivity):
    resist = lookup(regions, resistivity)
    coarse_step = fine_step * STEPS
    start = start_values[0]
    resist_pad = pad_slab(padded(resist, (("space", 0),), 1))
    start_pad = pad_slab(padded(start, (("space", 0),), 1))
    field = conduct(start_pad, resist_pad, fine_step)
    for repeat in range(STEPS - 1):
        field_rim = padded(field, (("space", 0),), 1)
        field = conduct(pad_slab(field_rim), resist_pad, fine_step)
    guess = conduct(start_pad, resist_pad, coarse_step)
    first = lax.axis_index("tm") == 0
    sent = jnp.where(first, field, field - guess)

    def relay_turn(turn, carry):
        incoming = passed_along(carry, "tm", 1)
        incoming_rim = padded(incoming, (("space", 0),), 1)
        advanced = conduct(pad_slab(incoming_rim), resist_pad, coarse_step) + sent
        return jnp.where(first, sent, advanced)

    result = lax.fori_loop(0, lax.axis_size("tm") - 1, relay_turn, sent)
    return result[None]


def solution(mesh):
    in_specs = (P("tm", "space", None, None), P("space", None, None), P())
    out_specs = P("tm", "space", None, None)
    return jax.shard_map(
        per_device, mesh=mesh, in_specs=in_specs, out_specs=out_specs, check_vma=False
    )
```

profile of v0, /device:TPU:34, one launch (start us, length us, event | category | flops | bytes accessed | tf_op | source)
XLA Modules:
  0.0 512.5 jit_solution(8598983016923141648)
XLA Ops:
  1.5 3.7 select_add_fusion
  7.1 3.6 collective-permute-start.4
  13.0 3.4 collective-permute-start.6
  21.2 4.0 collective-permute-start.7
  31.2 3.7 collective-permute-start.10
  37.1 3.4 collective-permute-done.9
  44.6 3.6 collective-permute-start.12
  52.5 5.3 %collective-permute-start.13 = (f32[1,128,128]{2,1,0:T(8,128)S(1)}, f32[1,128,128]{2,1,0:T(8,128)S(1)}, u32[]{:S(2)}, u32[]{:S(2)}) collective-permute-start(f32[1,128,128]{2,1,0:T(8,128)S(1)} %get-tuple-element.110), channel_id=1, source_target_pairs={{0,1},{1,2},{2,3},{3,4},{4,5},{5,6},{6,7},{7,8},{8,9},{9,10},{10,1... | collective-permute-start | bytes 196616 | tf_op jit(solution)/shard_map/ppermute | solution.py:17
  63.8 6.1 %collective-permute-start.15 = (f32[1,128,128]{2,1,0:T(8,128)S(1)}, f32[1,128,128]{2,1,0:T(8,128)S(1)}, u32[]{:S(2)}, u32[]{:S(2)}) collective-permute-start(f32[1,128,128]{2,1,0:T(8,128)S(1)} %get-tuple-element.108), channel_id=1, source_target_pairs={{0,1},{1,2},{2,3},{3,4},{4,5},{5,6},{6,7},{7,8},{8,9},{9,10},{10,1... | collective-permute-start | bytes 196616 | tf_op jit(solution)/shard_map/ppermute | solution.py:17
  75.9 8.5 %collective-permute-start.17 = (f32[1,128,128]{2,1,0:T(8,128)S(1)}, f32[1,128,128]{2,1,0:T(8,128)S(1)}, u32[]{:S(2)}, u32[]{:S(2)}) collective-permute-start(f32[1,128,128]{2,1,0:T(8,128)S(1)} %get-tuple-element.106), channel_id=1, source_target_pairs={{0,1},{1,2},{2,3},{3,4},{4,5},{5,6},{6,7},{7,8},{8,9},{9,10},{10,1... | collective-permute-start | bytes 196616 | tf_op jit(solution)/shard_map/ppermute | solution.py:17
  90.3 4.9 collective-permute-start.19
  101.2 410.5 %while.12 = (s32[]{:T(128)}, f32[8,128,128]{2,1,0:T(8,128)S(1)}, pred[]{:T(512)}, f32[10,130,130]{2,1,0:T(8,128)S(1)}, f32[8,128,128]{2,1,0:T(8,128)S(1)}, /*index=5*/s32[]{:T(128)}) while((s32[]{:T(128)}, f32[8,128,128]{2,1,0:T(8,128)S(1)}, pred[]{:T(512)}, f32[10,130,130]{2,1,0:T(8,128)S(1)}, f32[8,128,128]{2,1,0:T(8,128)S(1)}, ...), condition=%wide.region_1.2_spmd, body=%wide.region_0.1_spmd.sunk | while | flops 7967522 | bytes 13038238 | solution.py:78
  101.3 3.5 collective-permute-start
  104.8 13.3 %collective-permute-done = f32[8,128,128]{2,1,0:T(8,128)S(1)} collective-permute-done((f32[8,128,128]{2,1,0:T(8,128)S(1)}, f32[8,128,128]{2,1,0:T(8,128)S(1)}, u32[]{:S(2)}, u32[]{:S(2)}) %collective-permute-start) | collective-permute-done | bytes 524320 | tf_op jit(solution)/shard_map/while/body/eval_jaxpr/ppermute | solution.py:28
  120.0 3.8 collective-permute-start.2
  129.4 16.6 %collective-permute-done = f32[8,128,128]{2,1,0:T(8,128)S(1)} collective-permute-done((f32[8,128,128]{2,1,0:T(8,128)S(1)}, f32[8,128,128]{2,1,0:T(8,128)S(1)}, u32[]{:S(2)}, u32[]{:S(2)}) %collective-permute-start) | collective-permute-done | bytes 524320 | tf_op jit(solution)/shard_map/while/body/eval_jaxpr/ppermute | solution.py:28
  150.4 3.2 collective-permute-done.2
  157.4 16.7 %collective-permute-done = f32[8,128,128]{2,1,0:T(8,128)S(1)} collective-permute-done((f32[8,128,128]{2,1,0:T(8,128)S(1)}, f32[8,128,128]{2,1,0:T(8,128)S(1)}, u32[]{:S(2)}, u32[]{:S(2)}) %collective-permute-start) | collective-permute-done | bytes 524320 | tf_op jit(solution)/shard_map/while/body/eval_jaxpr/ppermute | solution.py:28
  178.5 3.2 collective-permute-done.2
  185.4 16.3 %collective-permute-done = f32[8,128,128]{2,1,0:T(8,128)S(1)} collective-permute-done((f32[8,128,128]{2,1,0:T(8,128)S(1)}, f32[8,128,128]{2,1,0:T(8,128)S(1)}, u32[]{:S(2)}, u32[]{:S(2)}) %collective-permute-start) | collective-permute-done | bytes 524320 | tf_op jit(solution)/shard_map/while/body/eval_jaxpr/ppermute | solution.py:28
  206.1 3.2 collective-permute-done.2
  213.1 16.6 %collective-permute-done = f32[8,128,128]{2,1,0:T(8,128)S(1)} collective-permute-done((f32[8,128,128]{2,1,0:T(8,128)S(1)}, f32[8,128,128]{2,1,0:T(8,128)S(1)}, u32[]{:S(2)}, u32[]{:S(2)}) %collective-permute-start) | collective-permute-done | bytes 524320 | tf_op jit(solution)/shard_map/while/body/eval_jaxpr/ppermute | solution.py:28
  241.1 16.6 %collective-permute-done = f32[8,128,128]{2,1,0:T(8,128)S(1)} collective-permute-done((f32[8,128,128]{2,1,0:T(8,128)S(1)}, f32[8,128,128]{2,1,0:T(8,128)S(1)}, u32[]{:S(2)}, u32[]{:S(2)}) %collective-permute-start) | collective-permute-done | bytes 524320 | tf_op jit(solution)/shard_map/while/body/eval_jaxpr/ppermute | solution.py:28
  269.0 16.3 %collective-permute-done = f32[8,128,128]{2,1,0:T(8,128)S(1)} collective-permute-done((f32[8,128,128]{2,1,0:T(8,128)S(1)}, f32[8,128,128]{2,1,0:T(8,128)S(1)}, u32[]{:S(2)}, u32[]{:S(2)}) %collective-permute-start) | collective-permute-done | bytes 524320 | tf_op jit(solution)/shard_map/while/body/eval_jaxpr/ppermute | solution.py:28
  296.7 16.1 %collective-permute-done = f32[8,128,128]{2,1,0:T(8,128)S(1)} collective-permute-done((f32[8,128,128]{2,1,0:T(8,128)S(1)}, f32[8,128,128]{2,1,0:T(8,128)S(1)}, u32[]{:S(2)}, u32[]{:S(2)}) %collective-permute-start) | collective-permute-done | bytes 524320 | tf_op jit(solution)/shard_map/while/body/eval_jaxpr/ppermute | solution.py:28
  324.1 15.8 %collective-permute-done = f32[8,128,128]{2,1,0:T(8,128)S(1)} collective-permute-done((f32[8,128,128]{2,1,0:T(8,128)S(1)}, f32[8,128,128]{2,1,0:T(8,128)S(1)}, u32[]{:S(2)}, u32[]{:S(2)}) %collective-permute-start) | collective-permute-done | bytes 524320 | tf_op jit(solution)/shard_map/while/body/eval_jaxpr/ppermute | solution.py:28
  351.3 15.5 %collective-permute-done = f32[8,128,128]{2,1,0:T(8,128)S(1)} collective-permute-done((f32[8,128,128]{2,1,0:T(8,128)S(1)}, f32[8,128,128]{2,1,0:T(8,128)S(1)}, u32[]{:S(2)}, u32[]{:S(2)}) %collective-permute-start) | collective-permute-done | bytes 524320 | tf_op jit(solution)/shard_map/while/body/eval_jaxpr/ppermute | solution.py:28
  378.1 16.2 %collective-permute-done = f32[8,128,128]{2,1,0:T(8,128)S(1)} collective-permute-done((f32[8,128,128]{2,1,0:T(8,128)S(1)}, f32[8,128,128]{2,1,0:T(8,128)S(1)}, u32[]{:S(2)}, u32[]{:S(2)}) %collective-permute-start) | collective-permute-done | bytes 524320 | tf_op jit(solution)/shard_map/while/body/eval_jaxpr/ppermute | solution.py:28
  405.7 16.1 %collective-permute-done = f32[8,128,128]{2,1,0:T(8,128)S(1)} collective-permute-done((f32[8,128,128]{2,1,0:T(8,128)S(1)}, f32[8,128,128]{2,1,0:T(8,128)S(1)}, u32[]{:S(2)}, u32[]{:S(2)}) %collective-permute-start) | collective-permute-done | bytes 524320 | tf_op jit(solution)/shard_map/while/body/eval_jaxpr/ppermute | solution.py:28
  433.1 15.8 %collective-permute-done = f32[8,128,128]{2,1,0:T(8,128)S(1)} collective-permute-done((f32[8,128,128]{2,1,0:T(8,128)S(1)}, f32[8,128,128]{2,1,0:T(8,128)S(1)}, u32[]{:S(2)}, u32[]{:S(2)}) %collective-permute-start) | collective-permute-done | bytes 524320 | tf_op jit(solution)/shard_map/while/body/eval_jaxpr/ppermute | solution.py:28
  460.2 15.5 %collective-permute-done = f32[8,128,128]{2,1,0:T(8,128)S(1)} collective-permute-done((f32[8,128,128]{2,1,0:T(8,128)S(1)}, f32[8,128,128]{2,1,0:T(8,128)S(1)}, u32[]{:S(2)}, u32[]{:S(2)}) %collective-permute-start) | collective-permute-done | bytes 524320 | tf_op jit(solution)/shard_map/while/body/eval_jaxpr/ppermute | solution.py:28
  487.1 15.2 %collective-permute-done = f32[8,128,128]{2,1,0:T(8,128)S(1)} collective-permute-done((f32[8,128,128]{2,1,0:T(8,128)S(1)}, f32[8,128,128]{2,1,0:T(8,128)S(1)}, u32[]{:S(2)}, u32[]{:S(2)}) %collective-permute-start) | collective-permute-done | bytes 524320 | tf_op jit(solution)/shard_map/while/body/eval_jaxpr/ppermute | solution.py:28
  (174 shorter events, 205.7 us)
Async XLA Ops:
  5.2 11.2 %collective-permute-start.3 = (f32[1,128,128]{2,1,0:T(8,128)S(1)}, f32[1,128,128]{2,1,0:T(8,128)S(1)}, u32[]{:S(2)}, u32[]{:S(2)}) collective-permute-start(f32[1,128,128]{2,1,0:T(8,128)S(1)} %get-tuple-element.118), channel_id=1, source_target_pairs={{0,1},{1,2},{2,3},{3,4},{4,5},{5,6},{6,7},{7,8},{8,9},{9,10},{10,1... | collective-permute-start | bytes 196616 | tf_op jit(solution)/shard_map/ppermute | solution.py:17
  7.1 9.3 %collective-permute-start.4 = (f32[1,128,128]{2,1,0:T(8,128)S(1)}, f32[1,128,128]{2,1,0:T(8,128)S(1)}, u32[]{:S(2)}, u32[]{:S(2)}) collective-permute-start(f32[1,128,128]{2,1,0:T(8,128)S(1)} %get-tuple-element.119), channel_id=1, source_target_pairs={{1,0},{2,1},{3,2},{4,3},{5,4},{6,5},{7,6},{8,7},{9,8},{10,9},{11,1... | collective-permute-start | bytes 196616 | tf_op jit(solution)/shard_map/ppermute | solution.py:20
  10.8 5.6 %collective-permute-start.5 = (f32[1,128,128]{2,1,0:T(8,128)S(1)}, f32[1,128,128]{2,1,0:T(8,128)S(1)}, u32[]{:S(2)}, u32[]{:S(2)}) collective-permute-start(f32[1,128,128]{2,1,0:T(8,128)S(1)} %get-tuple-element.120), channel_id=1, source_target_pairs={{0,1},{1,2},{2,3},{3,4},{4,5},{5,6},{6,7},{7,8},{8,9},{9,10},{10,1... | collective-permute-start | bytes 196616 | tf_op jit(solution)/shard_map/ppermute | solution.py:17
  21.2 5.9 %collective-permute-start.7 = (f32[1,128,128]{2,1,0:T(8,128)S(1)}, f32[1,128,128]{2,1,0:T(8,128)S(1)}, u32[]{:S(2)}, u32[]{:S(2)}) collective-permute-start(f32[1,128,128]{2,1,0:T(8,128)S(1)} %get-tuple-element.116), channel_id=1, source_target_pairs={{0,1},{1,2},{2,3},{3,4},{4,5},{5,6},{6,7},{7,8},{8,9},{9,10},{10,1... | collective-permute-start | bytes 196616 | tf_op jit(solution)/shard_map/ppermute | solution.py:17
  31.2 5.9 %collective-permute-start.10 = (f32[1,128,128]{2,1,0:T(8,128)S(1)}, f32[1,128,128]{2,1,0:T(8,128)S(1)}, u32[]{:S(2)}, u32[]{:S(2)}) collective-permute-start(f32[1,128,128]{2,1,0:T(8,128)S(1)} %get-tuple-element.115), channel_id=1, source_target_pairs={{1,0},{2,1},{3,2},{4,3},{5,4},{6,5},{7,6},{8,7},{9,8},{10,9},{11,1... | collective-permute-start | bytes 196616 | tf_op jit(solution)/shard_map/ppermute | solution.py:20
  34.9 5.6 %collective-permute-start.9 = (f32[1,128,128]{2,1,0:T(8,128)S(1)}, f32[1,128,128]{2,1,0:T(8,128)S(1)}, u32[]{:S(2)}, u32[]{:S(2)}) collective-permute-start(f32[1,128,128]{2,1,0:T(8,128)S(1)} %get-tuple-element.114), channel_id=1, source_target_pairs={{0,1},{1,2},{2,3},{3,4},{4,5},{5,6},{6,7},{7,8},{8,9},{9,10},{10,1... | collective-permute-start | bytes 196616 | tf_op jit(solution)/shard_map/ppermute | solution.py:17
  42.6 5.6 %collective-permute-start.11 = (f32[1,128,128]{2,1,0:T(8,128)S(1)}, f32[1,128,128]{2,1,0:T(8,128)S(1)}, u32[]{:S(2)}, u32[]{:S(2)}) collective-permute-start(f32[1,128,128]{2,1,0:T(8,128)S(1)} %get-tuple-element.112), channel_id=1, source_target_pairs={{0,1},{1,2},{2,3},{3,4},{4,5},{5,6},{6,7},{7,8},{8,9},{9,10},{10,1... | collective-permute-start | bytes 196616 | tf_op jit(solution)/shard_map/ppermute | solution.py:17
  44.6 5.8 %collective-permute-start.12 = (f32[1,128,128]{2,1,0:T(8,128)S(1)}, f32[1,128,128]{2,1,0:T(8,128)S(1)}, u32[]{:S(2)}, u32[]{:S(2)}) collective-permute-start(f32[1,128,128]{2,1,0:T(8,128)S(1)} %get-tuple-element.113), channel_id=1, source_target_pairs={{1,0},{2,1},{3,2},{4,3},{5,4},{6,5},{7,6},{8,7},{9,8},{10,9},{11,1... | collective-permute-start | bytes 196616 | tf_op jit(solution)/shard_map/ppermute | solution.py:20
  52.5 7.4 %collective-permute-start.13 = (f32[1,128,128]{2,1,0:T(8,128)S(1)}, f32[1,128,128]{2,1,0:T(8,128)S(1)}, u32[]{:S(2)}, u32[]{:S(2)}) collective-permute-start(f32[1,128,128]{2,1,0:T(8,128)S(1)} %get-tuple-element.110), channel_id=1, source_target_pairs={{0,1},{1,2},{2,3},{3,4},{4,5},{5,6},{6,7},{7,8},{8,9},{9,10},{10,1... | collective-permute-start | bytes 196616 | tf_op jit(solution)/shard_map/ppermute | solution.py:17
  63.8 8.1 %collective-permute-start.15 = (f32[1,128,128]{2,1,0:T(8,128)S(1)}, f32[1,128,128]{2,1,0:T(8,128)S(1)}, u32[]{:S(2)}, u32[]{:S(2)}) collective-permute-start(f32[1,128,128]{2,1,0:T(8,128)S(1)} %get-tuple-element.108), channel_id=1, source_target_pairs={{0,1},{1,2},{2,3},{3,4},{4,5},{5,6},{6,7},{7,8},{8,9},{9,10},{10,1... | collective-permute-start | bytes 196616 | tf_op jit(solution)/shard_map/ppermute | solution.py:17
  75.9 10.4 %collective-permute-start.17 = (f32[1,128,128]{2,1,0:T(8,128)S(1)}, f32[1,128,128]{2,1,0:T(8,128)S(1)}, u32[]{:S(2)}, u32[]{:S(2)}) collective-permute-start(f32[1,128,128]{2,1,0:T(8,128)S(1)} %get-tuple-element.106), channel_id=1, source_target_pairs={{0,1},{1,2},{2,3},{3,4},{4,5},{5,6},{6,7},{7,8},{8,9},{9,10},{10,1... | collective-permute-start | bytes 196616 | tf_op jit(solution)/shard_map/ppermute | solution.py:17
  90.3 6.9 %collective-permute-start.19 = (f32[1,128,128]{2,1,0:T(8,128)S(1)}, f32[1,128,128]{2,1,0:T(8,128)S(1)}, u32[]{:S(2)}, u32[]{:S(2)}) collective-permute-start(f32[1,128,128]{2,1,0:T(8,128)S(1)} %get-tuple-element.104), channel_id=1, source_target_pairs={{0,1},{1,2},{2,3},{3,4},{4,5},{5,6},{6,7},{7,8},{8,9},{9,10},{10,1... | collective-permute-start | bytes 196616 | tf_op jit(solution)/shard_map/ppermute | solution.py:17
  101.3 16.8 %collective-permute-start = (f32[8,128,128]{2,1,0:T(8,128)S(1)}, f32[8,128,128]{2,1,0:T(8,128)S(1)}, u32[]{:S(2)}, u32[]{:S(2)}) collective-permute-start(f32[8,128,128]{2,1,0:T(8,128)S(1)} %get-tuple-element.172), channel_id=1, source_target_pairs={{0,32},{32,64},{64,96},{96,128},{128,160},{160,192},{192,224},{224... | collective-permute-start | bytes 1572872 | tf_op jit(solution)/shard_map/while/body/eval_jaxpr/ppermute | solution.py:28
  118.0 5.7 %collective-permute-start.1 = (f32[1,128,128]{2,1,0:T(8,128)S(1)}, f32[1,128,128]{2,1,0:T(8,128)S(1)}, u32[]{:S(2)}, u32[]{:S(2)}) collective-permute-start(f32[1,128,128]{2,1,0:T(8,128)S(1)} %get-tuple-element.161), channel_id=1, source_target_pairs={{1,0},{2,1},{3,2},{4,3},{5,4},{6,5},{7,6},{8,7},{9,8},{10,9},{11,1... | collective-permute-start | bytes 196616 | tf_op jit(solution)/shard_map/while/body/eval_jaxpr/ppermute | solution.py:20
  120.0 5.6 %collective-permute-start.2 = (f32[1,128,128]{2,1,0:T(8,128)S(1)}, f32[1,128,128]{2,1,0:T(8,128)S(1)}, u32[]{:S(2)}, u32[]{:S(2)}) collective-permute-start(f32[1,128,128]{2,1,0:T(8,128)S(1)} %get-tuple-element.162), channel_id=1, source_target_pairs={{0,1},{1,2},{2,3},{3,4},{4,5},{5,6},{6,7},{7,8},{8,9},{9,10},{10,1... | collective-permute-start | bytes 196616 | tf_op jit(solution)/shard_map/while/body/eval_jaxpr/ppermute | solution.py:17
  127.5 18.5 %collective-permute-start = (f32[8,128,128]{2,1,0:T(8,128)S(1)}, f32[8,128,128]{2,1,0:T(8,128)S(1)}, u32[]{:S(2)}, u32[]{:S(2)}) collective-permute-start(f32[8,128,128]{2,1,0:T(8,128)S(1)} %get-tuple-element.172), channel_id=1, source_target_pairs={{0,32},{32,64},{64,96},{96,128},{128,160},{160,192},{192,224},{224... | collective-permute-start | bytes 1572872 | tf_op jit(solution)/shard_map/while/body/eval_jaxpr/ppermute | solution.py:28
  147.9 5.6 %collective-permute-start.2 = (f32[1,128,128]{2,1,0:T(8,128)S(1)}, f32[1,128,128]{2,1,0:T(8,128)S(1)}, u32[]{:S(2)}, u32[]{:S(2)}) collective-permute-start(f32[1,128,128]{2,1,0:T(8,128)S(1)} %get-tuple-element.162), channel_id=1, source_target_pairs={{0,1},{1,2},{2,3},{3,4},{4,5},{5,6},{6,7},{7,8},{8,9},{9,10},{10,1... | collective-permute-start | bytes 196616 | tf_op jit(solution)/shard_map/while/body/eval_jaxpr/ppermute | solution.py:17
  155.4 18.7 %collective-permute-start = (f32[8,128,128]{2,1,0:T(8,128)S(1)}, f32[8,128,128]{2,1,0:T(8,128)S(1)}, u32[]{:S(2)}, u32[]{:S(2)}) collective-permute-start(f32[8,128,128]{2,1,0:T(8,128)S(1)} %get-tuple-element.172), channel_id=1, source_target_pairs={{0,32},{32,64},{64,96},{96,128},{128,160},{160,192},{192,224},{224... | collective-permute-start | bytes 1572872 | tf_op jit(solution)/shard_map/while/body/eval_jaxpr/ppermute | solution.py:28
  176.0 5.6 %collective-permute-start.2 = (f32[1,128,128]{2,1,0:T(8,128)S(1)}, f32[1,128,128]{2,1,0:T(8,128)S(1)}, u32[]{:S(2)}, u32[]{:S(2)}) collective-permute-start(f32[1,128,128]{2,1,0:T(8,128)S(1)} %get-tuple-element.162), channel_id=1, source_target_pairs={{0,1},{1,2},{2,3},{3,4},{4,5},{5,6},{6,7},{7,8},{8,9},{9,10},{10,1... | collective-permute-start | bytes 196616 | tf_op jit(solution)/shard_map/while/body/eval_jaxpr/ppermute | solution.py:17
  183.5 18.2 %collective-permute-start = (f32[8,128,128]{2,1,0:T(8,128)S(1)}, f32[8,128,128]{2,1,0:T(8,128)S(1)}, u32[]{:S(2)}, u32[]{:S(2)}) collective-permute-start(f32[8,128,128]{2,1,0:T(8,128)S(1)} %get-tuple-element.172), channel_id=1, source_target_pairs={{0,32},{32,64},{64,96},{96,128},{128,160},{160,192},{192,224},{224... | collective-permute-start | bytes 1572872 | tf_op jit(solution)/shard_map/while/body/eval_jaxpr/ppermute | solution.py:28
  203.7 5.6 %collective-permute-start.2 = (f32[1,128,128]{2,1,0:T(8,128)S(1)}, f32[1,128,128]{2,1,0:T(8,128)S(1)}, u32[]{:S(2)}, u32[]{:S(2)}) collective-permute-start(f32[1,128,128]{2,1,0:T(8,128)S(1)} %get-tuple-element.162), channel_id=1, source_target_pairs={{0,1},{1,2},{2,3},{3,4},{4,5},{5,6},{6,7},{7,8},{8,9},{9,10},{10,1... | collective-permute-start | bytes 196616 | tf_op jit(solution)/shard_map/while/body/eval_jaxpr/ppermute | solution.py:17
  211.2 18.5 %collective-permute-start = (f32[8,128,128]{2,1,0:T(8,128)S(1)}, f32[8,128,128]{2,1,0:T(8,128)S(1)}, u32[]{:S(2)}, u32[]{:S(2)}) collective-permute-start(f32[8,128,128]{2,1,0:T(8,128)S(1)} %get-tuple-element.172), channel_id=1, source_target_pairs={{0,32},{32,64},{64,96},{96,128},{128,160},{160,192},{192,224},{224... | collective-permute-start | bytes 1572872 | tf_op jit(solution)/shard_map/while/body/eval_jaxpr/ppermute | solution.py:28
  239.1 18.5 %collective-permute-start = (f32[8,128,128]{2,1,0:T(8,128)S(1)}, f32[8,128,128]{2,1,0:T(8,128)S(1)}, u32[]{:S(2)}, u32[]{:S(2)}) collective-permute-start(f32[8,128,128]{2,1,0:T(8,128)S(1)} %get-tuple-element.172), channel_id=1, source_target_pairs={{0,32},{32,64},{64,96},{96,128},{128,160},{160,192},{192,224},{224... | collective-permute-start | bytes 1572872 | tf_op jit(solution)/shard_map/while/body/eval_jaxpr/ppermute | solution.py:28
  267.1 18.3 %collective-permute-start = (f32[8,128,128]{2,1,0:T(8,128)S(1)}, f32[8,128,128]{2,1,0:T(8,128)S(1)}, u32[]{:S(2)}, u32[]{:S(2)}) collective-permute-start(f32[8,128,128]{2,1,0:T(8,128)S(1)} %get-tuple-element.172), channel_id=1, source_target_pairs={{0,32},{32,64},{64,96},{96,128},{128,160},{160,192},{192,224},{224... | collective-permute-start | bytes 1572872 | tf_op jit(solution)/shard_map/while/body/eval_jaxpr/ppermute | solution.py:28
  294.8 18.0 %collective-permute-start = (f32[8,128,128]{2,1,0:T(8,128)S(1)}, f32[8,128,128]{2,1,0:T(8,128)S(1)}, u32[]{:S(2)}, u32[]{:S(2)}) collective-permute-start(f32[8,128,128]{2,1,0:T(8,128)S(1)} %get-tuple-element.172), channel_id=1, source_target_pairs={{0,32},{32,64},{64,96},{96,128},{128,160},{160,192},{192,224},{224... | collective-permute-start | bytes 1572872 | tf_op jit(solution)/shard_map/while/body/eval_jaxpr/ppermute | solution.py:28
  322.2 17.7 %collective-permute-start = (f32[8,128,128]{2,1,0:T(8,128)S(1)}, f32[8,128,128]{2,1,0:T(8,128)S(1)}, u32[]{:S(2)}, u32[]{:S(2)}) collective-permute-start(f32[8,128,128]{2,1,0:T(8,128)S(1)} %get-tuple-element.172), channel_id=1, source_target_pairs={{0,32},{32,64},{64,96},{96,128},{128,160},{160,192},{192,224},{224... | collective-permute-start | bytes 1572872 | tf_op jit(solution)/shard_map/while/body/eval_jaxpr/ppermute | solution.py:28
  349.3 17.4 %collective-permute-start = (f32[8,128,128]{2,1,0:T(8,128)S(1)}, f32[8,128,128]{2,1,0:T(8,128)S(1)}, u32[]{:S(2)}, u32[]{:S(2)}) collective-permute-start(f32[8,128,128]{2,1,0:T(8,128)S(1)} %get-tuple-element.172), channel_id=1, source_target_pairs={{0,32},{32,64},{64,96},{96,128},{128,160},{160,192},{192,224},{224... | collective-permute-start | bytes 1572872 | tf_op jit(solution)/shard_map/while/body/eval_jaxpr/ppermute | solution.py:28
  376.2 18.1 %collective-permute-start = (f32[8,128,128]{2,1,0:T(8,128)S(1)}, f32[8,128,128]{2,1,0:T(8,128)S(1)}, u32[]{:S(2)}, u32[]{:S(2)}) collective-permute-start(f32[8,128,128]{2,1,0:T(8,128)S(1)} %get-tuple-element.172), channel_id=1, source_target_pairs={{0,32},{32,64},{64,96},{96,128},{128,160},{160,192},{192,224},{224... | collective-permute-start | bytes 1572872 | tf_op jit(solution)/shard_map/while/body/eval_jaxpr/ppermute | solution.py:28
  403.7 18.0 %collective-permute-start = (f32[8,128,128]{2,1,0:T(8,128)S(1)}, f32[8,128,128]{2,1,0:T(8,128)S(1)}, u32[]{:S(2)}, u32[]{:S(2)}) collective-permute-start(f32[8,128,128]{2,1,0:T(8,128)S(1)} %get-tuple-element.172), channel_id=1, source_target_pairs={{0,32},{32,64},{64,96},{96,128},{128,160},{160,192},{192,224},{224... | collective-permute-start | bytes 1572872 | tf_op jit(solution)/shard_map/while/body/eval_jaxpr/ppermute | solution.py:28
  431.2 17.7 %collective-permute-start = (f32[8,128,128]{2,1,0:T(8,128)S(1)}, f32[8,128,128]{2,1,0:T(8,128)S(1)}, u32[]{:S(2)}, u32[]{:S(2)}) collective-permute-start(f32[8,128,128]{2,1,0:T(8,128)S(1)} %get-tuple-element.172), channel_id=1, source_target_pairs={{0,32},{32,64},{64,96},{96,128},{128,160},{160,192},{192,224},{224... | collective-permute-start | bytes 1572872 | tf_op jit(solution)/shard_map/while/body/eval_jaxpr/ppermute | solution.py:28
  458.3 17.4 %collective-permute-start = (f32[8,128,128]{2,1,0:T(8,128)S(1)}, f32[8,128,128]{2,1,0:T(8,128)S(1)}, u32[]{:S(2)}, u32[]{:S(2)}) collective-permute-start(f32[8,128,128]{2,1,0:T(8,128)S(1)} %get-tuple-element.172), channel_id=1, source_target_pairs={{0,32},{32,64},{64,96},{96,128},{128,160},{160,192},{192,224},{224... | collective-permute-start | bytes 1572872 | tf_op jit(solution)/shard_map/while/body/eval_jaxpr/ppermute | solution.py:28
  485.2 17.2 %collective-permute-start = (f32[8,128,128]{2,1,0:T(8,128)S(1)}, f32[8,128,128]{2,1,0:T(8,128)S(1)}, u32[]{:S(2)}, u32[]{:S(2)}) collective-permute-start(f32[8,128,128]{2,1,0:T(8,128)S(1)} %get-tuple-element.172), channel_id=1, source_target_pairs={{0,32},{32,64},{64,96},{96,128},{128,160},{160,192},{192,224},{224... | collective-permute-start | bytes 1572872 | tf_op jit(solution)/shard_map/while/body/eval_jaxpr/ppermute | solution.py:28
  (34 other events, 160.9 us)
where the time goes:
time: 514 us; the launch traced here: 513 us
  waiting for transfers between devices  301 us (59%)
  starting transfers between devices  158 us (31%)
  other arithmetic  49.7 us (10%)
    ppermute x15, waiting for transfers between devices, passed_along(): lax.ppermute(value, axis, [(source, source + steps) for source in range(i...  239 us
    ppermute x24, starting transfers between devices, padded(): lax.ppermute(lax.slice_in_dim(block, block.shape[dim] - width, None, axis...  74.4 us
    ppermute x24, starting transfers between devices, padded(): lax.ppermute(lax.slice_in_dim(block, 0, width, axis=dim), axis, backward)  52.9 us
    ppermute x24, waiting for transfers between devices, padded(): lax.ppermute(lax.slice_in_dim(block, block.shape[dim] - width, None, axis...  49.4 us
    ppermute x15, starting transfers between devices, passed_along(): lax.ppermute(value, axis, [(source, source + steps) for source in range(i...  30.4 us
    select_n x15, other arithmetic, relay_turn(): return jnp.where(first, sent, advanced)  19.8 us
    mul x22, other arithmetic, conduct(): coeff = resist_pad * (1.0 + squared / (1.0 + squared))  14.1 us
    ppermute x24, waiting for transfers between devices, padded(): lax.ppermute(lax.slice_in_dim(block, 0, width, axis=dim), axis, backward)  13.2 us
  transfers between devices with their start and end apart: 63, of which 38 were waited for; matrix products, arithmetic and copies ran while one was open for 0% of the time, Pallas kernels for 0%

commit v1 on v0

v1 whole, which is shorter than its diff:
```python
import jax
import jax.numpy as jnp
from jax import lax
from jax.experimental import pallas as pl
from jax.experimental.pallas import tpu as pltpu
from jax.sharding import PartitionSpec as P

STEPS = 8
fine_step = 0.008

BX = 8
NY = 128
NZ = 128
SLICES = 16
ROWS = 8
EXT = 3 * ROWS
FIRST = 7
VMEM = pl.BlockSpec(memory_space=pltpu.VMEM)


def halo_depth(i):
    return FIRST - i if i <= FIRST else SLICES - 1 - i


def packed_tiles():
    tiles = []
    for i in range(SLICES):
        depth = halo_depth(i)
        for d in range(1, depth + 1):
            tiles.append((i, d, "mid"))
            beyond = depth - d
            if 1 <= beyond <= 4:
                tiles.append((i, d, "both"))
            elif beyond > 4:
                tiles.append((i, d, "low"))
                tiles.append((i, d, "high"))
    return tiles


TILES = packed_tiles()


def coeff(eta, u):
    return eta * (2.0 - 1.0 / (1.0 + u * u))


def z_flux(u0, k0, lane):
    up = pltpu.roll(u0, NZ - 1, 1)
    kp = pltpu.roll(k0, NZ - 1, 1)
    edge = k0 * u0
    upper = jnp.where(lane == NZ - 1, -edge, (k0 + kp) * (up - u0))
    lower = jnp.where(lane == 0, edge, pltpu.roll(upper, 1, 1))
    return upper - lower


def fine_kernel(low, own, high, out, u_ref, k_ref, e_ref, g_ref, f_ref, s_ref):
    space = lax.axis_index("space")
    lo = jnp.where(space == 0, BX, 0)
    hi = jnp.where(space == lax.axis_size("space") - 1, 2 * BX - 1, 3 * BX - 1)
    later = jnp.where(lax.axis_index("tm") == 0, 0.0, 1.0).astype(jnp.float32)
    lane = lax.broadcasted_iota(jnp.int32, (8, NZ), 1)
    sub = lax.broadcasted_iota(jnp.int32, (8, NZ), 0)
    parts = NY // 8

    for b, ref in enumerate((low, own, high)):

        def stage(x, _, b=b, ref=ref):
            for r in range(parts):
                u = ref[x, pl.ds(r, 8, stride=parts), :]
                e = ref[BX + x, pl.ds(r, 8, stride=parts), :]
                u_ref[b * BX + x, r] = u
                e_ref[b * BX + x, r] = e
                k_ref[b * BX + x, r] = coeff(e, u)
            return 0

        lax.fori_loop(0, BX, stage, 0)

    def step(first, last, emit):
        for r in range(parts):
            a = f_ref
            a[r] = (k_ref[first - 1, r] + k_ref[first, r]) * (
                u_ref[first, r] - u_ref[first - 1, r]
            )

        def plane(x, _):
            u0, k0 = u_ref[x, 0], k_ref[x, 0]
            u_end, k_end = u_ref[x, parts - 1], k_ref[x, parts - 1]
            wrap_u = jnp.where(sub == 7, 0.0, pltpu.roll(u0, 7, 0))
            wrap_k = jnp.where(sub == 7, 0.0, pltpu.roll(k0, 7, 0))
            top = (k_end + wrap_k) * (wrap_u - u_end)
            y_low = jnp.where(sub == 0, k0 * u0, pltpu.roll(top, 1, 0))
            for r in range(parts):
                if r < parts - 1:
                    u1, k1 = u_ref[x, r + 1], k_ref[x, r + 1]
                    y_up = (k0 + k1) * (u1 - u0)
                else:
                    u1 = k1 = None
                    y_up = top
                x_up = (k0 + k_ref[x + 1, r]) * (u_ref[x + 1, r] - u0)
                x_low = f_ref[r]
                f_ref[r] = x_up
                total = (x_up - x_low) + (y_up - y_low) + z_flux(u0, k0, lane)
                emit(x, r, u0, total)
                u0, k0, y_low = u1, k1, y_up
            return 0

        lax.fori_loop(first, last + 1, plane, 0)

    def keep(x, r, u0, total):
        new = u0 + total
        u_ref[x, r] = new
        k_ref[x, r] = coeff(e_ref[x, r], new)

    def keep_first(x, r, u0, total):
        g_ref[x, r] = later * (u0 + STEPS * total)
        keep(x, r, u0, total)

    def keep_last(x, r, u0, total):
        s_ref[x - BX, pl.ds(r, 8, stride=parts), :] = (u0 + total) - g_ref[x, r]

    step(jnp.maximum(1, lo), jnp.minimum(3 * BX - 2, hi), keep_first)

    def middle(t, _):
        step(jnp.maximum(t, lo), jnp.minimum(3 * BX - 1 - t, hi), keep)
        return 0

    lax.fori_loop(2, STEPS, middle, 0)
    step(BX, 2 * BX - 1, keep_last)

    def spread(x, _):
        for j in range(SLICES):
            for c in range(3):
                strip = j + c - 1
                if 0 <= strip < SLICES:
                    tile = s_ref[x, strip * ROWS : (strip + 1) * ROWS, :]
                else:
                    tile = jnp.zeros((ROWS, NZ), jnp.float32)
                out[j, x, c * ROWS : (c + 1) * ROWS, :] = tile
        return 0

    lax.fori_loop(0, BX, spread, 0)


def fine(low, own, high):
    f32 = jnp.float32
    grid = (3 * BX + 1, NY // 8, 8, NZ)
    return pl.pallas_call(
        fine_kernel,
        out_shape=jax.ShapeDtypeStruct((SLICES, BX, EXT, NZ), f32),
        in_specs=[VMEM] * 3,
        out_specs=VMEM,
        scratch_shapes=[
            pltpu.VMEM(grid, f32),
            pltpu.VMEM(grid, f32),
            pltpu.VMEM(grid, f32),
            pltpu.VMEM(grid, f32),
            pltpu.VMEM(grid[1:], f32),
            pltpu.VMEM((BX, NY, NZ), f32),
        ],
        compiler_params=pltpu.CompilerParams(vmem_limit_bytes=24 << 20),
        name="fine",
    )(low, own, high)


def pack_kernel(sent, down, up):
    row = lax.broadcasted_iota(jnp.int32, (ROWS, NZ), 0)

    def tile(i, x, c):
        return sent[i, x, c * ROWS : (c + 1) * ROWS, :]

    for n, (i, d, kind) in enumerate(TILES):
        for ref, x in ((down, d - 1), (up, BX - d)):
            if kind == "mid":
                value = tile(i, x, 1)
            elif kind == "both":
                value = jnp.where(row < 4, tile(i, x, 2), tile(i, x, 0))
            else:
                value = tile(i, x, 0 if kind == "low" else 2)
            ref[n] = value


def pack(sent):
    shape = jax.ShapeDtypeStruct((len(TILES), ROWS, NZ), jnp.float32)
    return pl.pallas_call(
        pack_kernel,
        out_shape=(shape, shape),
        in_specs=[VMEM],
        out_specs=(VMEM, VMEM),
        compiler_params=pltpu.CompilerParams(vmem_limit_bytes=8 << 20),
        name="pack",
    )(sent)


def stage_coarse(slices, low_eta, own_eta, high_eta, sent, below, above, e_ref, n_ref):
    tm = lax.axis_index("tm")
    for c in range(3):
        strip = tm + (c - 1)
        inside = jnp.where((strip >= 0) & (strip < SLICES), float(STEPS), 0.0)
        start = pl.multiple_of(jnp.clip(strip, 0, SLICES - 1) * ROWS, ROWS)
        for b, ref in enumerate((low_eta, own_eta, high_eta)):

            def one(x, _, b=b, ref=ref):
                e_ref[b * BX + x, c * ROWS : (c + 1) * ROWS, :] = (
                    inside.astype(jnp.float32) * ref[BX + x, pl.ds(start, ROWS), :]
                )
                return 0

            lax.fori_loop(0, BX, one, 0, unroll=True)

    base = slices[0]

    def own_part(i, _):
        for x in range(BX):
            for c in range(3):
                n_ref[i, BX + x, c * ROWS : (c + 1) * ROWS, :] = sent[
                    base + i, x, c * ROWS : (c + 1) * ROWS, :
                ]
        return 0

    lax.fori_loop(0, len(slices), own_part, 0)
    for n, (i, d, kind) in enumerate(TILES):
        if i not in slices:
            continue
        where = {"mid": (1,), "both": (0, 2), "low": (0,), "high": (2,)}[kind]
        for c in where:
            n_ref[i - base, BX - d, c * ROWS : (c + 1) * ROWS, :] = below[n]
            n_ref[i - base, 2 * BX - 1 + d, c * ROWS : (c + 1) * ROWS, :] = above[n]


def coarse_steps(count, base, e_ref, n_ref, u_ref, k_ref, f_ref, s_ref, out):
    space, tm = lax.axis_index("space"), lax.axis_index("tm")
    lo = jnp.where(space == 0, BX, 0)
    hi = jnp.where(space == lax.axis_size("space") - 1, 2 * BX - 1, 3 * BX - 1)
    lane = lax.broadcasted_iota(jnp.int32, (8, NZ), 1)
    sub = lax.broadcasted_iota(jnp.int32, (8, NZ), 0)
    y_lo = jnp.where(tm == 0, ROWS, 0)
    y_hi = jnp.where(tm == SLICES - 1, 2 * ROWS, EXT)
    masks = []
    for r in range(3):
        y = 3 * sub + r
        masks.append(jnp.where((y >= y_lo) & (y < y_hi), 1.0, 0.0).astype(jnp.float32))

    def setup(x, _):
        for r in range(3):
            k_ref[x, r] = coeff(e_ref[x, pl.ds(r, 8, stride=3), :], u_ref[x, r])
        return 0

    lax.fori_loop(BX - count, 2 * BX + count, setup, 0)

    for n in range(1, count + 1):
        first = jnp.maximum(BX - count + n, lo)
        last = jnp.minimum(2 * BX - 1 + count - n, hi)
        for r in range(3):
            f_ref[r] = (k_ref[first - 1, r] + k_ref[first, r]) * (
                u_ref[first, r] - u_ref[first - 1, r]
            )

        def plane(x, _, n=n):
            us = [u_ref[x, r] for r in range(3)]
            ks = [k_ref[x, r] for r in range(3)]
            us.append(pltpu.roll(us[0], 7, 0))
            ks.append(pltpu.roll(ks[0], 7, 0))
            ups = [(ks[r] + ks[r + 1]) * (us[r + 1] - us[r]) for r in range(3)]
            lows = [pltpu.roll(ups[2], 1, 0), ups[0], ups[1]]
            for r in range(3):
                u0, k0 = us[r], ks[r]
                x_up = (k0 + k_ref[x + 1, r]) * (u_ref[x + 1, r] - u0)
                x_low = f_ref[r]
                f_ref[r] = x_up
                total = (x_up - x_low) + (ups[r] - lows[r]) + z_flux(u0, k0, lane)
                new = masks[r] * (u0 + total + n_ref[base + n, x, pl.ds(r, 8, stride=3), :])
                u_ref[x, r] = new
                k_ref[x, r] = coeff(e_ref[x, pl.ds(r, 8, stride=3), :], new)
            return 0

        lax.fori_loop(first, last + 1, plane, 0)

        def emit(x, _, n=n):
            for r in range(3):
                s_ref[x, pl.ds(r, 8, stride=3), :] = u_ref[BX + x, r]
            out(n, x, s_ref[x, ROWS : 2 * ROWS, :])
            return 0

        lax.fori_loop(0, BX, emit, 0, unroll=True)


def first_kernel(
    low_eta, own_eta, high_eta, sent, below, above, out, e_ref, n_ref, u_ref, k_ref, f_ref, s_ref
):
    slices = list(range(FIRST + 1))
    stage_coarse(slices, low_eta, own_eta, high_eta, sent, below, above, e_ref, n_ref)

    def load(x, _):
        for r in range(3):
            u_ref[x, r] = n_ref[0, x, pl.ds(r, 8, stride=3), :]
        return 0

    lax.fori_loop(BX - FIRST, 2 * BX + FIRST, load, 0)
    for x in range(BX):
        out[0, x] = sent[0, x, ROWS : 2 * ROWS, :]

    def put(n, x, value):
        out[n, x] = value

    coarse_steps(FIRST, 0, e_ref, n_ref, u_ref, k_ref, f_ref, s_ref, put)


def second_kernel(
    low_eta, own_eta, high_eta, sent, below, above, low_u, own_u, high_u, done, out,
    e_ref, n_ref, u_ref, k_ref, f_ref, s_ref,
):
    slices = list(range(FIRST + 1, SLICES))
    stage_coarse(slices, low_eta, own_eta, high_eta, sent, below, above, e_ref, n_ref)
    for b, ref in enumerate((low_u, own_u, high_u)):
        for x in range(BX):
            for r in range(3):
                u_ref[b * BX + x, r] = ref[x, pl.ds(r, 8, stride=3), :]
    for i in range(FIRST + 1):
        for x in range(BX):
            out[i, x] = done[i, x]

    def put(n, x, value):
        out[FIRST + n, x] = value

    coarse_steps(len(slices), -1, e_ref, n_ref, u_ref, k_ref, f_ref, s_ref, put)


def coarse_call(kernel, name, count, *operands):
    f32 = jnp.float32
    return pl.pallas_call(
        kernel,
        out_shape=jax.ShapeDtypeStruct((count, BX, ROWS, NZ), f32),
        in_specs=[VMEM] * len(operands),
        out_specs=VMEM,
        scratch_shapes=[
            pltpu.VMEM((3 * BX + 1, EXT, NZ), f32),
            pltpu.VMEM((FIRST + 1, 3 * BX + 1, EXT, NZ), f32),
            pltpu.VMEM((3 * BX + 1, 3, 8, NZ), f32),
            pltpu.VMEM((3 * BX + 1, 3, 8, NZ), f32),
            pltpu.VMEM((3, 8, NZ), f32),
            pltpu.VMEM((BX, EXT, NZ), f32),
        ],
        compiler_params=pltpu.CompilerParams(vmem_limit_bytes=16 << 20),
        name=name,
    )(*operands)


def lookup(regions, resistivity):
    result = jnp.zeros(regions.shape, jnp.float32)
    for region in range(resistivity.shape[0]):
        result = result + jnp.where(regions == region, resistivity[region], jnp.float32(0.0))
    return result


def both_ways(down, up, axis):
    count = lax.axis_size(axis)
    forward = [(i, i + 1) for i in range(count - 1)]
    backward = [(i + 1, i) for i in range(count - 1)]
    return lax.ppermute(up, axis, forward), lax.ppermute(down, axis, backward)


def per_device(start_values, regions, resistivity):
    half = lookup(regions, resistivity) * jnp.float32(0.5 * fine_step)
    own = jnp.concatenate([start_values[0], half], axis=0)
    low, high = both_ways(own, own, "space")
    spread = fine(low, own, high)
    sent = lax.all_to_all(spread, "tm", 0, 0)
    below, above = both_ways(*pack(sent), "space")
    done = coarse_call(first_kernel, "first", FIRST + 1, low, own, high, sent, below, above)
    state = done[FIRST]
    y_low, y_high = both_ways(state, state, "tm")
    strip = jnp.concatenate([y_low, state, y_high], axis=1)
    x_low, x_high = both_ways(strip, strip, "space")
    ends = coarse_call(
        second_kernel, "second", SLICES, low, own, high, sent, below, above,
        x_low, strip, x_high, done,
    )
    result = lax.all_to_all(ends, "tm", 0, 0)
    result = jnp.transpose(result, (1, 0, 2, 3)).reshape(BX, NY, NZ)
    return result[None]


def solution(mesh):
    in_specs = (P("tm", "space", None, None), P("space", None, None), P())
    out_specs = P("tm", "space", None, None)
    return jax.shard_map(
        per_device, mesh=mesh, in_specs=in_specs, out_specs=out_specs, check_vma=False
    )
```

time: 514 us -> 162 us (0.32)
  the two profiles are of different devices: /device:TPU:34 before, /device:TPU:128 now
where the time goes in v1:
time: 162 us; the launch traced here: 161 us
  Pallas kernels  59.8 us (37%)
  blocking collectives  44.3 us (27%)
  waiting for transfers between devices  27.5 us (17%)
  starting transfers between devices  22.6 us (14%)
  other arithmetic  4.89 us (3%)
  local copies, waits for them, and re-layouts  2.28 us (1%)
    pallas_call x2, Pallas kernels, coarse_call(): pl.pallas_call(kernel, out_shape=jax.ShapeDtypeStruct((count, BX, ROWS, N...  36.1 us
    all_to_all x1, blocking collectives, per_device(): sent = lax.all_to_all(spread, 'tm', 0, 0)  27.9 us
    ppermute x8, waiting for transfers between devices, both_ways(): return (lax.ppermute(up, axis, forward), lax.ppermute(down, axis, backward))  27.5 us
    pallas_call x1, Pallas kernels, fine(): pl.pallas_call(fine_kernel, out_shape=jax.ShapeDtypeStruct((SLICES, BX, E...  23.7 us
    ppermute x8, starting transfers between devices, both_ways(): return (lax.ppermute(up, axis, forward), lax.ppermute(down, axis, backward))  22.6 us
    all_to_all x1, blocking collectives, per_device(): result = lax.all_to_all(ends, 'tm', 0, 0)  16.5 us
    mul x1, other arithmetic, per_device(): half = lookup(regions, resistivity) * jnp.float32(0.5 * fine_step)  3.77 us
  transfers between devices with their start and end apart: 8, of which 8 were waited for; matrix products, arithmetic and copies ran while one was open for 0% of the time, Pallas kernels for 0%

profile of v1, /device:TPU:128, one launch (start us, length us, event | category | flops | bytes accessed | tf_op | source)
XLA Modules:
  0.0 161.5 jit_solution(11928257762926260873)
XLA Ops:
  0.0 1.5 fusion
  1.5 3.8 %add_multiply_fusion = f32[8,128,128]{2,1,0:T(8,128)S(1)} fusion(s32[8,128,128]{2,1,0:T(8,128)} %param.4, f32[]{:T(128)} %bitcast.4, f32[]{:T(128)} %bitcast.3, f32[]{:T(128)} %bitcast.2, f32[]{:T(128)} %bitcast.1), kind=kLoop, calls=%fused_computation.2 | loop fusion | flops 1572864 | bytes 1048592 | tf_op jit(solution)/shard_map/mul | solution.py:363
  5.2 1.1 pad_maximum_fusion.own.own_eta
  6.3 1.9 %collective-permute-start.1 = (f32[16,128,128]{2,1,0:T(8,128)S(1)}, f32[16,128,128]{2,1,0:T(8,128)S(1)}, u32[]{:S(2)}, u32[]{:S(2)}) collective-permute-start(f32[16,128,128]{2,1,0:T(8,128)S(1)} %pad_maximum_fusion.own.own_eta), channel_id=1, source_target_pairs={{1,0},{2,1},{3,2},{4,3},{5,4},{6,5},{7,6},{8,7},{9,8},{10,9},{11,1... | collective-permute-start | bytes 3145736 | tf_op jit(solution)/shard_map/ppermute | solution.py:359
  8.3 2.4 %collective-permute-start = (f32[16,128,128]{2,1,0:T(8,128)S(1)}, f32[16,128,128]{2,1,0:T(8,128)S(1)}, u32[]{:S(2)}, u32[]{:S(2)}) collective-permute-start(f32[16,128,128]{2,1,0:T(8,128)S(1)} %pad_maximum_fusion.own.own_eta), channel_id=1, source_target_pairs={{0,1},{1,2},{2,3},{3,4},{4,5},{5,6},{6,7},{7,8},{8,9},{9,10},{10,1... | collective-permute-start | bytes 3145736 | tf_op jit(solution)/shard_map/ppermute | solution.py:359
  10.7 9.9 %collective-permute-done.1.high.high_eta = f32[16,128,128]{2,1,0:T(8,128)S(1)} collective-permute-done((f32[16,128,128]{2,1,0:T(8,128)S(1)}, f32[16,128,128]{2,1,0:T(8,128)S(1)}, u32[]{:S(2)}, u32[]{:S(2)}) %collective-permute-start.1) | collective-permute-done | bytes 1048608 | tf_op jit(solution)/shard_map/ppermute | solution.py:359
  20.6 5.0 %collective-permute-done.low.low_eta = f32[16,128,128]{2,1,0:T(8,128)S(1)} collective-permute-done((f32[16,128,128]{2,1,0:T(8,128)S(1)}, f32[16,128,128]{2,1,0:T(8,128)S(1)}, u32[]{:S(2)}, u32[]{:S(2)}) %collective-permute-start) | collective-permute-done | bytes 1048608 | tf_op jit(solution)/shard_map/ppermute | solution.py:359
  25.6 23.7 %fine.1 = f32[16,8,24,128]{3,2,1,0:T(8,128)S(1)} custom-call(f32[16,128,128]{2,1,0:T(8,128)S(1)} %collective-permute-done.low.low_eta, f32[16,128,128]{2,1,0:T(8,128)S(1)} %pad_maximum_fusion.own.own_eta, f32[16,128,128]{2,1,0:T(8,128)S(1)} %collective-permute-done.1.high.high_eta), custom_call_target="tpu_custom_call" | custom-call | tf_op jit(solution)/shard_map/fine/pallas_call | solution.py:147
  49.3 27.9 %all_to_all.10.sent = f32[16,8,24,128]{3,2,1,0:T(8,128)S(1)} all-to-all(f32[16,8,24,128]{3,2,1,0:T(8,128)S(1)} %fine.1), channel_id=1, replica_groups=mesh['tm'=16,'space'=32] {'tm'}, dimensions={0} | all-to-all | bytes 3145728 | tf_op jit(solution)/shard_map/all_to_all | solution.py:367
  77.1 0.1 pack.1
  77.2 1.9 %collective-permute-start.2 = (f32[104,8,128]{2,1,0:T(8,128)S(1)}, f32[104,8,128]{2,1,0:T(8,128)S(1)}, u32[]{:S(2)}, u32[]{:S(2)}) collective-permute-start(f32[104,8,128]{2,1,0:T(8,128)S(1)} %get-tuple-element.7), channel_id=1, source_target_pairs={{0,1},{1,2},{2,3},{3,4},{4,5},{5,6},{6,7},{7,8},{8,9},{9,10},{10,1... | collective-permute-start | bytes 1277960 | tf_op jit(solution)/shard_map/ppermute | solution.py:359
  79.1 4.9 %collective-permute-start.3 = (f32[104,8,128]{2,1,0:T(8,128)S(1)}, f32[104,8,128]{2,1,0:T(8,128)S(1)}, u32[]{:S(2)}, u32[]{:S(2)}) collective-permute-start(f32[104,8,128]{2,1,0:T(8,128)S(1)} %get-tuple-element.8), channel_id=1, source_target_pairs={{1,0},{2,1},{3,2},{4,3},{5,4},{6,5},{7,6},{8,7},{9,8},{10,9},{11,1... | collective-permute-start | bytes 1277960 | tf_op jit(solution)/shard_map/ppermute | solution.py:359
  84.0 3.9 %collective-permute-done.2.below = f32[104,8,128]{2,1,0:T(8,128)S(1)} collective-permute-done((f32[104,8,128]{2,1,0:T(8,128)S(1)}, f32[104,8,128]{2,1,0:T(8,128)S(1)}, u32[]{:S(2)}, u32[]{:S(2)}) %collective-permute-start.2) | collective-permute-done | bytes 426016 | tf_op jit(solution)/shard_map/ppermute | solution.py:359
  87.8 1.8 %collective-permute-done.3.above = f32[104,8,128]{2,1,0:T(8,128)S(1)} collective-permute-done((f32[104,8,128]{2,1,0:T(8,128)S(1)}, f32[104,8,128]{2,1,0:T(8,128)S(1)}, u32[]{:S(2)}, u32[]{:S(2)}) %collective-permute-start.3) | collective-permute-done | bytes 426016 | tf_op jit(solution)/shard_map/ppermute | solution.py:359
  89.6 16.3 %first.1.done = f32[8,8,8,128]{3,2,1,0:T(8,128)S(1)} custom-call(f32[16,128,128]{2,1,0:T(8,128)S(1)} %collective-permute-done.low.low_eta, f32[16,128,128]{2,1,0:T(8,128)S(1)} %pad_maximum_fusion.own.own_eta, f32[16,128,128]{2,1,0:T(8,128)S(1)} %collective-permute-done.1.high.high_eta, f32[16,8,24,128]{3,2,1,0:T(8,128)S(1)} %all_to_all.10.sent, ...), custom_call_target="tpu_custom_call" | custom-call | tf_op jit(solution)/shard_map/first/pallas_call | solution.py:330
  105.9 1.3 collective-permute-start.5
  107.2 4.5 %collective-permute-start.4 = (f32[8,8,128]{2,1,0:T(8,128)S(1)}, f32[8,8,128]{2,1,0:T(8,128)S(1)}, u32[]{:S(2)}, u32[]{:S(2)}) collective-permute-start(f32[8,8,128]{2,1,0:T(8,128)S(1)} %slice_bitcast_fusion), channel_id=1, source_target_pairs={{0,32},{32,64},{64,96},{96,128},{128,160},{160,192},{192,224},{224... | collective-permute-start | bytes 98312 | tf_op jit(solution)/shard_map/ppermute | solution.py:359
  111.8 0.1 collective-permute-done.5
  111.8 1.7 %collective-permute-done.4 = f32[8,8,128]{2,1,0:T(8,128)S(1)} collective-permute-done((f32[8,8,128]{2,1,0:T(8,128)S(1)}, f32[8,8,128]{2,1,0:T(8,128)S(1)}, u32[]{:S(2)}, u32[]{:S(2)}) %collective-permute-start.4) | collective-permute-done | bytes 32800 | tf_op jit(solution)/shard_map/ppermute | solution.py:359
  113.5 3.7 %collective-permute-start.7 = (f32[8,24,128]{2,1,0:T(8,128)S(1)}, f32[8,24,128]{2,1,0:T(8,128)S(1)}, u32[]{:S(2)}, u32[]{:S(2)}) collective-permute-start(f32[8,24,128]{2,1,0:T(8,128)S(1)} %pad_maximum_fusion.1.own_u), channel_id=1, source_target_pairs={{1,0},{2,1},{3,2},{4,3},{5,4},{6,5},{7,6},{8,7},{9,8},{10,9},{11,1... | collective-permute-start | bytes 294920 | tf_op jit(solution)/shard_map/ppermute | solution.py:359
  117.3 1.9 %collective-permute-start.6 = (f32[8,24,128]{2,1,0:T(8,128)S(1)}, f32[8,24,128]{2,1,0:T(8,128)S(1)}, u32[]{:S(2)}, u32[]{:S(2)}) collective-permute-start(f32[8,24,128]{2,1,0:T(8,128)S(1)} %pad_maximum_fusion.1.own_u), channel_id=1, source_target_pairs={{0,1},{1,2},{2,3},{3,4},{4,5},{5,6},{6,7},{7,8},{8,9},{9,10},{10,1... | collective-permute-start | bytes 294920 | tf_op jit(solution)/shard_map/ppermute | solution.py:359
  119.2 0.3 collective-permute-done.7.high_u
  119.4 5.0 %collective-permute-done.6.low_u = f32[8,24,128]{2,1,0:T(8,128)S(1)} collective-permute-done((f32[8,24,128]{2,1,0:T(8,128)S(1)}, f32[8,24,128]{2,1,0:T(8,128)S(1)}, u32[]{:S(2)}, u32[]{:S(2)}) %collective-permute-start.6) | collective-permute-done | bytes 98336 | tf_op jit(solution)/shard_map/ppermute | solution.py:359
  124.4 19.8 %second.1 = f32[16,8,8,128]{3,2,1,0:T(8,128)S(1)} custom-call(f32[16,128,128]{2,1,0:T(8,128)S(1)} %collective-permute-done.low.low_eta, f32[16,128,128]{2,1,0:T(8,128)S(1)} %pad_maximum_fusion.own.own_eta, f32[16,128,128]{2,1,0:T(8,128)S(1)} %collective-permute-done.1.high.high_eta, f32[16,8,24,128]{3,2,1,0:T(8,128)S(1)} %all_to_all.10.sent, ...), custom_call_target="tpu_custom_call" | custom-call | tf_op jit(solution)/shard_map/second/pallas_call | solution.py:330
  144.2 16.5 %all_to_all.11 = f32[16,8,8,128]{3,2,1,0:T(8,128)S(1)} all-to-all(f32[16,8,8,128]{3,2,1,0:T(8,128)S(1)} %second.1), channel_id=1, replica_groups=mesh['tm'=16,'space'=32] {'tm'}, dimensions={0} | all-to-all | bytes 1048576 | tf_op jit(solution)/shard_map/all_to_all | solution.py:378
  160.6 0.8 copy_bitcast_fusion
  (2 shorter events, 0.0 us)
Async XLA Ops:
  6.3 14.2 %collective-permute-start.1 = (f32[16,128,128]{2,1,0:T(8,128)S(1)}, f32[16,128,128]{2,1,0:T(8,128)S(1)}, u32[]{:S(2)}, u32[]{:S(2)}) collective-permute-start(f32[16,128,128]{2,1,0:T(8,128)S(1)} %pad_maximum_fusion.own.own_eta), channel_id=1, source_target_pairs={{1,0},{2,1},{3,2},{4,3},{5,4},{6,5},{7,6},{8,7},{9,8},{10,9},{11,1... | collective-permute-start | bytes 3145736 | tf_op jit(solution)/shard_map/ppermute | solution.py:359
  8.3 17.3 %collective-permute-start = (f32[16,128,128]{2,1,0:T(8,128)S(1)}, f32[16,128,128]{2,1,0:T(8,128)S(1)}, u32[]{:S(2)}, u32[]{:S(2)}) collective-permute-start(f32[16,128,128]{2,1,0:T(8,128)S(1)} %pad_maximum_fusion.own.own_eta), channel_id=1, source_target_pairs={{0,1},{1,2},{2,3},{3,4},{4,5},{5,6},{6,7},{7,8},{8,9},{9,10},{10,1... | collective-permute-start | bytes 3145736 | tf_op jit(solution)/shard_map/ppermute | solution.py:359
  77.2 10.7 %collective-permute-start.2 = (f32[104,8,128]{2,1,0:T(8,128)S(1)}, f32[104,8,128]{2,1,0:T(8,128)S(1)}, u32[]{:S(2)}, u32[]{:S(2)}) collective-permute-start(f32[104,8,128]{2,1,0:T(8,128)S(1)} %get-tuple-element.7), channel_id=1, source_target_pairs={{0,1},{1,2},{2,3},{3,4},{4,5},{5,6},{6,7},{7,8},{8,9},{9,10},{10,1... | collective-permute-start | bytes 1277960 | tf_op jit(solution)/shard_map/ppermute | solution.py:359
  79.1 10.5 %collective-permute-start.3 = (f32[104,8,128]{2,1,0:T(8,128)S(1)}, f32[104,8,128]{2,1,0:T(8,128)S(1)}, u32[]{:S(2)}, u32[]{:S(2)}) collective-permute-start(f32[104,8,128]{2,1,0:T(8,128)S(1)} %get-tuple-element.8), channel_id=1, source_target_pairs={{1,0},{2,1},{3,2},{4,3},{5,4},{6,5},{7,6},{8,7},{9,8},{10,9},{11,1... | collective-permute-start | bytes 1277960 | tf_op jit(solution)/shard_map/ppermute | solution.py:359
  105.9 5.9 %collective-permute-start.5 = (f32[8,8,128]{2,1,0:T(8,128)S(1)}, f32[8,8,128]{2,1,0:T(8,128)S(1)}, u32[]{:S(2)}, u32[]{:S(2)}) collective-permute-start(f32[8,8,128]{2,1,0:T(8,128)S(1)} %slice_bitcast_fusion), channel_id=1, source_target_pairs={{32,0},{64,32},{96,64},{128,96},{160,128},{192,160},{224,192},{256... | collective-permute-start | bytes 98312 | tf_op jit(solution)/shard_map/ppermute | solution.py:359
  107.2 6.3 %collective-permute-start.4 = (f32[8,8,128]{2,1,0:T(8,128)S(1)}, f32[8,8,128]{2,1,0:T(8,128)S(1)}, u32[]{:S(2)}, u32[]{:S(2)}) collective-permute-start(f32[8,8,128]{2,1,0:T(8,128)S(1)} %slice_bitcast_fusion), channel_id=1, source_target_pairs={{0,32},{32,64},{64,96},{96,128},{128,160},{160,192},{192,224},{224... | collective-permute-start | bytes 98312 | tf_op jit(solution)/shard_map/ppermute | solution.py:359
  113.5 5.9 %collective-permute-start.7 = (f32[8,24,128]{2,1,0:T(8,128)S(1)}, f32[8,24,128]{2,1,0:T(8,128)S(1)}, u32[]{:S(2)}, u32[]{:S(2)}) collective-permute-start(f32[8,24,128]{2,1,0:T(8,128)S(1)} %pad_maximum_fusion.1.own_u), channel_id=1, source_target_pairs={{1,0},{2,1},{3,2},{4,3},{5,4},{6,5},{7,6},{8,7},{9,8},{10,9},{11,1... | collective-permute-start | bytes 294920 | tf_op jit(solution)/shard_map/ppermute | solution.py:359
  117.3 7.1 %collective-permute-start.6 = (f32[8,24,128]{2,1,0:T(8,128)S(1)}, f32[8,24,128]{2,1,0:T(8,128)S(1)}, u32[]{:S(2)}, u32[]{:S(2)}) collective-permute-start(f32[8,24,128]{2,1,0:T(8,128)S(1)} %pad_maximum_fusion.1.own_u), channel_id=1, source_target_pairs={{0,1},{1,2},{2,3},{3,4},{4,5},{5,6},{6,7},{7,8},{8,9},{9,10},{10,1... | collective-permute-start | bytes 294920 | tf_op jit(solution)/shard_map/ppermute | solution.py:359

commit v2 on v1

v2 whole, which is shorter than its diff:
```python
import jax
import jax.numpy as jnp
from jax import lax
from jax.experimental import pallas as pl
from jax.experimental.pallas import tpu as pltpu
from jax.sharding import PartitionSpec as P

STEPS = 8
fine_step = 0.008

BX = 8
NY = 128
NZ = 128
SLICES = 16
REGIONS = 4
ROWS = 8
EXT = 3 * ROWS
SMEM = pl.BlockSpec(memory_space=pltpu.SMEM)
FIRST = 7
VMEM = pl.BlockSpec(memory_space=pltpu.VMEM)


def halo_depth(i):
    return FIRST - i if i <= FIRST else SLICES - 1 - i


def packed_tiles():
    tiles = []
    for i in range(SLICES):
        depth = halo_depth(i)
        for d in range(1, depth + 1):
            tiles.append((i, d, "mid"))
            beyond = depth - d
            if 1 <= beyond <= 4:
                tiles.append((i, d, "both"))
            elif beyond > 4:
                tiles.append((i, d, "low"))
                tiles.append((i, d, "high"))
    return tiles


TILES = packed_tiles()
PLACE = {}
for _n, (_i, _d, _kind) in enumerate(TILES):
    for _c in {"mid": (1,), "both": (0, 2), "low": (0,), "high": (2,)}[_kind]:
        PLACE[_i, _d, _c] = _n
PARTS = NY // 8
GROUP = 40


def coeff(eta, u):
    return eta * (2.0 - 1.0 / (1.0 + u * u))


def z_flux(u0, k0, lane):
    up = pltpu.roll(u0, NZ - 1, 1)
    kp = pltpu.roll(k0, NZ - 1, 1)
    edge = k0 * u0
    upper = jnp.where(lane == NZ - 1, -edge, (k0 + kp) * (up - u0))
    lower = jnp.where(lane == 0, edge, pltpu.roll(upper, 1, 1))
    return upper - lower


def iotas():
    shape = (8, NZ)
    return lax.broadcasted_iota(jnp.int32, shape, 1), lax.broadcasted_iota(jnp.int32, shape, 0)


def has_neighbours(axis):
    index = lax.axis_index(axis)
    below = jnp.where(index == 0, 0.0, 1.0).astype(jnp.float32)
    above = jnp.where(index == lax.axis_size(axis) - 1, 0.0, 1.0).astype(jnp.float32)
    return below, above


def own_kernel(start, regions, resistivity, out):
    scaled = [resistivity[i] * jnp.float32(0.5 * fine_step) for i in range(REGIONS)]

    def plane(x, _):
        for r in range(PARTS):
            out[x, r] = start[x, pl.ds(r, 8, stride=PARTS), :]
            region = regions[x, pl.ds(r, 8, stride=PARTS), :]
            value = jnp.zeros((8, NZ), jnp.float32)
            for i in range(REGIONS):
                value = jnp.where(region == i, scaled[i], value)
            out[BX + x, r] = value
        return 0

    lax.fori_loop(0, BX, plane, 0)


def own_part(start, regions, resistivity):
    return pl.pallas_call(
        own_kernel,
        out_shape=jax.ShapeDtypeStruct((2 * BX, PARTS, 8, NZ), jnp.float32),
        in_specs=[VMEM, VMEM, SMEM],
        out_specs=VMEM,
        compiler_params=pltpu.CompilerParams(vmem_limit_bytes=8 << 20),
        name="own",
    )(start, regions, resistivity)


def fine_kernel(low, own, high, out, u_ref, k_ref, e_ref, g_ref, f_ref, s_ref):
    below, above = has_neighbours("space")
    later = jnp.where(lax.axis_index("tm") == 0, 0.0, 1.0).astype(jnp.float32)
    lane, sub = iotas()

    for b, ref in enumerate((low, own, high)):

        def stage(x, _, b=b, ref=ref):
            for r in range(PARTS):
                u, e = ref[x, r], ref[BX + x, r]
                u_ref[b * BX + x, r] = u
                e_ref[b * BX + x, r] = e
                k_ref[b * BX + x, r] = coeff(e, u)
            return 0

        lax.fori_loop(0, BX, stage, 0)

    def plane(x, emit):
        u0, k0 = u_ref[x, 0], k_ref[x, 0]
        u_end, k_end = u_ref[x, PARTS - 1], k_ref[x, PARTS - 1]
        wrap_u = jnp.where(sub == 7, 0.0, pltpu.roll(u0, 7, 0))
        wrap_k = jnp.where(sub == 7, 0.0, pltpu.roll(k0, 7, 0))
        top = (k_end + wrap_k) * (wrap_u - u_end)
        y_low = jnp.where(sub == 0, k0 * u0, pltpu.roll(top, 1, 0))
        for r in range(PARTS):
            if r < PARTS - 1:
                u1, k1 = u_ref[x, r + 1], k_ref[x, r + 1]
                y_up = (k0 + k1) * (u1 - u0)
            else:
                u1 = k1 = None
                y_up = top
            x_up = (k0 + k_ref[x + 1, r]) * (u_ref[x + 1, r] - u0)
            x_low = f_ref[r]
            f_ref[r] = x_up
            total = (x_up - x_low) + (y_up - y_low) + z_flux(u0, k0, lane)
            emit(x, r, u0, total)
            u0, k0, y_low = u1, k1, y_up

    def step(first, pairs, emit):
        for r in range(PARTS):
            f_ref[r] = (k_ref[first - 1, r] + k_ref[first, r]) * (
                u_ref[first, r] - u_ref[first - 1, r]
            )

        def pair(n, _):
            for q in range(2):
                plane(first + 2 * n + q, emit)
            return 0

        lax.fori_loop(0, pairs, pair, 0)

    def inside(x):
        return jnp.where(x < BX, below, jnp.where(x < 2 * BX, jnp.float32(1.0), above))

    def keep(x, r, u0, total):
        new = inside(x) * (u0 + total)
        u_ref[x, r] = new
        k_ref[x, r] = coeff(e_ref[x, r], new)

    def keep_first(x, r, u0, total):
        g_ref[x, r] = later * (u0 + STEPS * total)
        keep(x, r, u0, total)

    def keep_last(x, r, u0, total):
        s_ref[x - BX, pl.ds(r, 8, stride=PARTS), :] = (u0 + total) - g_ref[x, r]

    step(1, 3 * BX // 2 - 1, keep_first)

    def middle(t, _):
        step(t, 3 * BX // 2 - t, keep)
        return 0

    lax.fori_loop(2, STEPS, middle, 0)
    step(BX, BX // 2, keep_last)

    def spread(x, _):
        for j in range(SLICES):
            for c in range(3):
                strip = j + c - 1
                if 0 <= strip < SLICES:
                    tile = s_ref[x, strip * ROWS : (strip + 1) * ROWS, :]
                else:
                    tile = jnp.zeros((ROWS, NZ), jnp.float32)
                out[j, x, c * ROWS : (c + 1) * ROWS, :] = tile
        return 0

    lax.fori_loop(0, BX, spread, 0)


def fine(low, own, high):
    f32 = jnp.float32
    grid = (3 * BX + 1, PARTS, 8, NZ)
    return pl.pallas_call(
        fine_kernel,
        out_shape=jax.ShapeDtypeStruct((SLICES, BX, EXT, NZ), f32),
        in_specs=[VMEM] * 3,
        out_specs=VMEM,
        scratch_shapes=[
            pltpu.VMEM(grid, f32),
            pltpu.VMEM(grid, f32),
            pltpu.VMEM(grid, f32),
            pltpu.VMEM(grid, f32),
            pltpu.VMEM(grid[1:], f32),
            pltpu.VMEM((BX, NY, NZ), f32),
        ],
        compiler_params=pltpu.CompilerParams(vmem_limit_bytes=24 << 20),
        name="fine",
    )(low, own, high)


def pack_kernel(sent, down, up):
    row = lax.broadcasted_iota(jnp.int32, (ROWS, NZ), 0)

    def tile(i, x, c):
        return sent[i, x, c * ROWS : (c + 1) * ROWS, :]

    for n, (i, d, kind) in enumerate(TILES):
        for ref, x in ((down, d - 1), (up, BX - d)):
            if kind == "mid":
                value = tile(i, x, 1)
            elif kind == "both":
                value = jnp.where(row < 4, tile(i, x, 2), tile(i, x, 0))
            else:
                value = tile(i, x, 0 if kind == "low" else 2)
            ref[n] = value


def pack(sent):
    shape = jax.ShapeDtypeStruct((len(TILES), ROWS, NZ), jnp.float32)
    return pl.pallas_call(
        pack_kernel,
        out_shape=(shape, shape),
        in_specs=[VMEM],
        out_specs=(VMEM, VMEM),
        compiler_params=pltpu.CompilerParams(vmem_limit_bytes=8 << 20),
        name="pack",
    )(sent)


def strip_kernel(low, own, high, out):
    tm = lax.axis_index("tm")
    for c in range(3):
        strip = tm + (c - 1)
        scale = jnp.where((strip >= 0) & (strip < SLICES), float(STEPS), 0.0).astype(jnp.float32)
        strip = jnp.clip(strip, 0, SLICES - 1)
        start = lax.rem(strip, 2) * 64 + lax.div(strip, 2)
        for b, ref in enumerate((low, own, high)):
            for x in range(BX):
                out[b * BX + x, c] = scale * ref[BX + x, pl.ds(start, 8, stride=8), :]


def strip_part(low, own, high):
    flat = [a.reshape(2 * BX, NY, NZ) for a in (low, own, high)]
    return pl.pallas_call(
        strip_kernel,
        out_shape=jax.ShapeDtypeStruct((3 * BX, 3, 8, NZ), jnp.float32),
        in_specs=[VMEM] * 3,
        out_specs=VMEM,
        compiler_params=pltpu.CompilerParams(vmem_limit_bytes=8 << 20),
        cost_estimate=pl.CostEstimate(flops=10**6, bytes_accessed=10**6, transcendentals=0),
        name="strip",
    )(*flat)


def sent_tile(refs, i, x, c):
    sent, below, above = refs
    if x < BX:
        return below[PLACE[i, BX - x, c]]
    if x >= 2 * BX:
        return above[PLACE[i, x - 2 * BX + 1, c]]
    return sent[i, x - BX, c * ROWS : (c + 1) * ROWS, :]


def coarse_steps(count, base, eta, refs, u_ref, k_ref, f_ref, out):
    lane, row = iotas()
    x_below, x_above = has_neighbours("space")
    y_below, y_above = has_neighbours("tm")
    once = jnp.where(lax.axis_index("space") < 0, 2, 1)

    def mask(x, c):
        factors = []
        if not BX <= x < 2 * BX:
            factors.append(x_below if x < BX else x_above)
        if c != 1:
            factors.append(y_below if c == 0 else y_above)
        return factors[0] * factors[1] if len(factors) == 2 else (factors or [None])[0]

    def begin(x, _):
        for c in range(3):
            k_ref[x, c] = coeff(eta[x, c], u_ref[x, c])
        return 0

    lax.fori_loop(BX - count, 2 * BX + count, begin, 0, unroll=4)

    def stretch(n, left, planes):
        def body(_, carry):
            flux = [None] * 3
            for x in planes:
                far = max(BX - x, x - (2 * BX - 1), 0)
                tiles = (0, 1, 2) if left - far >= 1 else (1,)
                us = [u_ref[x, c] for c in range(3)]
                ks = [k_ref[x, c] for c in range(3)]
                ru = [pltpu.roll(u, 7, 0) for u in us]
                rk = [pltpu.roll(k, 7, 0) for k in ks]
                ups = []
                for c in range(max(tiles) + 1):
                    un, kn = ru[c], rk[c]
                    if c < 2:
                        un = jnp.where(row == 7, ru[c + 1], un)
                        kn = jnp.where(row == 7, rk[c + 1], kn)
                    ups.append((ks[c] + kn) * (un - us[c]))
                rolled = [pltpu.roll(v, 1, 0) for v in ups]
                for c in tiles:
                    low = rolled[c]
                    if c > 0:
                        low = jnp.where(row == 0, rolled[c - 1], low)
                    u0, k0 = us[c], ks[c]
                    x_up = (k0 + k_ref[x + 1, c]) * (u_ref[x + 1, c] - u0)
                    x_low = flux[c]
                    if x_low is None:
                        if x == BX - (left if c == 1 else left - 1):
                            x_low = (k0 + k_ref[x - 1, c]) * (u0 - u_ref[x - 1, c])
                        else:
                            x_low = f_ref[c]
                    flux[c] = x_up
                    new = (u0 + (x_up - x_low) + (ups[c] - low) + z_flux(u0, k0, lane)) + (
                        sent_tile(refs, base + n, x, c)
                    )
                    m = mask(x, c)
                    if m is not None:
                        new = m * new
                    if left > 0:
                        u_ref[x, c] = new
                        k_ref[x, c] = coeff(eta[x, c], new)
                    if c == 1 and far == 0:
                        out[base + n, x - BX] = new
            for c in range(3):
                if flux[c] is not None:
                    f_ref[c] = flux[c]
            return carry

        lax.fori_loop(0, once, body, 0)

    for n in range(1, count + 1):
        left = count - n
        planes = list(range(BX - left, 2 * BX + left))
        parts = -(-len(planes) * (3 if left else 1) // GROUP)
        size = -(-len(planes) // parts)
        for a in range(0, len(planes), size):
            stretch(n, left, planes[a : a + size])


def first_kernel(eta, sent, below, above, out, u_ref, k_ref, f_ref):
    refs = (sent, below, above)
    for x in range(BX - FIRST, 2 * BX + FIRST):
        for c in range(3):
            if BX <= x < 2 * BX or c == 1 or max(BX - x, x - 2 * BX + 1) < FIRST:
                u_ref[x, c] = sent_tile(refs, 0, x, c)
            else:
                u_ref[x, c] = jnp.zeros((8, NZ), jnp.float32)
    for x in range(BX):
        out[0, x] = sent[0, x, ROWS : 2 * ROWS, :]
    coarse_steps(FIRST, 0, eta, refs, u_ref, k_ref, f_ref, out)


def second_kernel(eta, sent, below, above, low_u, own_u, high_u, done, out, u_ref, k_ref, f_ref):
    for b, ref in enumerate((low_u, own_u, high_u)):
        for x in range(BX):
            for c in range(3):
                u_ref[b * BX + x, c] = ref[x, c * ROWS : (c + 1) * ROWS, :]
    for i in range(FIRST + 1):
        for x in range(BX):
            out[i, x] = done[i, x]
    refs = (sent, below, above)
    coarse_steps(SLICES - 1 - FIRST, FIRST, eta, refs, u_ref, k_ref, f_ref, out)


def coarse_call(kernel, name, count, *operands):
    f32 = jnp.float32
    return pl.pallas_call(
        kernel,
        out_shape=jax.ShapeDtypeStruct((count, BX, ROWS, NZ), f32),
        in_specs=[VMEM] * len(operands),
        out_specs=VMEM,
        scratch_shapes=[
            pltpu.VMEM((3 * BX, 3, 8, NZ), f32),
            pltpu.VMEM((3 * BX, 3, 8, NZ), f32),
            pltpu.VMEM((3, 8, NZ), f32),
        ],
        compiler_params=pltpu.CompilerParams(vmem_limit_bytes=8 << 20),
        name=name,
    )(*operands)


def both_ways(down, up, axis):
    count = lax.axis_size(axis)
    forward = [(i, i + 1) for i in range(count - 1)]
    backward = [(i + 1, i) for i in range(count - 1)]
    return lax.ppermute(up, axis, forward), lax.ppermute(down, axis, backward)


def per_device(start_values, regions, resistivity):
    own = own_part(start_values[0], regions, resistivity)
    low, high = both_ways(own, own, "space")
    sent = lax.all_to_all(fine(low, own, high), "tm", 0, 0)
    below, above = both_ways(*pack(sent), "space")
    eta = strip_part(low, own, high)
    done = coarse_call(first_kernel, "first", FIRST + 1, eta, sent, below, above)
    state = done[FIRST]
    y_low, y_high = both_ways(state, state, "tm")
    strip = jnp.concatenate([y_low, state, y_high], axis=1)
    x_low, x_high = both_ways(strip, strip, "space")
    ends = coarse_call(
        second_kernel, "second", SLICES, eta, sent, below, above, x_low, strip, x_high, done
    )
    result = lax.all_to_all(ends, "tm", 0, 0)
    result = jnp.transpose(result, (1, 0, 2, 3)).reshape(BX, NY, NZ)
    return result[None]


def solution(mesh):
    in_specs = (P("tm", "space", None, None), P("space", None, None), P())
    out_specs = P("tm", "space", None, None)
    return jax.shard_map(
        per_device, mesh=mesh, in_specs=in_specs, out_specs=out_specs, check_vma=False
    )
```

time: 162 us -> 119 us (0.73)
  the two profiles are of different devices: /device:TPU:128 before, /device:TPU:96 now
where the time goes in v2:
time: 119 us; the launch traced here: 117 us
  blocking collectives  47.6 us (40%)
  waiting for transfers between devices  23.5 us (20%)
  starting transfers between devices  21.6 us (18%)
  Pallas kernels  20.4 us (17%)
  local copies, waits for them, and re-layouts  3.57 us (3%)
    all_to_all x1, blocking collectives, per_device(): sent = lax.all_to_all(fine(low, own, high), 'tm', 0, 0)  30.5 us
    ppermute x8, waiting for transfers between devices, both_ways(): return (lax.ppermute(up, axis, forward), lax.ppermute(down, axis, backward))  23.5 us
    ppermute x8, starting transfers between devices, both_ways(): return (lax.ppermute(up, axis, forward), lax.ppermute(down, axis, backward))  21.6 us
    all_to_all x1, blocking collectives, per_device(): result = lax.all_to_all(ends, 'tm', 0, 0)  17.1 us
    pallas_call x1, Pallas kernels, fine(): pl.pallas_call(fine_kernel, out_shape=jax.ShapeDtypeStruct((SLICES, BX, E...  14.1 us
    pallas_call x2, Pallas kernels, coarse_call(): pl.pallas_call(kernel, out_shape=jax.ShapeDtypeStruct((count, BX, ROWS, N...  5.16 us
    unnamed x6, local copies, waits for them, and re-layouts  2.74 us
  transfers between devices with their start and end apart: 8, of which 6 were waited for; matrix products, arithmetic and copies ran while one was open for 0% of the time, Pallas kernels for 0%

profile of v2, /device:TPU:96, one launch (start us, length us, event | category | flops | bytes accessed | tf_op | source)
XLA Modules:
  0.0 116.8 jit_solution(11994555620968579208)
XLA Ops:
  0.0 0.0 copy-start
  0.0 1.0 copy-done
  1.0 0.0 copy-start.1
  1.0 1.0 copy-done.1
  2.1 0.0 copy-start.2
  2.1 0.7 copy-done.2
  2.7 1.0 own.1
  3.7 1.9 %collective-permute-start.1 = (f32[16,16,8,128]{3,2,1,0:T(8,128)S(1)}, f32[16,16,8,128]{3,2,1,0:T(8,128)S(1)}, u32[]{:S(2)}, u32[]{:S(2)}) collective-permute-start(f32[16,16,8,128]{3,2,1,0:T(8,128)S(1)} %own.1), channel_id=1, source_target_pairs={{1,0},{2,1},{3,2},{4,3},{5,4},{6,5},{7,6},{8,7},{9,8},{10,9},{11,1... | collective-permute-start | bytes 3145736 | tf_op jit(solution)/shard_map/ppermute | solution.py:401
  5.7 2.4 %collective-permute-start = (f32[16,16,8,128]{3,2,1,0:T(8,128)S(1)}, f32[16,16,8,128]{3,2,1,0:T(8,128)S(1)}, u32[]{:S(2)}, u32[]{:S(2)}) collective-permute-start(f32[16,16,8,128]{3,2,1,0:T(8,128)S(1)} %own.1), channel_id=1, source_target_pairs={{0,1},{1,2},{2,3},{3,4},{4,5},{5,6},{6,7},{7,8},{8,9},{9,10},{10,1... | collective-permute-start | bytes 3145736 | tf_op jit(solution)/shard_map/ppermute | solution.py:401
  8.1 9.9 %collective-permute-done.1.high = f32[16,16,8,128]{3,2,1,0:T(8,128)S(1)} collective-permute-done((f32[16,16,8,128]{3,2,1,0:T(8,128)S(1)}, f32[16,16,8,128]{3,2,1,0:T(8,128)S(1)}, u32[]{:S(2)}, u32[]{:S(2)}) %collective-permute-start.1) | collective-permute-done | bytes 1048608 | tf_op jit(solution)/shard_map/ppermute | solution.py:401
  18.0 3.8 %collective-permute-done.low = f32[16,16,8,128]{3,2,1,0:T(8,128)S(1)} collective-permute-done((f32[16,16,8,128]{3,2,1,0:T(8,128)S(1)}, f32[16,16,8,128]{3,2,1,0:T(8,128)S(1)}, u32[]{:S(2)}, u32[]{:S(2)}) %collective-permute-start) | collective-permute-done | bytes 1048608 | tf_op jit(solution)/shard_map/ppermute | solution.py:401
  21.8 14.1 %fine.1 = f32[16,8,24,128]{3,2,1,0:T(8,128)S(1)} custom-call(f32[16,16,8,128]{3,2,1,0:T(8,128)S(1)} %collective-permute-done.low, f32[16,16,8,128]{3,2,1,0:T(8,128)S(1)} %own.1, f32[16,16,8,128]{3,2,1,0:T(8,128)S(1)} %collective-permute-done.1.high), custom_call_target="tpu_custom_call" | custom-call | tf_op jit(solution)/shard_map/fine/pallas_call | solution.py:195
  35.9 30.5 %all_to_all.10.sent = f32[16,8,24,128]{3,2,1,0:T(8,128)S(1)} all-to-all(f32[16,8,24,128]{3,2,1,0:T(8,128)S(1)} %fine.1), channel_id=1, replica_groups=mesh['tm'=16,'space'=32] {'tm'}, dimensions={0} | all-to-all | bytes 3145728 | tf_op jit(solution)/shard_map/all_to_all | solution.py:407
  66.3 0.1 pack.1
  66.4 1.9 %collective-permute-start.2 = (f32[104,8,128]{2,1,0:T(8,128)S(1)}, f32[104,8,128]{2,1,0:T(8,128)S(1)}, u32[]{:S(2)}, u32[]{:S(2)}) collective-permute-start(f32[104,8,128]{2,1,0:T(8,128)S(1)} %get-tuple-element.7), channel_id=1, source_target_pairs={{0,1},{1,2},{2,3},{3,4},{4,5},{5,6},{6,7},{7,8},{8,9},{9,10},{10,1... | collective-permute-start | bytes 1277960 | tf_op jit(solution)/shard_map/ppermute | solution.py:401
  68.3 3.6 %collective-permute-start.3 = (f32[104,8,128]{2,1,0:T(8,128)S(1)}, f32[104,8,128]{2,1,0:T(8,128)S(1)}, u32[]{:S(2)}, u32[]{:S(2)}) collective-permute-start(f32[104,8,128]{2,1,0:T(8,128)S(1)} %get-tuple-element.8), channel_id=1, source_target_pairs={{1,0},{2,1},{3,2},{4,3},{5,4},{6,5},{7,6},{8,7},{9,8},{10,9},{11,1... | collective-permute-start | bytes 1277960 | tf_op jit(solution)/shard_map/ppermute | solution.py:401
  72.0 0.1 strip.1.eta
  72.1 3.8 %collective-permute-done.2.below = f32[104,8,128]{2,1,0:T(8,128)S(1)} collective-permute-done((f32[104,8,128]{2,1,0:T(8,128)S(1)}, f32[104,8,128]{2,1,0:T(8,128)S(1)}, u32[]{:S(2)}, u32[]{:S(2)}) %collective-permute-start.2) | collective-permute-done | bytes 426016 | tf_op jit(solution)/shard_map/ppermute | solution.py:401
  75.9 1.8 %collective-permute-done.3.above = f32[104,8,128]{2,1,0:T(8,128)S(1)} collective-permute-done((f32[104,8,128]{2,1,0:T(8,128)S(1)}, f32[104,8,128]{2,1,0:T(8,128)S(1)}, u32[]{:S(2)}, u32[]{:S(2)}) %collective-permute-start.3) | collective-permute-done | bytes 426016 | tf_op jit(solution)/shard_map/ppermute | solution.py:401
  77.6 2.4 %first.1.done = f32[8,8,8,128]{3,2,1,0:T(8,128)S(1)} custom-call(f32[24,3,8,128]{3,2,1,0:T(8,128)S(1)} %strip.1.eta, f32[16,8,24,128]{3,2,1,0:T(8,128)S(1)} %all_to_all.10.sent, f32[104,8,128]{2,1,0:T(8,128)S(1)} %collective-permute-done.2.below, f32[104,8,128]{2,1,0:T(8,128)S(1)} %collective-permute-done.3.above), custom_call_target="tpu_custom_call" | custom-call | tf_op jit(solution)/shard_map/first/pallas_call | solution.py:382
  80.0 1.3 %collective-permute-start.5 = (f32[8,8,128]{2,1,0:T(8,128)S(1)}, f32[8,8,128]{2,1,0:T(8,128)S(1)}, u32[]{:S(2)}, u32[]{:S(2)}) collective-permute-start(f32[8,8,128]{2,1,0:T(8,128)S(1)} %slice_bitcast_fusion), channel_id=1, source_target_pairs={{32,0},{64,32},{96,64},{128,96},{160,128},{192,160},{224,192},{256... | collective-permute-start | bytes 98312 | tf_op jit(solution)/shard_map/ppermute | solution.py:401
  81.3 4.5 %collective-permute-start.4 = (f32[8,8,128]{2,1,0:T(8,128)S(1)}, f32[8,8,128]{2,1,0:T(8,128)S(1)}, u32[]{:S(2)}, u32[]{:S(2)}) collective-permute-start(f32[8,8,128]{2,1,0:T(8,128)S(1)} %slice_bitcast_fusion), channel_id=1, source_target_pairs={{0,32},{32,64},{64,96},{96,128},{128,160},{160,192},{192,224},{224... | collective-permute-start | bytes 98312 | tf_op jit(solution)/shard_map/ppermute | solution.py:401
  85.8 0.0 collective-permute-done.5
  85.9 1.6 %collective-permute-done.4 = f32[8,8,128]{2,1,0:T(8,128)S(1)} collective-permute-done((f32[8,8,128]{2,1,0:T(8,128)S(1)}, f32[8,8,128]{2,1,0:T(8,128)S(1)}, u32[]{:S(2)}, u32[]{:S(2)}) %collective-permute-start.4) | collective-permute-done | bytes 32800 | tf_op jit(solution)/shard_map/ppermute | solution.py:401
  87.4 2.7 %collective-permute-start.7 = (f32[8,24,128]{2,1,0:T(8,128)S(1)}, f32[8,24,128]{2,1,0:T(8,128)S(1)}, u32[]{:S(2)}, u32[]{:S(2)}) collective-permute-start(f32[8,24,128]{2,1,0:T(8,128)S(1)} %pad_maximum_fusion.own_u), channel_id=1, source_target_pairs={{1,0},{2,1},{3,2},{4,3},{5,4},{6,5},{7,6},{8,7},{9,8},{10,9},{11,1... | collective-permute-start | bytes 294920 | tf_op jit(solution)/shard_map/ppermute | solution.py:401
  90.1 3.2 %collective-permute-start.6 = (f32[8,24,128]{2,1,0:T(8,128)S(1)}, f32[8,24,128]{2,1,0:T(8,128)S(1)}, u32[]{:S(2)}, u32[]{:S(2)}) collective-permute-start(f32[8,24,128]{2,1,0:T(8,128)S(1)} %pad_maximum_fusion.own_u), channel_id=1, source_target_pairs={{0,1},{1,2},{2,3},{3,4},{4,5},{5,6},{6,7},{7,8},{8,9},{9,10},{10,1... | collective-permute-start | bytes 294920 | tf_op jit(solution)/shard_map/ppermute | solution.py:401
  93.3 0.0 collective-permute-done.7.high_u
  93.3 2.7 %collective-permute-done.6.low_u = f32[8,24,128]{2,1,0:T(8,128)S(1)} collective-permute-done((f32[8,24,128]{2,1,0:T(8,128)S(1)}, f32[8,24,128]{2,1,0:T(8,128)S(1)}, u32[]{:S(2)}, u32[]{:S(2)}) %collective-permute-start.6) | collective-permute-done | bytes 98336 | tf_op jit(solution)/shard_map/ppermute | solution.py:401
  96.0 2.8 %second.1 = f32[16,8,8,128]{3,2,1,0:T(8,128)S(1)} custom-call(f32[24,3,8,128]{3,2,1,0:T(8,128)S(1)} %strip.1.eta, f32[16,8,24,128]{3,2,1,0:T(8,128)S(1)} %all_to_all.10.sent, f32[104,8,128]{2,1,0:T(8,128)S(1)} %collective-permute-done.2.below, f32[104,8,128]{2,1,0:T(8,128)S(1)} %collective-permute-done.3.above, ...), custom_call_target="tpu_custom_call" | custom-call | tf_op jit(solution)/shard_map/second/pallas_call | solution.py:382
  98.9 17.1 %all_to_all.11 = f32[16,8,8,128]{3,2,1,0:T(8,128)S(1)} all-to-all(f32[16,8,8,128]{3,2,1,0:T(8,128)S(1)} %second.1), channel_id=1, replica_groups=mesh['tm'=16,'space'=32] {'tm'}, dimensions={0} | all-to-all | bytes 1048576 | tf_op jit(solution)/shard_map/all_to_all | solution.py:418
  116.0 0.8 copy_bitcast_fusion
  (2 shorter events, 0.0 us)
Async XLA Ops:
  0.0 1.0 copy-start
  1.0 1.0 copy-start.1
  2.1 0.7 copy-start.2
  3.7 14.2 %collective-permute-start.1 = (f32[16,16,8,128]{3,2,1,0:T(8,128)S(1)}, f32[16,16,8,128]{3,2,1,0:T(8,128)S(1)}, u32[]{:S(2)}, u32[]{:S(2)}) collective-permute-start(f32[16,16,8,128]{3,2,1,0:T(8,128)S(1)} %own.1), channel_id=1, source_target_pairs={{1,0},{2,1},{3,2},{4,3},{5,4},{6,5},{7,6},{8,7},{9,8},{10,9},{11,1... | collective-permute-start | bytes 3145736 | tf_op jit(solution)/shard_map/ppermute | solution.py:401
  5.7 16.1 %collective-permute-start = (f32[16,16,8,128]{3,2,1,0:T(8,128)S(1)}, f32[16,16,8,128]{3,2,1,0:T(8,128)S(1)}, u32[]{:S(2)}, u32[]{:S(2)}) collective-permute-start(f32[16,16,8,128]{3,2,1,0:T(8,128)S(1)} %own.1), channel_id=1, source_target_pairs={{0,1},{1,2},{2,3},{3,4},{4,5},{5,6},{6,7},{7,8},{8,9},{9,10},{10,1... | collective-permute-start | bytes 3145736 | tf_op jit(solution)/shard_map/ppermute | solution.py:401
  66.4 9.4 %collective-permute-start.2 = (f32[104,8,128]{2,1,0:T(8,128)S(1)}, f32[104,8,128]{2,1,0:T(8,128)S(1)}, u32[]{:S(2)}, u32[]{:S(2)}) collective-permute-start(f32[104,8,128]{2,1,0:T(8,128)S(1)} %get-tuple-element.7), channel_id=1, source_target_pairs={{0,1},{1,2},{2,3},{3,4},{4,5},{5,6},{6,7},{7,8},{8,9},{9,10},{10,1... | collective-permute-start | bytes 1277960 | tf_op jit(solution)/shard_map/ppermute | solution.py:401
  68.3 9.3 %collective-permute-start.3 = (f32[104,8,128]{2,1,0:T(8,128)S(1)}, f32[104,8,128]{2,1,0:T(8,128)S(1)}, u32[]{:S(2)}, u32[]{:S(2)}) collective-permute-start(f32[104,8,128]{2,1,0:T(8,128)S(1)} %get-tuple-element.8), channel_id=1, source_target_pairs={{1,0},{2,1},{3,2},{4,3},{5,4},{6,5},{7,6},{8,7},{9,8},{10,9},{11,1... | collective-permute-start | bytes 1277960 | tf_op jit(solution)/shard_map/ppermute | solution.py:401
  80.0 5.9 %collective-permute-start.5 = (f32[8,8,128]{2,1,0:T(8,128)S(1)}, f32[8,8,128]{2,1,0:T(8,128)S(1)}, u32[]{:S(2)}, u32[]{:S(2)}) collective-permute-start(f32[8,8,128]{2,1,0:T(8,128)S(1)} %slice_bitcast_fusion), channel_id=1, source_target_pairs={{32,0},{64,32},{96,64},{128,96},{160,128},{192,160},{224,192},{256... | collective-permute-start | bytes 98312 | tf_op jit(solution)/shard_map/ppermute | solution.py:401
  81.3 6.1 %collective-permute-start.4 = (f32[8,8,128]{2,1,0:T(8,128)S(1)}, f32[8,8,128]{2,1,0:T(8,128)S(1)}, u32[]{:S(2)}, u32[]{:S(2)}) collective-permute-start(f32[8,8,128]{2,1,0:T(8,128)S(1)} %slice_bitcast_fusion), channel_id=1, source_target_pairs={{0,32},{32,64},{64,96},{96,128},{128,160},{160,192},{192,224},{224... | collective-permute-start | bytes 98312 | tf_op jit(solution)/shard_map/ppermute | solution.py:401
  87.4 5.9 %collective-permute-start.7 = (f32[8,24,128]{2,1,0:T(8,128)S(1)}, f32[8,24,128]{2,1,0:T(8,128)S(1)}, u32[]{:S(2)}, u32[]{:S(2)}) collective-permute-start(f32[8,24,128]{2,1,0:T(8,128)S(1)} %pad_maximum_fusion.own_u), channel_id=1, source_target_pairs={{1,0},{2,1},{3,2},{4,3},{5,4},{6,5},{7,6},{8,7},{9,8},{10,9},{11,1... | collective-permute-start | bytes 294920 | tf_op jit(solution)/shard_map/ppermute | solution.py:401
  90.1 5.9 %collective-permute-start.6 = (f32[8,24,128]{2,1,0:T(8,128)S(1)}, f32[8,24,128]{2,1,0:T(8,128)S(1)}, u32[]{:S(2)}, u32[]{:S(2)}) collective-permute-start(f32[8,24,128]{2,1,0:T(8,128)S(1)} %pad_maximum_fusion.own_u), channel_id=1, source_target_pairs={{0,1},{1,2},{2,3},{3,4},{4,5},{5,6},{6,7},{7,8},{8,9},{9,10},{10,1... | collective-permute-start | bytes 294920 | tf_op jit(solution)/shard_map/ppermute | solution.py:401

commit v3 on v2

--- a/solution.py
+++ b/solution.py
@@ -9,6 +9,7 @@
 fine_step = 0.008
 
 BX = 8
+HALF = BX // 2
 NY = 128
 NZ = 128
 SLICES = 16
@@ -73,51 +74,79 @@
     return below, above
 
 
-def own_kernel(start, regions, resistivity, out):
-    scaled = [resistivity[i] * jnp.float32(0.5 * fine_step) for i in range(REGIONS)]
-
-    def plane(x, _):
-        for r in range(PARTS):
-            out[x, r] = start[x, pl.ds(r, 8, stride=PARTS), :]
-            region = regions[x, pl.ds(r, 8, stride=PARTS), :]
-            value = jnp.zeros((8, NZ), jnp.float32)
-            for i in range(REGIONS):
-                value = jnp.where(region == i, scaled[i], value)
-            out[BX + x, r] = value
-        return 0
-
-    lax.fori_loop(0, BX, plane, 0)
+def own_kernel(start, regions, resistivity, *refs):
+    outs, (start_v, regions_v, resistivity_s, sems) = refs[:2], refs[2:]
+    small = pltpu.make_async_copy(resistivity, resistivity_s, sems.at[4])
+    small.start()
+    copies = []
+    for h in range(2):
+        part = pl.ds(h * HALF, HALF)
+        pair = (
+            pltpu.make_async_copy(start.at[part], start_v.at[part], sems.at[2 * h]),
+            pltpu.make_async_copy(regions.at[part], regions_v.at[part], sems.at[2 * h + 1]),
+        )
+        for copy in pair:
+            copy.start()
+        copies.append(pair)
+    small.wait()
+    scaled = [resistivity_s[i] * jnp.float32(0.5 * fine_step) for i in range(REGIONS)]
+    for h in range(2):
+        for copy in copies[h]:
+            copy.wait()
+
+        def plane(x, _, h=h):
+            for r in range(PARTS):
+                outs[h][x, r] = start_v[h * HALF + x, pl.ds(r, 8, stride=PARTS), :]
+                region = regions_v[h * HALF + x, pl.ds(r, 8, stride=PARTS), :]
+                value = jnp.zeros((8, NZ), jnp.float32)
+                for i in range(REGIONS):
+                    value = jnp.where(region == i, scaled[i], value)
+                outs[h][HALF + x, r] = value
+            return 0
+
+        lax.fori_loop(0, HALF, plane, 0)
 
 
 def own_part(start, regions, resistivity):
+    hbm = pl.BlockSpec(memory_space=pltpu.MemorySpace.HBM)
+    shape = jax.ShapeDtypeStruct((2 * HALF, PARTS, 8, NZ), jnp.float32)
     return pl.pallas_call(
         own_kernel,
-        out_shape=jax.ShapeDtypeStruct((2 * BX, PARTS, 8, NZ), jnp.float32),
-        in_specs=[VMEM, VMEM, SMEM],
-        out_specs=VMEM,
-        compiler_params=pltpu.CompilerParams(vmem_limit_bytes=8 << 20),
+        out_shape=(shape, shape),
+        in_specs=[hbm] * 3,
+        out_specs=(VMEM, VMEM),
+        scratch_shapes=[
+            pltpu.VMEM((BX, NY, NZ), jnp.float32),
+            pltpu.VMEM((BX, NY, NZ), jnp.int32),
+            pltpu.SMEM((REGIONS,), jnp.float32),
+            pltpu.SemaphoreType.DMA((5,)),
+        ],
+        compiler_params=pltpu.CompilerParams(vmem_limit_bytes=60 << 20),
         name="own",
     )(start, regions, resistivity)
 
 
-def fine_kernel(low, own, high, out, u_ref, k_ref, e_ref, g_ref, f_ref, s_ref):
-    below, above = has_neighbours("space")
-    later = jnp.where(lax.axis_index("tm") == 0, 0.0, 1.0).astype(jnp.float32)
-    lane, sub = iotas()
-
-    for b, ref in enumerate((low, own, high)):
-
-        def stage(x, _, b=b, ref=ref):
+class Fine:
+    def __init__(self, u_ref, k_ref, e_ref, f_ref):
+        self.u, self.k, self.e, self.f = u_ref, k_ref, e_ref, f_ref
+        self.below, self.above = has_neighbours("space")
+        self.lane, self.sub = iotas()
+
+    def stage(self, ref, base):
+        def one(x, _):
             for r in range(PARTS):
-                u, e = ref[x, r], ref[BX + x, r]
-                u_ref[b * BX + x, r] = u
-                e_ref[b * BX + x, r] = e
-                k_ref[b * BX + x, r] = coeff(e, u)
+                u, e = ref[x, r], ref[HALF + x, r]
+                self.u[base + x, r] = u
+                self.e[base + x, r] = e
+                self.k[base + x, r] = coeff(e, u)
             return 0
 
-        lax.fori_loop(0, BX, stage, 0)
-
-    def plane(x, emit):
+        lax.fori_loop(0, HALF, one, 0)
+
+    def plane(self, x, emit, next_u=None, next_k=None):
+        u_ref, k_ref, f_ref, sub = self.u, self.k, self.f, self.sub
+        if next_u is None:
+            next_u, next_k = u_ref.at[x + 1], k_ref.at[x + 1]
         u0, k0 = u_ref[x, 0], k_ref[x, 0]
         u_end, k_end = u_ref[x, PARTS - 1], k_ref[x, PARTS - 1]
         wrap_u = jnp.where(sub == 7, 0.0, pltpu.roll(u0, 7, 0))
@@ -131,49 +160,90 @@
             else:
                 u1 = k1 = None
                 y_up = top
-            x_up = (k0 + k_ref[x + 1, r]) * (u_ref[x + 1, r] - u0)
+            x_up = (k0 + next_k[r]) * (next_u[r] - u0)
             x_low = f_ref[r]
             f_ref[r] = x_up
-            total = (x_up - x_low) + (y_up - y_low) + z_flux(u0, k0, lane)
+            total = (x_up - x_low) + (y_up - y_low) + z_flux(u0, k0, self.lane)
             emit(x, r, u0, total)
             u0, k0, y_low = u1, k1, y_up
 
-    def step(first, pairs, emit):
+    def begin(self, x, low_u, low_k):
         for r in range(PARTS):
-            f_ref[r] = (k_ref[first - 1, r] + k_ref[first, r]) * (
-                u_ref[first, r] - u_ref[first - 1, r]
-            )
-
+            self.f[r] = (low_k[r] + self.k[x, r]) * (self.u[x, r] - low_u[r])
+
+    def pairs(self, first, count, emit):
         def pair(n, _):
             for q in range(2):
-                plane(first + 2 * n + q, emit)
+                self.plane(first + 2 * n + q, emit)
             return 0
 
-        lax.fori_loop(0, pairs, pair, 0)
-
-    def inside(x):
-        return jnp.where(x < BX, below, jnp.where(x < 2 * BX, jnp.float32(1.0), above))
-
-    def keep(x, r, u0, total):
-        new = inside(x) * (u0 + total)
-        u_ref[x, r] = new
-        k_ref[x, r] = coeff(e_ref[x, r], new)
+        lax.fori_loop(0, count, pair, 0)
+
+    def step(self, first, count, emit):
+        self.begin(first, self.u.at[first - 1], self.k.at[first - 1])
+        self.pairs(first, count, emit)
+
+    def keep(self, x, r, u0, total):
+        inside = jnp.where(x < BX, self.below, jnp.where(x < 2 * BX, jnp.float32(1.0), self.above))
+        new = inside * (u0 + total)
+        self.u[x, r] = new
+        self.k[x, r] = coeff(self.e[x, r], new)
+
+
+def inner_kernel(low, own_a, own_b, high, u_ref, k_ref, e_ref, g_ref, save, f_ref):
+    later = jnp.where(lax.axis_index("tm") == 0, 0.0, 1.0).astype(jnp.float32)
+    fine = Fine(u_ref, k_ref, e_ref, f_ref)
+    for n, ref in enumerate((low, own_a, own_b, high)):
+        fine.stage(ref, (n + 1) * HALF)
 
     def keep_first(x, r, u0, total):
-        g_ref[x, r] = later * (u0 + STEPS * total)
-        keep(x, r, u0, total)
+        g_ref[x - HALF, r] = later * (u0 + STEPS * total)
+        fine.keep(x, r, u0, total)
+
+    def stow(t):
+        for r in range(PARTS):
+            save[0, t, r] = u_ref[HALF + t, r]
+            save[1, t, r] = k_ref[HALF + t, r]
+            save[2, t, r] = u_ref[5 * HALF - 1 - t, r]
+            save[3, t, r] = k_ref[5 * HALF - 1 - t, r]
+
+    stow(1)
+    fine.step(HALF + 1, 2 * HALF - 1, keep_first)
+
+    def later_step(t, _):
+        stow(t)
+        fine.step(HALF + t, 2 * HALF - t, fine.keep)
+        return 0
+
+    lax.fori_loop(2, HALF + 1, later_step, 0)
+
+
+def outer_kernel(low, high, u_in, k_in, e_in, g_ref, save, out, u_ref, k_ref, e_ref, f_ref, s_ref):
+    fine = Fine(u_ref, k_ref, e_ref, f_ref)
+    fine.stage(low, 0)
+    fine.stage(high, 5 * HALF)
+
+    def wedges(t, _):
+        fine.begin(t, u_ref.at[t - 1], k_ref.at[t - 1])
+        fine.pairs(t, 1, fine.keep)
+        fine.plane(t + 2, fine.keep)
+        fine.plane(t + 3, fine.keep, save.at[0, t], save.at[1, t])
+        fine.begin(5 * HALF - t, save.at[2, t], save.at[3, t])
+        fine.pairs(5 * HALF - t, 2, fine.keep)
+        return 0
+
+    lax.fori_loop(1, HALF + 1, wedges, 0)
+
+    def later_step(t, _):
+        fine.step(t, 3 * HALF - t, fine.keep)
+        return 0
+
+    lax.fori_loop(HALF + 1, STEPS, later_step, 0)
 
     def keep_last(x, r, u0, total):
-        s_ref[x - BX, pl.ds(r, 8, stride=PARTS), :] = (u0 + total) - g_ref[x, r]
-
-    step(1, 3 * BX // 2 - 1, keep_first)
-
-    def middle(t, _):
-        step(t, 3 * BX // 2 - t, keep)
-        return 0
-
-    lax.fori_loop(2, STEPS, middle, 0)
-    step(BX, BX // 2, keep_last)
+        s_ref[x - BX, pl.ds(r, 8, stride=PARTS), :] = (u0 + total) - g_ref[x - HALF, r]
+
+    fine.step(BX, HALF, keep_last)
 
     def spread(x, _):
         for j in range(SLICES):
@@ -189,25 +259,41 @@
     lax.fori_loop(0, BX, spread, 0)
 
 
-def fine(low, own, high):
+GRID = jax.ShapeDtypeStruct((3 * BX + 1, PARTS, 8, NZ), jnp.float32)
+
+
+def inner(low, own_a, own_b, high):
     f32 = jnp.float32
-    grid = (3 * BX + 1, PARTS, 8, NZ)
     return pl.pallas_call(
-        fine_kernel,
-        out_shape=jax.ShapeDtypeStruct((SLICES, BX, EXT, NZ), f32),
-        in_specs=[VMEM] * 3,
-        out_specs=VMEM,
-        scratch_shapes=[
-            pltpu.VMEM(grid, f32),
-            pltpu.VMEM(grid, f32),
-            pltpu.VMEM(grid, f32),
-            pltpu.VMEM(grid, f32),
-            pltpu.VMEM(grid[1:], f32),
-            pltpu.VMEM((BX, NY, NZ), f32),
-        ],
-        compiler_params=pltpu.CompilerParams(vmem_limit_bytes=24 << 20),
-        name="fine",
-    )(low, own, high)
+        inner_kernel,
+        out_shape=(
+            GRID,
+            GRID,
+            GRID,
+            jax.ShapeDtypeStruct((4 * HALF, PARTS, 8, NZ), f32),
+            jax.ShapeDtypeStruct((4, HALF + 1, PARTS, 8, NZ), f32),
+        ),
+        in_specs=[VMEM] * 4,
+        out_specs=(VMEM,) * 5,
+        scratch_shapes=[pltpu.VMEM((PARTS, 8, NZ), f32)],
+        compiler_params=pltpu.CompilerParams(vmem_limit_bytes=16 << 20),
+        cost_estimate=pl.CostEstimate(flops=10**8, bytes_accessed=10**7, transcendentals=0),
+        name="inner",
+    )(low, own_a, own_b, high)
+
+
+def outer(low, high, u, k, e, g, save):
+    f32 = jnp.float32
+    return pl.pallas_call(
+        outer_kernel,
+        out_shape=(jax.ShapeDtypeStruct((SLICES, BX, EXT, NZ), f32), GRID, GRID, GRID),
+        in_specs=[VMEM] * 7,
+        out_specs=(VMEM,) * 4,
+        scratch_shapes=[pltpu.VMEM((PARTS, 8, NZ), f32), pltpu.VMEM((BX, NY, NZ), f32)],
+        input_output_aliases={2: 1, 3: 2, 4: 3},
+        compiler_params=pltpu.CompilerParams(vmem_limit_bytes=16 << 20),
+        name="outer",
+    )(low, high, u, k, e, g, save)[0]
 
 
 def pack_kernel(sent, down, up):
@@ -239,24 +325,25 @@
     )(sent)
 
 
-def strip_kernel(low, own, high, out):
+def strip_kernel(*refs):
     tm = lax.axis_index("tm")
+    parts, out = refs[:-1], refs[-1]
     for c in range(3):
         strip = tm + (c - 1)
         scale = jnp.where((strip >= 0) & (strip < SLICES), float(STEPS), 0.0).astype(jnp.float32)
         strip = jnp.clip(strip, 0, SLICES - 1)
         start = lax.rem(strip, 2) * 64 + lax.div(strip, 2)
-        for b, ref in enumerate((low, own, high)):
-            for x in range(BX):
-                out[b * BX + x, c] = scale * ref[BX + x, pl.ds(start, 8, stride=8), :]
-
-
-def strip_part(low, own, high):
-    flat = [a.reshape(2 * BX, NY, NZ) for a in (low, own, high)]
+        for n, ref in enumerate(parts):
+            for x in range(HALF):
+                out[n * HALF + x, c] = scale * ref[HALF + x, pl.ds(start, 8, stride=8), :]
+
+
+def strip_part(*parts):
+    flat = [a.reshape(2 * HALF, NY, NZ) for a in parts]
     return pl.pallas_call(
         strip_kernel,
         out_shape=jax.ShapeDtypeStruct((3 * BX, 3, 8, NZ), jnp.float32),
-        in_specs=[VMEM] * 3,
+        in_specs=[VMEM] * len(parts),
         out_specs=VMEM,
         compiler_params=pltpu.CompilerParams(vmem_limit_bytes=8 << 20),
         cost_estimate=pl.CostEstimate(flops=10**6, bytes_accessed=10**6, transcendentals=0),
@@ -402,11 +489,13 @@
 
 
 def per_device(start_values, regions, resistivity):
-    own = own_part(start_values[0], regions, resistivity)
-    low, high = both_ways(own, own, "space")
-    sent = lax.all_to_all(fine(low, own, high), "tm", 0, 0)
+    own_a, own_b = own_part(start_values[0], regions, resistivity)
+    low_b, high_a = both_ways(own_a, own_b, "space")
+    low_a, high_b = both_ways(own_b, own_a, "space")
+    sent = outer(low_a, high_b, *inner(low_b, own_a, own_b, high_a))
+    sent = lax.all_to_all(sent, "tm", 0, 0)
     below, above = both_ways(*pack(sent), "space")
-    eta = strip_part(low, own, high)
+    eta = strip_part(low_a, low_b, own_a, own_b, high_a, high_b)
     done = coarse_call(first_kernel, "first", FIRST + 1, eta, sent, below, above)
     state = done[FIRST]
     y_low, y_high = both_ways(state, state, "tm")

time: 119 us -> 118 us (level); the launches traced: 117 us -> 117 us
  waiting for transfers between devices: 23.5 us -> 11.2 us
  starting transfers between devices: 21.6 us -> 28.5 us
  Pallas kernels: 20.4 us -> 24.9 us
  blocking collectives: 47.6 us -> 49.7 us
    ppermute x8 -> x10, waiting for transfers between devices: 23.5 us -> 11.2 us  [both_ways(): return (lax.ppermute(up, axis, forward), lax.ppermute(down, axis, backward))]
    ppermute x8 -> x10, starting transfers between devices: 21.6 us -> 28.5 us  [both_ways(): return (lax.ppermute(up, axis, forward), lax.ppermute(down, axis, backward))]
    pallas_call x2 -> x3, Pallas kernels: 15.1 us -> 19.6 us  [the longest x1 11.9 us: outer(): pl.pallas_call(outer_kernel, out_shape=(jax.ShapeDtypeStruct((SLICES, BX,...]
    all_to_all x1, blocking collectives: 17.1 us -> 19.4 us  [per_device(): result = lax.all_to_all(ends, 'tm', 0, 0)]
    unnamed x6 -> x4, local copies, waits for them, and re-layouts: 2.74 us -> 2.08 us
  transfers between devices with their start and end apart: 8 -> 10, of which waited for: 6 -> 5; matrix products, arithmetic and copies ran while one was open for 0% -> 0% of each run, Pallas kernels for 0% -> 5%
where the time goes in v3:
time: 118 us; the launch traced here: 117 us
  blocking collectives  49.7 us (42%)
  starting transfers between devices  28.5 us (24%)
  Pallas kernels  24.9 us (21%)
  waiting for transfers between devices  11.2 us (9%)
  local copies, waits for them, and re-layouts  2.91 us (2%)
    all_to_all x1, blocking collectives, per_device(): sent = lax.all_to_all(sent, 'tm', 0, 0)  30.3 us
    ppermute x10, starting transfers between devices, both_ways(): return (lax.ppermute(up, axis, forward), lax.ppermute(down, axis, backward))  28.5 us
    all_to_all x1, blocking collectives, per_device(): result = lax.all_to_all(ends, 'tm', 0, 0)  19.4 us
    pallas_call x1, Pallas kernels, outer(): pl.pallas_call(outer_kernel, out_shape=(jax.ShapeDtypeStruct((SLICES, BX,...  11.9 us
    ppermute x10, waiting for transfers between devices, both_ways(): return (lax.ppermute(up, axis, forward), lax.ppermute(down, axis, backward))  11.2 us
    pallas_call x1, Pallas kernels, inner(): pl.pallas_call(inner_kernel, out_shape=(GRID, GRID, GRID, jax.ShapeDtypeS...  5.31 us
    pallas_call x2, Pallas kernels, coarse_call(): pl.pallas_call(kernel, out_shape=jax.ShapeDtypeStruct((count, BX, ROWS, N...  5.16 us
    pallas_call x1, Pallas kernels, own_part(): pl.pallas_call(own_kernel, out_shape=(shape, shape), in_specs=[hbm] * 3,...  2.46 us
  transfers between devices with their start and end apart: 10, of which 5 were waited for; matrix products, arithmetic and copies ran while one was open for 0% of the time, Pallas kernels for 5%

profile of v3, /device:TPU:96, one launch (start us, length us, event | category | flops | bytes accessed | tf_op | source)
XLA Modules:
  0.0 117.4 jit_solution(16376118607517525627)
XLA Ops:
  0.0 2.5 %own.1 = (f32[8,16,8,128]{3,2,1,0:T(8,128)}, f32[8,16,8,128]{3,2,1,0:T(8,128)}) custom-call(f32[8,128,128]{2,1,0:T(8,128)} %bitcast.20, s32[8,128,128]{2,1,0:T(8,128)} %regions.1, f32[4]{0:T(128)} %resistivity.1), custom_call_target="tpu_custom_call" | custom-call | tf_op jit(solution)/shard_map/own/pallas_call | solution.py:113
  2.5 1.9 %collective-permute-start.2 = (f32[8,16,8,128]{3,2,1,0:T(8,128)}, f32[8,16,8,128]{3,2,1,0:T(8,128)S(1)}, u32[]{:S(2)}, u32[]{:S(2)}) collective-permute-start(f32[8,16,8,128]{3,2,1,0:T(8,128)} %get-tuple-element.15.own_a), channel_id=1, source_target_pairs={{1,0},{2,1},{3,2},{4,3},{5,4},{6,5},{7,6},{8,7},{9,8},{10,9},{11,1... | collective-permute-start | bytes 1572872 | tf_op jit(solution)/shard_map/ppermute | solution.py:488
  4.4 2.4 %collective-permute-start.1 = (f32[8,16,8,128]{3,2,1,0:T(8,128)}, f32[8,16,8,128]{3,2,1,0:T(8,128)S(1)}, u32[]{:S(2)}, u32[]{:S(2)}) collective-permute-start(f32[8,16,8,128]{3,2,1,0:T(8,128)} %get-tuple-element.16.own_b), channel_id=1, source_target_pairs={{0,1},{1,2},{2,3},{3,4},{4,5},{5,6},{6,7},{7,8},{8,9},{9,10},{10,1... | collective-permute-start | bytes 1572872 | tf_op jit(solution)/shard_map/ppermute | solution.py:488
  6.8 4.7 %collective-permute-start = (f32[8,16,8,128]{3,2,1,0:T(8,128)}, f32[8,16,8,128]{3,2,1,0:T(8,128)S(1)}, u32[]{:S(2)}, u32[]{:S(2)}) collective-permute-start(f32[8,16,8,128]{3,2,1,0:T(8,128)} %get-tuple-element.15.own_a), channel_id=1, source_target_pairs={{0,1},{1,2},{2,3},{3,4},{4,5},{5,6},{6,7},{7,8},{8,9},{9,10},{10,1... | collective-permute-start | bytes 1572872 | tf_op jit(solution)/shard_map/ppermute | solution.py:488
  11.5 1.9 %collective-permute-start.3 = (f32[8,16,8,128]{3,2,1,0:T(8,128)}, f32[8,16,8,128]{3,2,1,0:T(8,128)S(1)}, u32[]{:S(2)}, u32[]{:S(2)}) collective-permute-start(f32[8,16,8,128]{3,2,1,0:T(8,128)} %get-tuple-element.16.own_b), channel_id=1, source_target_pairs={{1,0},{2,1},{3,2},{4,3},{5,4},{6,5},{7,6},{8,7},{9,8},{10,9},{11,1... | collective-permute-start | bytes 1572872 | tf_op jit(solution)/shard_map/ppermute | solution.py:488
  13.4 0.0 collective-permute-done.2.high
  13.4 1.7 %collective-permute-done.1.low = f32[8,16,8,128]{3,2,1,0:T(8,128)S(1)} collective-permute-done((f32[8,16,8,128]{3,2,1,0:T(8,128)}, f32[8,16,8,128]{3,2,1,0:T(8,128)S(1)}, u32[]{:S(2)}, u32[]{:S(2)}) %collective-permute-start.1) | collective-permute-done | bytes 524320 | tf_op jit(solution)/shard_map/ppermute | solution.py:488
  15.1 1.0 copy-done
  16.2 1.0 copy-done.1
  17.2 5.3 %inner.1 = (f32[25,16,8,128]{3,2,1,0:T(8,128)S(1)}, f32[25,16,8,128]{3,2,1,0:T(8,128)S(1)}, f32[25,16,8,128]{3,2,1,0:T(8,128)S(1)}, f32[16,16,8,128]{3,2,1,0:T(8,128)S(1)}, f32[4,5,16,8,128]{4,3,2,1,0:T(8,128)S(1)}) custom-call(f32[8,16,8,128]{3,2,1,0:T(8,128)S(1)} %collective-permute-done.1.low, f32[8,16,8,128]{3,2,1,0:T(8,128)S(1)} %copy-done, ...), custom_call_target="tpu_custom_call" | custom-call | flops 100000000 | bytes 10000000 | tf_op jit(solution)/shard_map/inner/pallas_call | solution.py:267
  22.5 0.0 collective-permute-done.low
  22.5 0.0 collective-permute-done.3.high
  22.5 11.9 %outer.1 = (f32[16,8,24,128]{3,2,1,0:T(8,128)S(1)}, f32[25,16,8,128]{3,2,1,0:T(8,128)S(1)}, f32[25,16,8,128]{3,2,1,0:T(8,128)S(1)}, f32[25,16,8,128]{3,2,1,0:T(8,128)S(1)}) custom-call(f32[8,16,8,128]{3,2,1,0:T(8,128)S(1)} %collective-permute-done.low, ...), custom_call_target="tpu_custom_call", output_to_operand_aliasing={{1}: (2, {}), {2}: (3, {}), {3}: (4, {})} | custom-call | tf_op jit(solution)/shard_map/outer/pallas_call | solution.py:287
  34.4 30.3 %all_to_all.10.sent = f32[16,8,24,128]{3,2,1,0:T(8,128)S(1)} all-to-all(f32[16,8,24,128]{3,2,1,0:T(8,128)S(1)} %get-tuple-element.22), channel_id=1, replica_groups=mesh['tm'=16,'space'=32] {'tm'}, dimensions={0} | all-to-all | bytes 3145728 | tf_op jit(solution)/shard_map/all_to_all | solution.py:496
  64.7 0.1 pack.1
  64.7 2.4 %collective-permute-start.4 = (f32[104,8,128]{2,1,0:T(8,128)S(1)}, f32[104,8,128]{2,1,0:T(8,128)S(1)}, u32[]{:S(2)}, u32[]{:S(2)}) collective-permute-start(f32[104,8,128]{2,1,0:T(8,128)S(1)} %get-tuple-element.23), channel_id=1, source_target_pairs={{0,1},{1,2},{2,3},{3,4},{4,5},{5,6},{6,7},{7,8},{8,9},{9,10},{10,1... | collective-permute-start | bytes 1277960 | tf_op jit(solution)/shard_map/ppermute | solution.py:488
  67.2 3.1 %collective-permute-start.5 = (f32[104,8,128]{2,1,0:T(8,128)S(1)}, f32[104,8,128]{2,1,0:T(8,128)S(1)}, u32[]{:S(2)}, u32[]{:S(2)}) collective-permute-start(f32[104,8,128]{2,1,0:T(8,128)S(1)} %get-tuple-element.24), channel_id=1, source_target_pairs={{1,0},{2,1},{3,2},{4,3},{5,4},{6,5},{7,6},{8,7},{9,8},{10,9},{11,1... | collective-permute-start | bytes 1277960 | tf_op jit(solution)/shard_map/ppermute | solution.py:488
  70.3 0.1 strip.1.eta
  70.4 3.8 %collective-permute-done.4.below = f32[104,8,128]{2,1,0:T(8,128)S(1)} collective-permute-done((f32[104,8,128]{2,1,0:T(8,128)S(1)}, f32[104,8,128]{2,1,0:T(8,128)S(1)}, u32[]{:S(2)}, u32[]{:S(2)}) %collective-permute-start.4) | collective-permute-done | bytes 426016 | tf_op jit(solution)/shard_map/ppermute | solution.py:488
  74.2 1.8 %collective-permute-done.5.above = f32[104,8,128]{2,1,0:T(8,128)S(1)} collective-permute-done((f32[104,8,128]{2,1,0:T(8,128)S(1)}, f32[104,8,128]{2,1,0:T(8,128)S(1)}, u32[]{:S(2)}, u32[]{:S(2)}) %collective-permute-start.5) | collective-permute-done | bytes 426016 | tf_op jit(solution)/shard_map/ppermute | solution.py:488
  75.9 2.4 %first.1.done = f32[8,8,8,128]{3,2,1,0:T(8,128)S(1)} custom-call(f32[24,3,8,128]{3,2,1,0:T(8,128)S(1)} %strip.1.eta, f32[16,8,24,128]{3,2,1,0:T(8,128)S(1)} %all_to_all.10.sent, f32[104,8,128]{2,1,0:T(8,128)S(1)} %collective-permute-done.4.below, f32[104,8,128]{2,1,0:T(8,128)S(1)} %collective-permute-done.5.above), custom_call_target="tpu_custom_call" | custom-call | tf_op jit(solution)/shard_map/first/pallas_call | solution.py:469
  78.3 1.3 %collective-permute-start.7 = (f32[8,8,128]{2,1,0:T(8,128)S(1)}, f32[8,8,128]{2,1,0:T(8,128)S(1)}, u32[]{:S(2)}, u32[]{:S(2)}) collective-permute-start(f32[8,8,128]{2,1,0:T(8,128)S(1)} %slice_bitcast_fusion), channel_id=1, source_target_pairs={{32,0},{64,32},{96,64},{128,96},{160,128},{192,160},{224,192},{256... | collective-permute-start | bytes 98312 | tf_op jit(solution)/shard_map/ppermute | solution.py:488
  79.6 4.5 %collective-permute-start.6 = (f32[8,8,128]{2,1,0:T(8,128)S(1)}, f32[8,8,128]{2,1,0:T(8,128)S(1)}, u32[]{:S(2)}, u32[]{:S(2)}) collective-permute-start(f32[8,8,128]{2,1,0:T(8,128)S(1)} %slice_bitcast_fusion), channel_id=1, source_target_pairs={{0,32},{32,64},{64,96},{96,128},{128,160},{160,192},{192,224},{224... | collective-permute-start | bytes 98312 | tf_op jit(solution)/shard_map/ppermute | solution.py:488
  84.2 0.0 collective-permute-done.7
  84.2 1.6 %collective-permute-done.6 = f32[8,8,128]{2,1,0:T(8,128)S(1)} collective-permute-done((f32[8,8,128]{2,1,0:T(8,128)S(1)}, f32[8,8,128]{2,1,0:T(8,128)S(1)}, u32[]{:S(2)}, u32[]{:S(2)}) %collective-permute-start.6) | collective-permute-done | bytes 32800 | tf_op jit(solution)/shard_map/ppermute | solution.py:488
  85.7 2.7 %collective-permute-start.9 = (f32[8,24,128]{2,1,0:T(8,128)S(1)}, f32[8,24,128]{2,1,0:T(8,128)S(1)}, u32[]{:S(2)}, u32[]{:S(2)}) collective-permute-start(f32[8,24,128]{2,1,0:T(8,128)S(1)} %pad_maximum_fusion.own_u), channel_id=1, source_target_pairs={{1,0},{2,1},{3,2},{4,3},{5,4},{6,5},{7,6},{8,7},{9,8},{10,9},{11,1... | collective-permute-start | bytes 294920 | tf_op jit(solution)/shard_map/ppermute | solution.py:488
  88.4 3.5 %collective-permute-start.8 = (f32[8,24,128]{2,1,0:T(8,128)S(1)}, f32[8,24,128]{2,1,0:T(8,128)S(1)}, u32[]{:S(2)}, u32[]{:S(2)}) collective-permute-start(f32[8,24,128]{2,1,0:T(8,128)S(1)} %pad_maximum_fusion.own_u), channel_id=1, source_target_pairs={{0,1},{1,2},{2,3},{3,4},{4,5},{5,6},{6,7},{7,8},{8,9},{9,10},{10,1... | collective-permute-start | bytes 294920 | tf_op jit(solution)/shard_map/ppermute | solution.py:488
  92.0 0.0 collective-permute-done.9.high_u
  92.0 2.4 %collective-permute-done.8.low_u = f32[8,24,128]{2,1,0:T(8,128)S(1)} collective-permute-done((f32[8,24,128]{2,1,0:T(8,128)S(1)}, f32[8,24,128]{2,1,0:T(8,128)S(1)}, u32[]{:S(2)}, u32[]{:S(2)}) %collective-permute-start.8) | collective-permute-done | bytes 98336 | tf_op jit(solution)/shard_map/ppermute | solution.py:488
  94.4 2.8 %second.1 = f32[16,8,8,128]{3,2,1,0:T(8,128)S(1)} custom-call(f32[24,3,8,128]{3,2,1,0:T(8,128)S(1)} %strip.1.eta, f32[16,8,24,128]{3,2,1,0:T(8,128)S(1)} %all_to_all.10.sent, f32[104,8,128]{2,1,0:T(8,128)S(1)} %collective-permute-done.4.below, f32[104,8,128]{2,1,0:T(8,128)S(1)} %collective-permute-done.5.above, ...), custom_call_target="tpu_custom_call" | custom-call | tf_op jit(solution)/shard_map/second/pallas_call | solution.py:469
  97.2 19.4 %all_to_all.11 = f32[16,8,8,128]{3,2,1,0:T(8,128)S(1)} all-to-all(f32[16,8,8,128]{3,2,1,0:T(8,128)S(1)} %second.1), channel_id=1, replica_groups=mesh['tm'=16,'space'=32] {'tm'}, dimensions={0} | all-to-all | bytes 1048576 | tf_op jit(solution)/shard_map/all_to_all | solution.py:507
  116.6 0.8 copy_bitcast_fusion
  (4 shorter events, 0.0 us)
Async XLA Ops:
  2.5 10.9 %collective-permute-start.2 = (f32[8,16,8,128]{3,2,1,0:T(8,128)}, f32[8,16,8,128]{3,2,1,0:T(8,128)S(1)}, u32[]{:S(2)}, u32[]{:S(2)}) collective-permute-start(f32[8,16,8,128]{3,2,1,0:T(8,128)} %get-tuple-element.15.own_a), channel_id=1, source_target_pairs={{1,0},{2,1},{3,2},{4,3},{5,4},{6,5},{7,6},{8,7},{9,8},{10,9},{11,1... | collective-permute-start | bytes 1572872 | tf_op jit(solution)/shard_map/ppermute | solution.py:488
  4.4 10.7 %collective-permute-start.1 = (f32[8,16,8,128]{3,2,1,0:T(8,128)}, f32[8,16,8,128]{3,2,1,0:T(8,128)S(1)}, u32[]{:S(2)}, u32[]{:S(2)}) collective-permute-start(f32[8,16,8,128]{3,2,1,0:T(8,128)} %get-tuple-element.16.own_b), channel_id=1, source_target_pairs={{0,1},{1,2},{2,3},{3,4},{4,5},{5,6},{6,7},{7,8},{8,9},{9,10},{10,1... | collective-permute-start | bytes 1572872 | tf_op jit(solution)/shard_map/ppermute | solution.py:488
  6.8 15.7 %collective-permute-start = (f32[8,16,8,128]{3,2,1,0:T(8,128)}, f32[8,16,8,128]{3,2,1,0:T(8,128)S(1)}, u32[]{:S(2)}, u32[]{:S(2)}) collective-permute-start(f32[8,16,8,128]{3,2,1,0:T(8,128)} %get-tuple-element.15.own_a), channel_id=1, source_target_pairs={{0,1},{1,2},{2,3},{3,4},{4,5},{5,6},{6,7},{7,8},{8,9},{9,10},{10,1... | collective-permute-start | bytes 1572872 | tf_op jit(solution)/shard_map/ppermute | solution.py:488
  11.5 11.1 %collective-permute-start.3 = (f32[8,16,8,128]{3,2,1,0:T(8,128)}, f32[8,16,8,128]{3,2,1,0:T(8,128)S(1)}, u32[]{:S(2)}, u32[]{:S(2)}) collective-permute-start(f32[8,16,8,128]{3,2,1,0:T(8,128)} %get-tuple-element.16.own_b), channel_id=1, source_target_pairs={{1,0},{2,1},{3,2},{4,3},{5,4},{6,5},{7,6},{8,7},{9,8},{10,9},{11,1... | collective-permute-start | bytes 1572872 | tf_op jit(solution)/shard_map/ppermute | solution.py:488
  15.1 1.0 copy-start
  16.1 1.0 copy-start.1
  64.7 9.4 %collective-permute-start.4 = (f32[104,8,128]{2,1,0:T(8,128)S(1)}, f32[104,8,128]{2,1,0:T(8,128)S(1)}, u32[]{:S(2)}, u32[]{:S(2)}) collective-permute-start(f32[104,8,128]{2,1,0:T(8,128)S(1)} %get-tuple-element.23), channel_id=1, source_target_pairs={{0,1},{1,2},{2,3},{3,4},{4,5},{5,6},{6,7},{7,8},{8,9},{9,10},{10,1... | collective-permute-start | bytes 1277960 | tf_op jit(solution)/shard_map/ppermute | solution.py:488
  67.2 8.7 %collective-permute-start.5 = (f32[104,8,128]{2,1,0:T(8,128)S(1)}, f32[104,8,128]{2,1,0:T(8,128)S(1)}, u32[]{:S(2)}, u32[]{:S(2)}) collective-permute-start(f32[104,8,128]{2,1,0:T(8,128)S(1)} %get-tuple-element.24), channel_id=1, source_target_pairs={{1,0},{2,1},{3,2},{4,3},{5,4},{6,5},{7,6},{8,7},{9,8},{10,9},{11,1... | collective-permute-start | bytes 1277960 | tf_op jit(solution)/shard_map/ppermute | solution.py:488
  78.3 5.9 %collective-permute-start.7 = (f32[8,8,128]{2,1,0:T(8,128)S(1)}, f32[8,8,128]{2,1,0:T(8,128)S(1)}, u32[]{:S(2)}, u32[]{:S(2)}) collective-permute-start(f32[8,8,128]{2,1,0:T(8,128)S(1)} %slice_bitcast_fusion), channel_id=1, source_target_pairs={{32,0},{64,32},{96,64},{128,96},{160,128},{192,160},{224,192},{256... | collective-permute-start | bytes 98312 | tf_op jit(solution)/shard_map/ppermute | solution.py:488
  79.6 6.1 %collective-permute-start.6 = (f32[8,8,128]{2,1,0:T(8,128)S(1)}, f32[8,8,128]{2,1,0:T(8,128)S(1)}, u32[]{:S(2)}, u32[]{:S(2)}) collective-permute-start(f32[8,8,128]{2,1,0:T(8,128)S(1)} %slice_bitcast_fusion), channel_id=1, source_target_pairs={{0,32},{32,64},{64,96},{96,128},{128,160},{160,192},{192,224},{224... | collective-permute-start | bytes 98312 | tf_op jit(solution)/shard_map/ppermute | solution.py:488
  85.7 6.2 %collective-permute-start.9 = (f32[8,24,128]{2,1,0:T(8,128)S(1)}, f32[8,24,128]{2,1,0:T(8,128)S(1)}, u32[]{:S(2)}, u32[]{:S(2)}) collective-permute-start(f32[8,24,128]{2,1,0:T(8,128)S(1)} %pad_maximum_fusion.own_u), channel_id=1, source_target_pairs={{1,0},{2,1},{3,2},{4,3},{5,4},{6,5},{7,6},{8,7},{9,8},{10,9},{11,1... | collective-permute-start | bytes 294920 | tf_op jit(solution)/shard_map/ppermute | solution.py:488
  88.4 5.9 %collective-permute-start.8 = (f32[8,24,128]{2,1,0:T(8,128)S(1)}, f32[8,24,128]{2,1,0:T(8,128)S(1)}, u32[]{:S(2)}, u32[]{:S(2)}) collective-permute-start(f32[8,24,128]{2,1,0:T(8,128)S(1)} %pad_maximum_fusion.own_u), channel_id=1, source_target_pairs={{0,1},{1,2},{2,3},{3,4},{4,5},{5,6},{6,7},{7,8},{8,9},{9,10},{10,1... | collective-permute-start | bytes 294920 | tf_op jit(solution)/shard_map/ppermute | solution.py:488

commit v4 on v3

--- a/solution.py
+++ b/solution.py
@@ -8,6 +8,8 @@
 STEPS = 8
 fine_step = 0.008
 
+SIDE = 4
+ORDER = [a * SIDE + (b if a % 2 == 0 else SIDE - 1 - b) for a in range(SIDE) for b in range(SIDE)]
 BX = 8
 HALF = BX // 2
 NY = 128
@@ -19,6 +21,7 @@
 SMEM = pl.BlockSpec(memory_space=pltpu.SMEM)
 FIRST = 7
 VMEM = pl.BlockSpec(memory_space=pltpu.VMEM)
+HBM = pltpu.MemorySpace.HBM
 
 
 def halo_depth(i):
@@ -62,16 +65,24 @@
     return upper - lower
 
 
+def strip_of(tm):
+    across, along = lax.div(tm, SIDE), lax.rem(tm, SIDE)
+    return across * SIDE + jnp.where(lax.rem(across, 2) == 0, along, SIDE - 1 - along)
+
+
 def iotas():
     shape = (8, NZ)
     return lax.broadcasted_iota(jnp.int32, shape, 1), lax.broadcasted_iota(jnp.int32, shape, 0)
 
 
-def has_neighbours(axis):
-    index = lax.axis_index(axis)
+def has_neighbours(index, count):
     below = jnp.where(index == 0, 0.0, 1.0).astype(jnp.float32)
-    above = jnp.where(index == lax.axis_size(axis) - 1, 0.0, 1.0).astype(jnp.float32)
+    above = jnp.where(index == count - 1, 0.0, 1.0).astype(jnp.float32)
     return below, above
+
+
+def one_trip():
+    return jnp.where(lax.axis_index("space") < 0, 2, 1)
 
 
 def own_kernel(start, regions, resistivity, *refs):
@@ -108,7 +119,7 @@
 
 
 def own_part(start, regions, resistivity):
-    hbm = pl.BlockSpec(memory_space=pltpu.MemorySpace.HBM)
+    hbm = pl.BlockSpec(memory_space=HBM)
     shape = jax.ShapeDtypeStruct((2 * HALF, PARTS, 8, NZ), jnp.float32)
     return pl.pallas_call(
         own_kernel,
@@ -121,15 +132,15 @@
             pltpu.SMEM((REGIONS,), jnp.float32),
             pltpu.SemaphoreType.DMA((5,)),
         ],
-        compiler_params=pltpu.CompilerParams(vmem_limit_bytes=60 << 20),
+        compiler_params=pltpu.CompilerParams(vmem_limit_bytes=8 << 20),
         name="own",
-    )(start, regions, resistivity)
+    )(*(pltpu.with_memory_space_constraint(a, HBM) for a in (start, regions, resistivity)))
 
 
 class Fine:
     def __init__(self, u_ref, k_ref, e_ref, f_ref):
         self.u, self.k, self.e, self.f = u_ref, k_ref, e_ref, f_ref
-        self.below, self.above = has_neighbours("space")
+        self.below, self.above = has_neighbours(lax.axis_index("space"), lax.axis_size("space"))
         self.lane, self.sub = iotas()
 
     def stage(self, ref, base):
@@ -223,11 +234,18 @@
     fine.stage(low, 0)
     fine.stage(high, 5 * HALF)
 
+    once = one_trip()
+
     def wedges(t, _):
         fine.begin(t, u_ref.at[t - 1], k_ref.at[t - 1])
-        fine.pairs(t, 1, fine.keep)
-        fine.plane(t + 2, fine.keep)
-        fine.plane(t + 3, fine.keep, save.at[0, t], save.at[1, t])
+        fine.pairs(t, once, fine.keep)
+
+        def last_pair(_, carry):
+            fine.plane(t + 2, fine.keep)
+            fine.plane(t + 3, fine.keep, save.at[0, t], save.at[1, t])
+            return carry
+
+        lax.fori_loop(0, once, last_pair, 0)
         fine.begin(5 * HALF - t, save.at[2, t], save.at[3, t])
         fine.pairs(5 * HALF - t, 2, fine.keep)
         return 0
@@ -248,7 +266,7 @@
     def spread(x, _):
         for j in range(SLICES):
             for c in range(3):
-                strip = j + c - 1
+                strip = ORDER[j] + c - 1
                 if 0 <= strip < SLICES:
                     tile = s_ref[x, strip * ROWS : (strip + 1) * ROWS, :]
                 else:
@@ -326,10 +344,10 @@
 
 
 def strip_kernel(*refs):
-    tm = lax.axis_index("tm")
+    own = strip_of(lax.axis_index("tm"))
     parts, out = refs[:-1], refs[-1]
     for c in range(3):
-        strip = tm + (c - 1)
+        strip = own + (c - 1)
         scale = jnp.where((strip >= 0) & (strip < SLICES), float(STEPS), 0.0).astype(jnp.float32)
         strip = jnp.clip(strip, 0, SLICES - 1)
         start = lax.rem(strip, 2) * 64 + lax.div(strip, 2)
@@ -362,9 +380,9 @@
 
 def coarse_steps(count, base, eta, refs, u_ref, k_ref, f_ref, out):
     lane, row = iotas()
-    x_below, x_above = has_neighbours("space")
-    y_below, y_above = has_neighbours("tm")
-    once = jnp.where(lax.axis_index("space") < 0, 2, 1)
+    x_below, x_above = has_neighbours(lax.axis_index("space"), lax.axis_size("space"))
+    y_below, y_above = has_neighbours(strip_of(lax.axis_index("tm")), SLICES)
+    once = one_trip()
 
     def mask(x, c):
         factors = []
@@ -481,10 +499,35 @@
     )(*operands)
 
 
+def place_kernel(strips, out, sems):
+    copies = [
+        pltpu.make_async_copy(
+            strips.at[j], out.at[:, pl.ds(ORDER[j] * ROWS, ROWS), :], sems.at[j]
+        )
+        for j in range(SLICES)
+    ]
+    for copy in copies:
+        copy.start()
+    for copy in copies:
+        copy.wait()
+
+
+def place(strips):
+    return pl.pallas_call(
+        place_kernel,
+        out_shape=jax.ShapeDtypeStruct((BX, NY, NZ), jnp.float32),
+        in_specs=[VMEM],
+        out_specs=pl.BlockSpec(memory_space=HBM),
+        scratch_shapes=[pltpu.SemaphoreType.DMA((SLICES,))],
+        compiler_params=pltpu.CompilerParams(vmem_limit_bytes=4 << 20),
+        name="place",
+    )(strips)
+
+
 def both_ways(down, up, axis):
-    count = lax.axis_size(axis)
-    forward = [(i, i + 1) for i in range(count - 1)]
-    backward = [(i + 1, i) for i in range(count - 1)]
+    line = ORDER if axis == "tm" else range(lax.axis_size(axis))
+    forward = list(zip(line[:-1], line[1:]))
+    backward = [(b, a) for a, b in forward]
     return lax.ppermute(up, axis, forward), lax.ppermute(down, axis, backward)
 
 
@@ -505,8 +548,7 @@
         second_kernel, "second", SLICES, eta, sent, below, above, x_low, strip, x_high, done
     )
     result = lax.all_to_all(ends, "tm", 0, 0)
-    result = jnp.transpose(result, (1, 0, 2, 3)).reshape(BX, NY, NZ)
-    return result[None]
+    return place(result)[None]
 
 
 def solution(mesh):

time: 118 us -> 111 us (0.941)
  the two profiles are of different devices: /device:TPU:96 before, /device:TPU:128 now
where the time goes in v4:
time: 111 us
  blocking collectives  43.8 us (39%)
  starting transfers between devices  29.5 us (27%)
  Pallas kernels  22 us (20%)
  waiting for transfers between devices  15.1 us (14%)
    ppermute x10, starting transfers between devices, both_ways(): return (lax.ppermute(up, axis, forward), lax.ppermute(down, axis, backward))  29.5 us
    all_to_all x1, blocking collectives, per_device(): sent = lax.all_to_all(sent, 'tm', 0, 0)  29.4 us
    ppermute x10, waiting for transfers between devices, both_ways(): return (lax.ppermute(up, axis, forward), lax.ppermute(down, axis, backward))  15.1 us
    all_to_all x1, blocking collectives, per_device(): result = lax.all_to_all(ends, 'tm', 0, 0)  14.4 us
    pallas_call x1, Pallas kernels, outer(): pl.pallas_call(outer_kernel, out_shape=(jax.ShapeDtypeStruct((SLICES, BX,...  8.97 us
    pallas_call x1, Pallas kernels, inner(): pl.pallas_call(inner_kernel, out_shape=(GRID, GRID, GRID, jax.ShapeDtypeS...  5.31 us
    pallas_call x2, Pallas kernels, coarse_call(): pl.pallas_call(kernel, out_shape=jax.ShapeDtypeStruct((count, BX, ROWS, N...  5.15 us
  transfers between devices with their start and end apart: 10, of which 8 were waited for; matrix products, arithmetic and copies ran while one was open for 0% of the time, Pallas kernels for 5%

profile of v4, /device:TPU:128, one launch (start us, length us, event | category | flops | bytes accessed | tf_op | source)
XLA Modules:
  0.0 110.6 jit_solution(14178000454400378897)
XLA Ops:
  0.0 1.5 %own.1 = (f32[8,16,8,128]{3,2,1,0:T(8,128)S(1)}, f32[8,16,8,128]{3,2,1,0:T(8,128)S(1)}) custom-call(f32[8,128,128]{2,1,0:T(8,128)} %bitcast.16, s32[8,128,128]{2,1,0:T(8,128)} %regions.1, f32[4]{0:T(128)} %resistivity.1), custom_call_target="tpu_custom_call" | custom-call | tf_op jit(solution)/shard_map/own/pallas_call | solution.py:124
  1.5 1.9 %collective-permute-start.2 = (f32[8,16,8,128]{3,2,1,0:T(8,128)S(1)}, f32[8,16,8,128]{3,2,1,0:T(8,128)S(1)}, u32[]{:S(2)}, u32[]{:S(2)}) collective-permute-start(f32[8,16,8,128]{3,2,1,0:T(8,128)S(1)} %get-tuple-element.15.own_a), channel_id=1, source_target_pairs={{1,0},{2,1},{3,2},{4,3},{5,4},{6,5},{7,6},{8,7},{9,8},{10,9},{11,1... | collective-permute-start | bytes 1572872 | tf_op jit(solution)/shard_map/ppermute | solution.py:531
  3.4 2.4 %collective-permute-start.1 = (f32[8,16,8,128]{3,2,1,0:T(8,128)S(1)}, f32[8,16,8,128]{3,2,1,0:T(8,128)S(1)}, u32[]{:S(2)}, u32[]{:S(2)}) collective-permute-start(f32[8,16,8,128]{3,2,1,0:T(8,128)S(1)} %get-tuple-element.16.own_b), channel_id=1, source_target_pairs={{0,1},{1,2},{2,3},{3,4},{4,5},{5,6},{6,7},{7,8},{8,9},{9,10},{10,1... | collective-permute-start | bytes 1572872 | tf_op jit(solution)/shard_map/ppermute | solution.py:531
  5.8 3.4 %collective-permute-start = (f32[8,16,8,128]{3,2,1,0:T(8,128)S(1)}, f32[8,16,8,128]{3,2,1,0:T(8,128)S(1)}, u32[]{:S(2)}, u32[]{:S(2)}) collective-permute-start(f32[8,16,8,128]{3,2,1,0:T(8,128)S(1)} %get-tuple-element.15.own_a), channel_id=1, source_target_pairs={{0,1},{1,2},{2,3},{3,4},{4,5},{5,6},{6,7},{7,8},{8,9},{9,10},{10,1... | collective-permute-start | bytes 1572872 | tf_op jit(solution)/shard_map/ppermute | solution.py:531
  9.3 3.3 %collective-permute-start.3 = (f32[8,16,8,128]{3,2,1,0:T(8,128)S(1)}, f32[8,16,8,128]{3,2,1,0:T(8,128)S(1)}, u32[]{:S(2)}, u32[]{:S(2)}) collective-permute-start(f32[8,16,8,128]{3,2,1,0:T(8,128)S(1)} %get-tuple-element.16.own_b), channel_id=1, source_target_pairs={{1,0},{2,1},{3,2},{4,3},{5,4},{6,5},{7,6},{8,7},{9,8},{10,9},{11,1... | collective-permute-start | bytes 1572872 | tf_op jit(solution)/shard_map/ppermute | solution.py:531
  12.6 0.0 collective-permute-done.2.high
  12.6 2.5 %collective-permute-done.1.low = f32[8,16,8,128]{3,2,1,0:T(8,128)S(1)} collective-permute-done((f32[8,16,8,128]{3,2,1,0:T(8,128)S(1)}, f32[8,16,8,128]{3,2,1,0:T(8,128)S(1)}, u32[]{:S(2)}, u32[]{:S(2)}) %collective-permute-start.1) | collective-permute-done | bytes 524320 | tf_op jit(solution)/shard_map/ppermute | solution.py:531
  15.1 5.3 %inner.1 = (f32[25,16,8,128]{3,2,1,0:T(8,128)S(1)}, f32[25,16,8,128]{3,2,1,0:T(8,128)S(1)}, f32[25,16,8,128]{3,2,1,0:T(8,128)S(1)}, f32[16,16,8,128]{3,2,1,0:T(8,128)S(1)}, f32[4,5,16,8,128]{4,3,2,1,0:T(8,128)S(1)}) custom-call(f32[8,16,8,128]{3,2,1,0:T(8,128)S(1)} %collective-permute-done.1.low, f32[8,16,8,128]{3,2,1,0:T(8,128)S(1)} %get-tuple-element.15.own_a, ...), custom_call_target="tpu_custom_call" | custom-call | flops 100000000 | bytes 10000000 | tf_op jit(solution)/shard_map/inner/pallas_call | solution.py:285
  20.5 0.3 collective-permute-done.low
  20.8 0.0 collective-permute-done.3.high
  20.8 9.0 %outer.1 = (f32[16,8,24,128]{3,2,1,0:T(8,128)S(1)}, f32[25,16,8,128]{3,2,1,0:T(8,128)S(1)}, f32[25,16,8,128]{3,2,1,0:T(8,128)S(1)}, f32[25,16,8,128]{3,2,1,0:T(8,128)S(1)}) custom-call(f32[8,16,8,128]{3,2,1,0:T(8,128)S(1)} %collective-permute-done.low, ...), custom_call_target="tpu_custom_call", output_to_operand_aliasing={{1}: (2, {}), {2}: (3, {}), {3}: (4, {})} | custom-call | tf_op jit(solution)/shard_map/outer/pallas_call | solution.py:305
  29.7 29.4 %all_to_all.10.sent = f32[16,8,24,128]{3,2,1,0:T(8,128)S(1)} all-to-all(f32[16,8,24,128]{3,2,1,0:T(8,128)S(1)} %get-tuple-element.22), channel_id=1, replica_groups=mesh['tm'=16,'space'=32] {'tm'}, dimensions={0} | all-to-all | bytes 3145728 | tf_op jit(solution)/shard_map/all_to_all | solution.py:539
  59.1 0.1 pack.1
  59.2 1.9 %collective-permute-start.4 = (f32[104,8,128]{2,1,0:T(8,128)S(1)}, f32[104,8,128]{2,1,0:T(8,128)S(1)}, u32[]{:S(2)}, u32[]{:S(2)}) collective-permute-start(f32[104,8,128]{2,1,0:T(8,128)S(1)} %get-tuple-element.23), channel_id=1, source_target_pairs={{0,1},{1,2},{2,3},{3,4},{4,5},{5,6},{6,7},{7,8},{8,9},{9,10},{10,1... | collective-permute-start | bytes 1277960 | tf_op jit(solution)/shard_map/ppermute | solution.py:531
  61.1 4.9 %collective-permute-start.5 = (f32[104,8,128]{2,1,0:T(8,128)S(1)}, f32[104,8,128]{2,1,0:T(8,128)S(1)}, u32[]{:S(2)}, u32[]{:S(2)}) collective-permute-start(f32[104,8,128]{2,1,0:T(8,128)S(1)} %get-tuple-element.24), channel_id=1, source_target_pairs={{1,0},{2,1},{3,2},{4,3},{5,4},{6,5},{7,6},{8,7},{9,8},{10,9},{11,1... | collective-permute-start | bytes 1277960 | tf_op jit(solution)/shard_map/ppermute | solution.py:531
  66.0 0.1 strip.1.eta
  66.1 3.8 %collective-permute-done.4.below = f32[104,8,128]{2,1,0:T(8,128)S(1)} collective-permute-done((f32[104,8,128]{2,1,0:T(8,128)S(1)}, f32[104,8,128]{2,1,0:T(8,128)S(1)}, u32[]{:S(2)}, u32[]{:S(2)}) %collective-permute-start.4) | collective-permute-done | bytes 426016 | tf_op jit(solution)/shard_map/ppermute | solution.py:531
  69.8 1.8 %collective-permute-done.5.above = f32[104,8,128]{2,1,0:T(8,128)S(1)} collective-permute-done((f32[104,8,128]{2,1,0:T(8,128)S(1)}, f32[104,8,128]{2,1,0:T(8,128)S(1)}, u32[]{:S(2)}, u32[]{:S(2)}) %collective-permute-start.5) | collective-permute-done | bytes 426016 | tf_op jit(solution)/shard_map/ppermute | solution.py:531
  71.6 2.4 %first.1.done = f32[8,8,8,128]{3,2,1,0:T(8,128)S(1)} custom-call(f32[24,3,8,128]{3,2,1,0:T(8,128)S(1)} %strip.1.eta, f32[16,8,24,128]{3,2,1,0:T(8,128)S(1)} %all_to_all.10.sent, f32[104,8,128]{2,1,0:T(8,128)S(1)} %collective-permute-done.4.below, f32[104,8,128]{2,1,0:T(8,128)S(1)} %collective-permute-done.5.above), custom_call_target="tpu_custom_call" | custom-call | tf_op jit(solution)/shard_map/first/pallas_call | solution.py:487
  74.0 1.3 %collective-permute-start.7 = (f32[8,8,128]{2,1,0:T(8,128)S(1)}, f32[8,8,128]{2,1,0:T(8,128)S(1)}, u32[]{:S(2)}, u32[]{:S(2)}) collective-permute-start(f32[8,8,128]{2,1,0:T(8,128)S(1)} %slice_bitcast_fusion), channel_id=1, source_target_pairs={{32,0},{64,32},{96,64},{224,96},{192,224},{160,192},{128,160},{256... | collective-permute-start | bytes 98312 | tf_op jit(solution)/shard_map/ppermute | solution.py:531
  75.3 4.5 %collective-permute-start.6 = (f32[8,8,128]{2,1,0:T(8,128)S(1)}, f32[8,8,128]{2,1,0:T(8,128)S(1)}, u32[]{:S(2)}, u32[]{:S(2)}) collective-permute-start(f32[8,8,128]{2,1,0:T(8,128)S(1)} %slice_bitcast_fusion), channel_id=1, source_target_pairs={{0,32},{32,64},{64,96},{96,224},{224,192},{192,160},{160,128},{128... | collective-permute-start | bytes 98312 | tf_op jit(solution)/shard_map/ppermute | solution.py:531
  79.8 0.2 collective-permute-done.7
  80.0 1.4 %collective-permute-done.6 = f32[8,8,128]{2,1,0:T(8,128)S(1)} collective-permute-done((f32[8,8,128]{2,1,0:T(8,128)S(1)}, f32[8,8,128]{2,1,0:T(8,128)S(1)}, u32[]{:S(2)}, u32[]{:S(2)}) %collective-permute-start.6) | collective-permute-done | bytes 32800 | tf_op jit(solution)/shard_map/ppermute | solution.py:531
  81.4 3.9 %collective-permute-start.9 = (f32[8,24,128]{2,1,0:T(8,128)S(1)}, f32[8,24,128]{2,1,0:T(8,128)S(1)}, u32[]{:S(2)}, u32[]{:S(2)}) collective-permute-start(f32[8,24,128]{2,1,0:T(8,128)S(1)} %pad_maximum_fusion.own_u), channel_id=1, source_target_pairs={{1,0},{2,1},{3,2},{4,3},{5,4},{6,5},{7,6},{8,7},{9,8},{10,9},{11,1... | collective-permute-start | bytes 294920 | tf_op jit(solution)/shard_map/ppermute | solution.py:531
  85.3 1.9 %collective-permute-start.8 = (f32[8,24,128]{2,1,0:T(8,128)S(1)}, f32[8,24,128]{2,1,0:T(8,128)S(1)}, u32[]{:S(2)}, u32[]{:S(2)}) collective-permute-start(f32[8,24,128]{2,1,0:T(8,128)S(1)} %pad_maximum_fusion.own_u), channel_id=1, source_target_pairs={{0,1},{1,2},{2,3},{3,4},{4,5},{5,6},{6,7},{7,8},{8,9},{9,10},{10,1... | collective-permute-start | bytes 294920 | tf_op jit(solution)/shard_map/ppermute | solution.py:531
  87.2 0.3 collective-permute-done.9.high_u
  87.5 5.0 %collective-permute-done.8.low_u = f32[8,24,128]{2,1,0:T(8,128)S(1)} collective-permute-done((f32[8,24,128]{2,1,0:T(8,128)S(1)}, f32[8,24,128]{2,1,0:T(8,128)S(1)}, u32[]{:S(2)}, u32[]{:S(2)}) %collective-permute-start.8) | collective-permute-done | bytes 98336 | tf_op jit(solution)/shard_map/ppermute | solution.py:531
  92.5 2.8 %second.1 = f32[16,8,8,128]{3,2,1,0:T(8,128)S(1)} custom-call(f32[24,3,8,128]{3,2,1,0:T(8,128)S(1)} %strip.1.eta, f32[16,8,24,128]{3,2,1,0:T(8,128)S(1)} %all_to_all.10.sent, f32[104,8,128]{2,1,0:T(8,128)S(1)} %collective-permute-done.4.below, f32[104,8,128]{2,1,0:T(8,128)S(1)} %collective-permute-done.5.above, ...), custom_call_target="tpu_custom_call" | custom-call | tf_op jit(solution)/shard_map/second/pallas_call | solution.py:487
  95.3 14.4 %all_to_all.11.strips = f32[16,8,8,128]{3,2,1,0:T(8,128)S(1)} all-to-all(f32[16,8,8,128]{3,2,1,0:T(8,128)S(1)} %second.1), channel_id=1, replica_groups=mesh['tm'=16,'space'=32] {'tm'}, dimensions={0} | all-to-all | bytes 1048576 | tf_op jit(solution)/shard_map/all_to_all | solution.py:550
  109.7 0.9 place.1
  (2 shorter events, 0.0 us)
Async XLA Ops:
  1.5 11.1 %collective-permute-start.2 = (f32[8,16,8,128]{3,2,1,0:T(8,128)S(1)}, f32[8,16,8,128]{3,2,1,0:T(8,128)S(1)}, u32[]{:S(2)}, u32[]{:S(2)}) collective-permute-start(f32[8,16,8,128]{3,2,1,0:T(8,128)S(1)} %get-tuple-element.15.own_a), channel_id=1, source_target_pairs={{1,0},{2,1},{3,2},{4,3},{5,4},{6,5},{7,6},{8,7},{9,8},{10,9},{11,1... | collective-permute-start | bytes 1572872 | tf_op jit(solution)/shard_map/ppermute | solution.py:531
  3.4 11.7 %collective-permute-start.1 = (f32[8,16,8,128]{3,2,1,0:T(8,128)S(1)}, f32[8,16,8,128]{3,2,1,0:T(8,128)S(1)}, u32[]{:S(2)}, u32[]{:S(2)}) collective-permute-start(f32[8,16,8,128]{3,2,1,0:T(8,128)S(1)} %get-tuple-element.16.own_b), channel_id=1, source_target_pairs={{0,1},{1,2},{2,3},{3,4},{4,5},{5,6},{6,7},{7,8},{8,9},{9,10},{10,1... | collective-permute-start | bytes 1572872 | tf_op jit(solution)/shard_map/ppermute | solution.py:531
  5.8 14.9 %collective-permute-start = (f32[8,16,8,128]{3,2,1,0:T(8,128)S(1)}, f32[8,16,8,128]{3,2,1,0:T(8,128)S(1)}, u32[]{:S(2)}, u32[]{:S(2)}) collective-permute-start(f32[8,16,8,128]{3,2,1,0:T(8,128)S(1)} %get-tuple-element.15.own_a), channel_id=1, source_target_pairs={{0,1},{1,2},{2,3},{3,4},{4,5},{5,6},{6,7},{7,8},{8,9},{9,10},{10,1... | collective-permute-start | bytes 1572872 | tf_op jit(solution)/shard_map/ppermute | solution.py:531
  9.3 11.5 %collective-permute-start.3 = (f32[8,16,8,128]{3,2,1,0:T(8,128)S(1)}, f32[8,16,8,128]{3,2,1,0:T(8,128)S(1)}, u32[]{:S(2)}, u32[]{:S(2)}) collective-permute-start(f32[8,16,8,128]{3,2,1,0:T(8,128)S(1)} %get-tuple-element.16.own_b), channel_id=1, source_target_pairs={{1,0},{2,1},{3,2},{4,3},{5,4},{6,5},{7,6},{8,7},{9,8},{10,9},{11,1... | collective-permute-start | bytes 1572872 | tf_op jit(solution)/shard_map/ppermute | solution.py:531
  59.2 10.7 %collective-permute-start.4 = (f32[104,8,128]{2,1,0:T(8,128)S(1)}, f32[104,8,128]{2,1,0:T(8,128)S(1)}, u32[]{:S(2)}, u32[]{:S(2)}) collective-permute-start(f32[104,8,128]{2,1,0:T(8,128)S(1)} %get-tuple-element.23), channel_id=1, source_target_pairs={{0,1},{1,2},{2,3},{3,4},{4,5},{5,6},{6,7},{7,8},{8,9},{9,10},{10,1... | collective-permute-start | bytes 1277960 | tf_op jit(solution)/shard_map/ppermute | solution.py:531
  61.1 10.5 %collective-permute-start.5 = (f32[104,8,128]{2,1,0:T(8,128)S(1)}, f32[104,8,128]{2,1,0:T(8,128)S(1)}, u32[]{:S(2)}, u32[]{:S(2)}) collective-permute-start(f32[104,8,128]{2,1,0:T(8,128)S(1)} %get-tuple-element.24), channel_id=1, source_target_pairs={{1,0},{2,1},{3,2},{4,3},{5,4},{6,5},{7,6},{8,7},{9,8},{10,9},{11,1... | collective-permute-start | bytes 1277960 | tf_op jit(solution)/shard_map/ppermute | solution.py:531
  74.0 6.1 %collective-permute-start.7 = (f32[8,8,128]{2,1,0:T(8,128)S(1)}, f32[8,8,128]{2,1,0:T(8,128)S(1)}, u32[]{:S(2)}, u32[]{:S(2)}) collective-permute-start(f32[8,8,128]{2,1,0:T(8,128)S(1)} %slice_bitcast_fusion), channel_id=1, source_target_pairs={{32,0},{64,32},{96,64},{224,96},{192,224},{160,192},{128,160},{256... | collective-permute-start | bytes 98312 | tf_op jit(solution)/shard_map/ppermute | solution.py:531
  75.3 6.1 %collective-permute-start.6 = (f32[8,8,128]{2,1,0:T(8,128)S(1)}, f32[8,8,128]{2,1,0:T(8,128)S(1)}, u32[]{:S(2)}, u32[]{:S(2)}) collective-permute-start(f32[8,8,128]{2,1,0:T(8,128)S(1)} %slice_bitcast_fusion), channel_id=1, source_target_pairs={{0,32},{32,64},{64,96},{96,224},{224,192},{192,160},{160,128},{128... | collective-permute-start | bytes 98312 | tf_op jit(solution)/shard_map/ppermute | solution.py:531
  81.4 6.1 %collective-permute-start.9 = (f32[8,24,128]{2,1,0:T(8,128)S(1)}, f32[8,24,128]{2,1,0:T(8,128)S(1)}, u32[]{:S(2)}, u32[]{:S(2)}) collective-permute-start(f32[8,24,128]{2,1,0:T(8,128)S(1)} %pad_maximum_fusion.own_u), channel_id=1, source_target_pairs={{1,0},{2,1},{3,2},{4,3},{5,4},{6,5},{7,6},{8,7},{9,8},{10,9},{11,1... | collective-permute-start | bytes 294920 | tf_op jit(solution)/shard_map/ppermute | solution.py:531
  85.3 7.1 %collective-permute-start.8 = (f32[8,24,128]{2,1,0:T(8,128)S(1)}, f32[8,24,128]{2,1,0:T(8,128)S(1)}, u32[]{:S(2)}, u32[]{:S(2)}) collective-permute-start(f32[8,24,128]{2,1,0:T(8,128)S(1)} %pad_maximum_fusion.own_u), channel_id=1, source_target_pairs={{0,1},{1,2},{2,3},{3,4},{4,5},{5,6},{6,7},{7,8},{8,9},{9,10},{10,1... | collective-permute-start | bytes 294920 | tf_op jit(solution)/shard_map/ppermute | solution.py:531

commit v5 on v4

--- a/solution.py
+++ b/solution.py
@@ -63,6 +63,43 @@
     upper = jnp.where(lane == NZ - 1, -edge, (k0 + kp) * (up - u0))
     lower = jnp.where(lane == 0, edge, pltpu.roll(upper, 1, 1))
     return upper - lower
+
+
+Q = 4
+CHUNK = NZ // Q
+
+
+def by_chunk(lane, values):
+    low = jnp.where(lane < CHUNK, values[0], values[1])
+    return jnp.where(lane < 2 * CHUNK, low, jnp.where(lane < 3 * CHUNK, values[2], values[3]))
+
+
+def interleave(rows):
+    lane, _ = iotas()
+    turned = []
+    for h in range(Q):
+        source = Q * (lane & (CHUNK - 1)) + (((lane >> 5) - h) & (Q - 1))
+        turned.append(jnp.take_along_axis(rows[h], source, axis=1))
+    tiles = []
+    for rz in range(Q):
+        tile = by_chunk(lane, [turned[(c - rz) % Q] for c in range(Q)])
+        tiles.append(pltpu.roll(tile, NZ - CHUNK * rz, 1) if rz else tile)
+    return tiles
+
+
+def separate(tiles):
+    lane, _ = iotas()
+    turned = [pltpu.roll(t, CHUNK * rz, 1) if rz else t for rz, t in enumerate(tiles)]
+    rows = []
+    for h in range(Q):
+        mixed = by_chunk(lane, [turned[(c - h) % Q] for c in range(Q)])
+        source = CHUNK * (((lane & (Q - 1)) + h) & (Q - 1)) + (lane >> 2)
+        rows.append(jnp.take_along_axis(mixed, source, axis=1))
+    return rows
+
+
+def rows_at(h, ry):
+    return pl.ds(CHUNK * h + ry, 8, stride=Q)
 
 
 def strip_of(tm):
@@ -105,17 +142,25 @@
         for copy in copies[h]:
             copy.wait()
 
-        def plane(x, _, h=h):
-            for r in range(PARTS):
-                outs[h][x, r] = start_v[h * HALF + x, pl.ds(r, 8, stride=PARTS), :]
-                region = regions_v[h * HALF + x, pl.ds(r, 8, stride=PARTS), :]
-                value = jnp.zeros((8, NZ), jnp.float32)
-                for i in range(REGIONS):
-                    value = jnp.where(region == i, scaled[i], value)
-                outs[h][HALF + x, r] = value
+        def planes(n, _, h=h):
+            for x in (2 * n, 2 * n + 1):
+                for ry in range(Q):
+                    u, e = [], []
+                    for g in range(Q):
+                        where = rows_at(g, ry)
+                        u.append(start_v[h * HALF + x, where, :])
+                        region = regions_v[h * HALF + x, where, :]
+                        value = jnp.zeros((8, NZ), jnp.float32)
+                        for i in range(REGIONS):
+                            value = jnp.where(region == i, scaled[i], value)
+                        e.append(value)
+                    u, e = interleave(u), interleave(e)
+                    for rz in range(Q):
+                        outs[h][x, Q * ry + rz] = u[rz]
+                        outs[h][HALF + x, Q * ry + rz] = e[rz]
             return 0
 
-        lax.fori_loop(0, HALF, plane, 0)
+        lax.fori_loop(0, HALF // 2, planes, 0)
 
 
 def own_part(start, regions, resistivity):
@@ -141,7 +186,11 @@
     def __init__(self, u_ref, k_ref, e_ref, f_ref):
         self.u, self.k, self.e, self.f = u_ref, k_ref, e_ref, f_ref
         self.below, self.above = has_neighbours(lax.axis_index("space"), lax.axis_size("space"))
-        self.lane, self.sub = iotas()
+        lane, sub = iotas()
+        self.z_high, self.z_low = [(lane & (CHUNK - 1)) == v for v in (CHUNK - 1, 0)]
+        self.y_high, self.y_low = sub == 7, sub == 0
+        self.y_end = (sub == 7) & (lane >= NZ - CHUNK)
+        self.y_start = (sub == 0) & (lane < CHUNK)
 
     def stage(self, ref, base):
         def one(x, _):
@@ -154,51 +203,85 @@
 
         lax.fori_loop(0, HALF, one, 0)
 
+    def above_y(self, v):
+        turned = pltpu.roll(pltpu.roll(v, NZ - CHUNK, 1), 7, 0)
+        v = jnp.where(self.y_high, turned, pltpu.roll(v, 7, 0))
+        return jnp.where(self.y_end, 0.0, v)
+
     def plane(self, x, emit, next_u=None, next_k=None):
-        u_ref, k_ref, f_ref, sub = self.u, self.k, self.f, self.sub
+        f_ref = self.f
         if next_u is None:
-            next_u, next_k = u_ref.at[x + 1], k_ref.at[x + 1]
-        u0, k0 = u_ref[x, 0], k_ref[x, 0]
-        u_end, k_end = u_ref[x, PARTS - 1], k_ref[x, PARTS - 1]
-        wrap_u = jnp.where(sub == 7, 0.0, pltpu.roll(u0, 7, 0))
-        wrap_k = jnp.where(sub == 7, 0.0, pltpu.roll(k0, 7, 0))
-        top = (k_end + wrap_k) * (wrap_u - u_end)
-        y_low = jnp.where(sub == 0, k0 * u0, pltpu.roll(top, 1, 0))
-        for r in range(PARTS):
-            if r < PARTS - 1:
-                u1, k1 = u_ref[x, r + 1], k_ref[x, r + 1]
-                y_up = (k0 + k1) * (u1 - u0)
-            else:
-                u1 = k1 = None
-                y_up = top
-            x_up = (k0 + next_k[r]) * (next_u[r] - u0)
-            x_low = f_ref[r]
-            f_ref[r] = x_up
-            total = (x_up - x_low) + (y_up - y_low) + z_flux(u0, k0, self.lane)
-            emit(x, r, u0, total)
-            u0, k0, y_low = u1, k1, y_up
+            next_u, next_k = self.u.at[x + 1], self.k.at[x + 1]
+
+        def at(ry, rz):
+            return self.u[x, Q * ry + rz], self.k[x, Q * ry + rz]
+
+        z_ends, y_tops, y_lows = [], [], []
+        for ry in range(Q):
+            (u0, k0), (u3, k3) = at(ry, 0), at(ry, Q - 1)
+            un, kn = pltpu.roll(u0, NZ - 1, 1), pltpu.roll(k0, NZ - 1, 1)
+            top = jnp.where(self.z_high, -(k3 * u3), (k3 + kn) * (un - u3))
+            low = jnp.where(self.z_low, k0 * u0, pltpu.roll(top, 1, 1))
+            z_ends.append((low, top))
+        for rz in range(Q):
+            (u0, k0), (u3, k3) = at(0, rz), at(Q - 1, rz)
+            top = (k3 + self.above_y(k0)) * (self.above_y(u0) - u3)
+            turned = pltpu.roll(pltpu.roll(top, CHUNK, 1), 1, 0)
+            low = jnp.where(self.y_low, turned, pltpu.roll(top, 1, 0))
+            y_tops.append(top)
+            y_lows.append(jnp.where(self.y_start, k0 * u0, low))
+        for ry in range(Q):
+            z_low, z_top = z_ends[ry]
+            u0, k0 = at(ry, 0)
+            for rz in range(Q):
+                r = Q * ry + rz
+                if rz < Q - 1:
+                    u1, k1 = at(ry, rz + 1)
+                    z_up = (k0 + k1) * (u1 - u0)
+                else:
+                    u1 = k1 = None
+                    z_up = z_top
+                if ry < Q - 1:
+                    un, kn = at(ry + 1, rz)
+                    y_up = (k0 + kn) * (un - u0)
+                else:
+                    y_up = y_tops[rz]
+                x_up = (k0 + next_k[r]) * (next_u[r] - u0)
+                x_low = f_ref[r]
+                f_ref[r] = x_up
+                total = (x_up - x_low) + (y_up - y_lows[rz]) + (z_up - z_low)
+                emit(x, r, u0, total)
+                y_lows[rz], z_low = y_up, z_up
+                u0, k0 = u1, k1
 
     def begin(self, x, low_u, low_k):
         for r in range(PARTS):
             self.f[r] = (low_k[r] + self.k[x, r]) * (self.u[x, r] - low_u[r])
 
-    def pairs(self, first, count, emit):
-        def pair(n, _):
-            for q in range(2):
-                self.plane(first + 2 * n + q, emit)
+    def stretches(self, first, count, size, emit):
+        def stretch(n, _):
+            for q in range(size):
+                self.plane(first + size * n + q, emit)
             return 0
 
-        lax.fori_loop(0, count, pair, 0)
-
-    def step(self, first, count, emit):
+        lax.fori_loop(0, count, stretch, 0)
+
+    def step(self, first, count, size, emit):
         self.begin(first, self.u.at[first - 1], self.k.at[first - 1])
-        self.pairs(first, count, emit)
+        self.stretches(first, count, size, emit)
 
     def keep(self, x, r, u0, total):
         inside = jnp.where(x < BX, self.below, jnp.where(x < 2 * BX, jnp.float32(1.0), self.above))
         new = inside * (u0 + total)
         self.u[x, r] = new
         self.k[x, r] = coeff(self.e[x, r], new)
+
+
+def to_rows(tiles, rows):
+    for ry in range(Q):
+        parts = separate([tiles[Q * ry + rz] for rz in range(Q)])
+        for h in range(Q):
+            rows[rows_at(h, ry), :] = parts[h]
 
 
 def inner_kernel(low, own_a, own_b, high, u_ref, k_ref, e_ref, g_ref, save, f_ref):
@@ -218,15 +301,9 @@
             save[2, t, r] = u_ref[5 * HALF - 1 - t, r]
             save[3, t, r] = k_ref[5 * HALF - 1 - t, r]
 
-    stow(1)
-    fine.step(HALF + 1, 2 * HALF - 1, keep_first)
-
-    def later_step(t, _):
+    for t in range(1, HALF + 1):
         stow(t)
-        fine.step(HALF + t, 2 * HALF - t, fine.keep)
-        return 0
-
-    lax.fori_loop(2, HALF + 1, later_step, 0)
+        fine.step(HALF + t, 2, BX - t, keep_first if t == 1 else fine.keep)
 
 
 def outer_kernel(low, high, u_in, k_in, e_in, g_ref, save, out, u_ref, k_ref, e_ref, f_ref, s_ref):
@@ -238,30 +315,33 @@
 
     def wedges(t, _):
         fine.begin(t, u_ref.at[t - 1], k_ref.at[t - 1])
-        fine.pairs(t, once, fine.keep)
-
-        def last_pair(_, carry):
-            fine.plane(t + 2, fine.keep)
-            fine.plane(t + 3, fine.keep, save.at[0, t], save.at[1, t])
+
+        def low_side(_, carry):
+            for q in range(HALF - 1):
+                fine.plane(t + q, fine.keep)
+            fine.plane(t + HALF - 1, fine.keep, save.at[0, t], save.at[1, t])
             return carry
 
-        lax.fori_loop(0, once, last_pair, 0)
+        lax.fori_loop(0, once, low_side, 0)
         fine.begin(5 * HALF - t, save.at[2, t], save.at[3, t])
-        fine.pairs(5 * HALF - t, 2, fine.keep)
+        fine.stretches(5 * HALF - t, once, HALF, fine.keep)
         return 0
 
     lax.fori_loop(1, HALF + 1, wedges, 0)
-
-    def later_step(t, _):
-        fine.step(t, 3 * HALF - t, fine.keep)
+    for t in range(HALF + 1, STEPS):
+        fine.step(t, 2, 3 * HALF - t, fine.keep)
+
+    def keep_last(x, r, u0, total):
+        u_ref[x - BX, r] = (u0 + total) - g_ref[x - HALF, r]
+
+    fine.step(BX, 2, HALF, keep_last)
+
+    def natural(n, _):
+        for x in (2 * n, 2 * n + 1):
+            to_rows(u_ref.at[x], s_ref.at[x])
         return 0
 
-    lax.fori_loop(HALF + 1, STEPS, later_step, 0)
-
-    def keep_last(x, r, u0, total):
-        s_ref[x - BX, pl.ds(r, 8, stride=PARTS), :] = (u0 + total) - g_ref[x - HALF, r]
-
-    fine.step(BX, HALF, keep_last)
+    lax.fori_loop(0, BX // 2, natural, 0)
 
     def spread(x, _):
         for j in range(SLICES):
@@ -345,28 +425,34 @@
 
 def strip_kernel(*refs):
     own = strip_of(lax.axis_index("tm"))
-    parts, out = refs[:-1], refs[-1]
+    parts, (out, rows) = refs[:-2], refs[-2:]
+    for n, ref in enumerate(parts):
+
+        def natural(m, _, n=n, ref=ref):
+            for x in (2 * m, 2 * m + 1):
+                to_rows(ref.at[HALF + x], rows.at[n * HALF + x])
+            return 0
+
+        lax.fori_loop(0, HALF // 2, natural, 0)
     for c in range(3):
         strip = own + (c - 1)
         scale = jnp.where((strip >= 0) & (strip < SLICES), float(STEPS), 0.0).astype(jnp.float32)
-        strip = jnp.clip(strip, 0, SLICES - 1)
-        start = lax.rem(strip, 2) * 64 + lax.div(strip, 2)
-        for n, ref in enumerate(parts):
-            for x in range(HALF):
-                out[n * HALF + x, c] = scale * ref[HALF + x, pl.ds(start, 8, stride=8), :]
+        start = pl.multiple_of(jnp.clip(strip, 0, SLICES - 1) * ROWS, ROWS)
+        for x in range(3 * BX):
+            out[x, c] = scale * rows[x, pl.ds(start, ROWS), :]
 
 
 def strip_part(*parts):
-    flat = [a.reshape(2 * HALF, NY, NZ) for a in parts]
     return pl.pallas_call(
         strip_kernel,
         out_shape=jax.ShapeDtypeStruct((3 * BX, 3, 8, NZ), jnp.float32),
         in_specs=[VMEM] * len(parts),
         out_specs=VMEM,
+        scratch_shapes=[pltpu.VMEM((3 * BX, NY, NZ), jnp.float32)],
         compiler_params=pltpu.CompilerParams(vmem_limit_bytes=8 << 20),
         cost_estimate=pl.CostEstimate(flops=10**6, bytes_accessed=10**6, transcendentals=0),
         name="strip",
-    )(*flat)
+    )(*parts)
 
 
 def sent_tile(refs, i, x, c):

time: 111 us -> 110 us (level)
    pallas_call x1, Pallas kernels: 0.1 us -> 2.76 us  [strip_part(): pl.pallas_call(strip_kernel, out_shape=jax.ShapeDtypeStruct((3 * BX, 3, 8...]
    pallas_call x1, Pallas kernels: 8.97 us -> 6.72 us  [outer(): pl.pallas_call(outer_kernel, out_shape=(jax.ShapeDtypeStruct((SLICES, BX,...]
    pallas_call x1, Pallas kernels: 5.31 us -> 3.74 us  [inner(): pl.pallas_call(inner_kernel, out_shape=(GRID, GRID, GRID, jax.ShapeDtypeS...]
    pallas_call x1, Pallas kernels: 1.5 us -> 2.88 us  [own_part(): pl.pallas_call(own_kernel, out_shape=(shape, shape), in_specs=[hbm] * 3,...]
  transfers between devices with their start and end apart: 10 -> 10, of which waited for: 8 -> 8; matrix products, arithmetic and copies ran while one was open for 0% -> 0% of each run, Pallas kernels for 5% -> 6%
where the time goes in v5:
time: 110 us
  blocking collectives  43.8 us (40%)
  starting transfers between devices  29.5 us (27%)
  Pallas kernels  22.2 us (20%)
  waiting for transfers between devices  14 us (13%)
    ppermute x10, starting transfers between devices, both_ways(): return (lax.ppermute(up, axis, forward), lax.ppermute(down, axis, backward))  29.5 us
    all_to_all x1, blocking collectives, per_device(): sent = lax.all_to_all(sent, 'tm', 0, 0)  29.4 us
    all_to_all x1, blocking collectives, per_device(): result = lax.all_to_all(ends, 'tm', 0, 0)  14.4 us
    ppermute x10, waiting for transfers between devices, both_ways(): return (lax.ppermute(up, axis, forward), lax.ppermute(down, axis, backward))  14 us
    pallas_call x1, Pallas kernels, outer(): pl.pallas_call(outer_kernel, out_shape=(jax.ShapeDtypeStruct((SLICES, BX,...  6.72 us
    pallas_call x2, Pallas kernels, coarse_call(): pl.pallas_call(kernel, out_shape=jax.ShapeDtypeStruct((count, BX, ROWS, N...  5.15 us
    pallas_call x1, Pallas kernels, inner(): pl.pallas_call(inner_kernel, out_shape=(GRID, GRID, GRID, jax.ShapeDtypeS...  3.74 us
    pallas_call x1, Pallas kernels, own_part(): pl.pallas_call(own_kernel, out_shape=(shape, shape), in_specs=[hbm] * 3,...  2.88 us
  transfers between devices with their start and end apart: 10, of which 8 were waited for; matrix products, arithmetic and copies ran while one was open for 0% of the time, Pallas kernels for 6%

profile of v5, /device:TPU:128, one launch (start us, length us, event | category | flops | bytes accessed | tf_op | source)
XLA Modules:
  0.0 109.8 jit_solution(15387261613900299967)
XLA Ops:
  0.0 2.9 %own.1 = (f32[8,16,8,128]{3,2,1,0:T(8,128)S(1)}, f32[8,16,8,128]{3,2,1,0:T(8,128)S(1)}) custom-call(f32[8,128,128]{2,1,0:T(8,128)} %bitcast.4, s32[8,128,128]{2,1,0:T(8,128)} %regions.1, f32[4]{0:T(128)} %resistivity.1), custom_call_target="tpu_custom_call" | custom-call | tf_op jit(solution)/shard_map/own/pallas_call | solution.py:169
  2.9 1.9 %collective-permute-start.2 = (f32[8,16,8,128]{3,2,1,0:T(8,128)S(1)}, f32[8,16,8,128]{3,2,1,0:T(8,128)S(1)}, u32[]{:S(2)}, u32[]{:S(2)}) collective-permute-start(f32[8,16,8,128]{3,2,1,0:T(8,128)S(1)} %get-tuple-element.15.refs_2_.own_a), channel_id=1, source_target_pairs={{1,0},{2,1},{3,2},{4,3},{5,4},{6,5},{7,6},{8,7},{9,8},{10,9},{11,1... | collective-permute-start | bytes 1572872 | tf_op jit(solution)/shard_map/ppermute | solution.py:617
  4.8 2.4 %collective-permute-start.1 = (f32[8,16,8,128]{3,2,1,0:T(8,128)S(1)}, f32[8,16,8,128]{3,2,1,0:T(8,128)S(1)}, u32[]{:S(2)}, u32[]{:S(2)}) collective-permute-start(f32[8,16,8,128]{3,2,1,0:T(8,128)S(1)} %get-tuple-element.16.refs_3_.own_b), channel_id=1, source_target_pairs={{0,1},{1,2},{2,3},{3,4},{4,5},{5,6},{6,7},{7,8},{8,9},{9,10},{10,1... | collective-permute-start | bytes 1572872 | tf_op jit(solution)/shard_map/ppermute | solution.py:617
  7.2 3.4 %collective-permute-start = (f32[8,16,8,128]{3,2,1,0:T(8,128)S(1)}, f32[8,16,8,128]{3,2,1,0:T(8,128)S(1)}, u32[]{:S(2)}, u32[]{:S(2)}) collective-permute-start(f32[8,16,8,128]{3,2,1,0:T(8,128)S(1)} %get-tuple-element.15.refs_2_.own_a), channel_id=1, source_target_pairs={{0,1},{1,2},{2,3},{3,4},{4,5},{5,6},{6,7},{7,8},{8,9},{9,10},{10,1... | collective-permute-start | bytes 1572872 | tf_op jit(solution)/shard_map/ppermute | solution.py:617
  10.7 3.3 %collective-permute-start.3 = (f32[8,16,8,128]{3,2,1,0:T(8,128)S(1)}, f32[8,16,8,128]{3,2,1,0:T(8,128)S(1)}, u32[]{:S(2)}, u32[]{:S(2)}) collective-permute-start(f32[8,16,8,128]{3,2,1,0:T(8,128)S(1)} %get-tuple-element.16.refs_3_.own_b), channel_id=1, source_target_pairs={{1,0},{2,1},{3,2},{4,3},{5,4},{6,5},{7,6},{8,7},{9,8},{10,9},{11,1... | collective-permute-start | bytes 1572872 | tf_op jit(solution)/shard_map/ppermute | solution.py:617
  14.0 0.0 collective-permute-done.2.refs_4_.high
  14.0 2.5 %collective-permute-done.1.refs_1_.low = f32[8,16,8,128]{3,2,1,0:T(8,128)S(1)} collective-permute-done((f32[8,16,8,128]{3,2,1,0:T(8,128)S(1)}, f32[8,16,8,128]{3,2,1,0:T(8,128)S(1)}, u32[]{:S(2)}, u32[]{:S(2)}) %collective-permute-start.1) | collective-permute-done | bytes 524320 | tf_op jit(solution)/shard_map/ppermute | solution.py:617
  16.5 3.7 %inner.1 = (f32[25,16,8,128]{3,2,1,0:T(8,128)S(1)}, f32[25,16,8,128]{3,2,1,0:T(8,128)S(1)}, f32[25,16,8,128]{3,2,1,0:T(8,128)S(1)}, f32[16,16,8,128]{3,2,1,0:T(8,128)S(1)}, f32[4,5,16,8,128]{4,3,2,1,0:T(8,128)S(1)}) custom-call(f32[8,16,8,128]{3,2,1,0:T(8,128)S(1)} %collective-permute-done.1.refs_1_.low, ...), custom_call_target="tpu_custom_call" | custom-call | flops 100000000 | bytes 10000000 | tf_op jit(solution)/shard_map/inner/pallas_call | solution.py:365
  20.3 1.9 %collective-permute-done.refs_0_.low = f32[8,16,8,128]{3,2,1,0:T(8,128)S(1)} collective-permute-done((f32[8,16,8,128]{3,2,1,0:T(8,128)S(1)}, f32[8,16,8,128]{3,2,1,0:T(8,128)S(1)}, u32[]{:S(2)}, u32[]{:S(2)}) %collective-permute-start) | collective-permute-done | bytes 524320 | tf_op jit(solution)/shard_map/ppermute | solution.py:617
  22.2 0.0 collective-permute-done.3.refs_5_.high
  22.2 6.7 %outer.1 = (f32[16,8,24,128]{3,2,1,0:T(8,128)S(1)}, f32[25,16,8,128]{3,2,1,0:T(8,128)S(1)}, f32[25,16,8,128]{3,2,1,0:T(8,128)S(1)}, f32[25,16,8,128]{3,2,1,0:T(8,128)S(1)}) custom-call(f32[8,16,8,128]{3,2,1,0:T(8,128)S(1)} %collective-permute-done.refs_0_.low, ...), custom_call_target="tpu_custom_call", output_to_operand_aliasing={{1}: (2, {}), {2}: (3, {}), {3}: (4, {})} | custom-call | tf_op jit(solution)/shard_map/outer/pallas_call | solution.py:385
  28.9 29.4 %all_to_all.10.sent = f32[16,8,24,128]{3,2,1,0:T(8,128)S(1)} all-to-all(f32[16,8,24,128]{3,2,1,0:T(8,128)S(1)} %get-tuple-element.22), channel_id=1, replica_groups=mesh['tm'=16,'space'=32] {'tm'}, dimensions={0} | all-to-all | bytes 3145728 | tf_op jit(solution)/shard_map/all_to_all | solution.py:625
  58.3 0.1 pack.1
  58.3 1.9 %collective-permute-start.4 = (f32[104,8,128]{2,1,0:T(8,128)S(1)}, f32[104,8,128]{2,1,0:T(8,128)S(1)}, u32[]{:S(2)}, u32[]{:S(2)}) collective-permute-start(f32[104,8,128]{2,1,0:T(8,128)S(1)} %get-tuple-element.23), channel_id=1, source_target_pairs={{0,1},{1,2},{2,3},{3,4},{4,5},{5,6},{6,7},{7,8},{8,9},{9,10},{10,1... | collective-permute-start | bytes 1277960 | tf_op jit(solution)/shard_map/ppermute | solution.py:617
  60.3 4.9 %collective-permute-start.5 = (f32[104,8,128]{2,1,0:T(8,128)S(1)}, f32[104,8,128]{2,1,0:T(8,128)S(1)}, u32[]{:S(2)}, u32[]{:S(2)}) collective-permute-start(f32[104,8,128]{2,1,0:T(8,128)S(1)} %get-tuple-element.24), channel_id=1, source_target_pairs={{1,0},{2,1},{3,2},{4,3},{5,4},{6,5},{7,6},{8,7},{9,8},{10,9},{11,1... | collective-permute-start | bytes 1277960 | tf_op jit(solution)/shard_map/ppermute | solution.py:617
  65.1 2.8 %strip.1.eta = f32[24,3,8,128]{3,2,1,0:T(8,128)S(1)} custom-call(f32[8,16,8,128]{3,2,1,0:T(8,128)S(1)} %collective-permute-done.refs_0_.low, f32[8,16,8,128]{3,2,1,0:T(8,128)S(1)} %collective-permute-done.1.refs_1_.low, f32[8,16,8,128]{3,2,1,0:T(8,128)S(1)} %get-tuple-element.15.refs_2_.own_a, f32[8,16,8,128]{3,2,1,0:T(8,128)S(1)} %get-tuple-element.16.refs_3_.own_b, ...), custom_call_target="tpu_custom_call" | custom-call | flops 1000000 | bytes 1000000 | tf_op jit(solution)/shard_map/strip/pallas_call | solution.py:446
  67.9 1.1 %collective-permute-done.4.below = f32[104,8,128]{2,1,0:T(8,128)S(1)} collective-permute-done((f32[104,8,128]{2,1,0:T(8,128)S(1)}, f32[104,8,128]{2,1,0:T(8,128)S(1)}, u32[]{:S(2)}, u32[]{:S(2)}) %collective-permute-start.4) | collective-permute-done | bytes 426016 | tf_op jit(solution)/shard_map/ppermute | solution.py:617
  69.0 1.8 %collective-permute-done.5.above = f32[104,8,128]{2,1,0:T(8,128)S(1)} collective-permute-done((f32[104,8,128]{2,1,0:T(8,128)S(1)}, f32[104,8,128]{2,1,0:T(8,128)S(1)}, u32[]{:S(2)}, u32[]{:S(2)}) %collective-permute-start.5) | collective-permute-done | bytes 426016 | tf_op jit(solution)/shard_map/ppermute | solution.py:617
  70.7 2.4 %first.1.done = f32[8,8,8,128]{3,2,1,0:T(8,128)S(1)} custom-call(f32[24,3,8,128]{3,2,1,0:T(8,128)S(1)} %strip.1.eta, f32[16,8,24,128]{3,2,1,0:T(8,128)S(1)} %all_to_all.10.sent, f32[104,8,128]{2,1,0:T(8,128)S(1)} %collective-permute-done.4.below, f32[104,8,128]{2,1,0:T(8,128)S(1)} %collective-permute-done.5.above), custom_call_target="tpu_custom_call" | custom-call | tf_op jit(solution)/shard_map/first/pallas_call | solution.py:573
  73.1 1.3 %collective-permute-start.7 = (f32[8,8,128]{2,1,0:T(8,128)S(1)}, f32[8,8,128]{2,1,0:T(8,128)S(1)}, u32[]{:S(2)}, u32[]{:S(2)}) collective-permute-start(f32[8,8,128]{2,1,0:T(8,128)S(1)} %slice_bitcast_fusion), channel_id=1, source_target_pairs={{32,0},{64,32},{96,64},{224,96},{192,224},{160,192},{128,160},{256... | collective-permute-start | bytes 98312 | tf_op jit(solution)/shard_map/ppermute | solution.py:617
  74.4 4.5 %collective-permute-start.6 = (f32[8,8,128]{2,1,0:T(8,128)S(1)}, f32[8,8,128]{2,1,0:T(8,128)S(1)}, u32[]{:S(2)}, u32[]{:S(2)}) collective-permute-start(f32[8,8,128]{2,1,0:T(8,128)S(1)} %slice_bitcast_fusion), channel_id=1, source_target_pairs={{0,32},{32,64},{64,96},{96,224},{224,192},{192,160},{160,128},{128... | collective-permute-start | bytes 98312 | tf_op jit(solution)/shard_map/ppermute | solution.py:617
  79.0 0.2 collective-permute-done.7
  79.2 1.4 %collective-permute-done.6 = f32[8,8,128]{2,1,0:T(8,128)S(1)} collective-permute-done((f32[8,8,128]{2,1,0:T(8,128)S(1)}, f32[8,8,128]{2,1,0:T(8,128)S(1)}, u32[]{:S(2)}, u32[]{:S(2)}) %collective-permute-start.6) | collective-permute-done | bytes 32800 | tf_op jit(solution)/shard_map/ppermute | solution.py:617
  80.6 3.9 %collective-permute-start.9 = (f32[8,24,128]{2,1,0:T(8,128)S(1)}, f32[8,24,128]{2,1,0:T(8,128)S(1)}, u32[]{:S(2)}, u32[]{:S(2)}) collective-permute-start(f32[8,24,128]{2,1,0:T(8,128)S(1)} %pad_maximum_fusion.own_u), channel_id=1, source_target_pairs={{1,0},{2,1},{3,2},{4,3},{5,4},{6,5},{7,6},{8,7},{9,8},{10,9},{11,1... | collective-permute-start | bytes 294920 | tf_op jit(solution)/shard_map/ppermute | solution.py:617
  84.4 1.9 %collective-permute-start.8 = (f32[8,24,128]{2,1,0:T(8,128)S(1)}, f32[8,24,128]{2,1,0:T(8,128)S(1)}, u32[]{:S(2)}, u32[]{:S(2)}) collective-permute-start(f32[8,24,128]{2,1,0:T(8,128)S(1)} %pad_maximum_fusion.own_u), channel_id=1, source_target_pairs={{0,1},{1,2},{2,3},{3,4},{4,5},{5,6},{6,7},{7,8},{8,9},{9,10},{10,1... | collective-permute-start | bytes 294920 | tf_op jit(solution)/shard_map/ppermute | solution.py:617
  86.4 0.3 collective-permute-done.9.high_u
  86.6 5.0 %collective-permute-done.8.low_u = f32[8,24,128]{2,1,0:T(8,128)S(1)} collective-permute-done((f32[8,24,128]{2,1,0:T(8,128)S(1)}, f32[8,24,128]{2,1,0:T(8,128)S(1)}, u32[]{:S(2)}, u32[]{:S(2)}) %collective-permute-start.8) | collective-permute-done | bytes 98336 | tf_op jit(solution)/shard_map/ppermute | solution.py:617
  91.6 2.8 %second.1 = f32[16,8,8,128]{3,2,1,0:T(8,128)S(1)} custom-call(f32[24,3,8,128]{3,2,1,0:T(8,128)S(1)} %strip.1.eta, f32[16,8,24,128]{3,2,1,0:T(8,128)S(1)} %all_to_all.10.sent, f32[104,8,128]{2,1,0:T(8,128)S(1)} %collective-permute-done.4.below, f32[104,8,128]{2,1,0:T(8,128)S(1)} %collective-permute-done.5.above, ...), custom_call_target="tpu_custom_call" | custom-call | tf_op jit(solution)/shard_map/second/pallas_call | solution.py:573
  94.4 14.4 %all_to_all.11.strips = f32[16,8,8,128]{3,2,1,0:T(8,128)S(1)} all-to-all(f32[16,8,8,128]{3,2,1,0:T(8,128)S(1)} %second.1), channel_id=1, replica_groups=mesh['tm'=16,'space'=32] {'tm'}, dimensions={0} | all-to-all | bytes 1048576 | tf_op jit(solution)/shard_map/all_to_all | solution.py:636
  108.9 0.9 place.1
  (2 shorter events, 0.0 us)
Async XLA Ops:
  2.9 11.1 %collective-permute-start.2 = (f32[8,16,8,128]{3,2,1,0:T(8,128)S(1)}, f32[8,16,8,128]{3,2,1,0:T(8,128)S(1)}, u32[]{:S(2)}, u32[]{:S(2)}) collective-permute-start(f32[8,16,8,128]{3,2,1,0:T(8,128)S(1)} %get-tuple-element.15.refs_2_.own_a), channel_id=1, source_target_pairs={{1,0},{2,1},{3,2},{4,3},{5,4},{6,5},{7,6},{8,7},{9,8},{10,9},{11,1... | collective-permute-start | bytes 1572872 | tf_op jit(solution)/shard_map/ppermute | solution.py:617
  4.8 11.7 %collective-permute-start.1 = (f32[8,16,8,128]{3,2,1,0:T(8,128)S(1)}, f32[8,16,8,128]{3,2,1,0:T(8,128)S(1)}, u32[]{:S(2)}, u32[]{:S(2)}) collective-permute-start(f32[8,16,8,128]{3,2,1,0:T(8,128)S(1)} %get-tuple-element.16.refs_3_.own_b), channel_id=1, source_target_pairs={{0,1},{1,2},{2,3},{3,4},{4,5},{5,6},{6,7},{7,8},{8,9},{9,10},{10,1... | collective-permute-start | bytes 1572872 | tf_op jit(solution)/shard_map/ppermute | solution.py:617
  7.2 14.9 %collective-permute-start = (f32[8,16,8,128]{3,2,1,0:T(8,128)S(1)}, f32[8,16,8,128]{3,2,1,0:T(8,128)S(1)}, u32[]{:S(2)}, u32[]{:S(2)}) collective-permute-start(f32[8,16,8,128]{3,2,1,0:T(8,128)S(1)} %get-tuple-element.15.refs_2_.own_a), channel_id=1, source_target_pairs={{0,1},{1,2},{2,3},{3,4},{4,5},{5,6},{6,7},{7,8},{8,9},{9,10},{10,1... | collective-permute-start | bytes 1572872 | tf_op jit(solution)/shard_map/ppermute | solution.py:617
  10.7 11.5 %collective-permute-start.3 = (f32[8,16,8,128]{3,2,1,0:T(8,128)S(1)}, f32[8,16,8,128]{3,2,1,0:T(8,128)S(1)}, u32[]{:S(2)}, u32[]{:S(2)}) collective-permute-start(f32[8,16,8,128]{3,2,1,0:T(8,128)S(1)} %get-tuple-element.16.refs_3_.own_b), channel_id=1, source_target_pairs={{1,0},{2,1},{3,2},{4,3},{5,4},{6,5},{7,6},{8,7},{9,8},{10,9},{11,1... | collective-permute-start | bytes 1572872 | tf_op jit(solution)/shard_map/ppermute | solution.py:617
  58.3 10.7 %collective-permute-start.4 = (f32[104,8,128]{2,1,0:T(8,128)S(1)}, f32[104,8,128]{2,1,0:T(8,128)S(1)}, u32[]{:S(2)}, u32[]{:S(2)}) collective-permute-start(f32[104,8,128]{2,1,0:T(8,128)S(1)} %get-tuple-element.23), channel_id=1, source_target_pairs={{0,1},{1,2},{2,3},{3,4},{4,5},{5,6},{6,7},{7,8},{8,9},{9,10},{10,1... | collective-permute-start | bytes 1277960 | tf_op jit(solution)/shard_map/ppermute | solution.py:617
  60.3 10.5 %collective-permute-start.5 = (f32[104,8,128]{2,1,0:T(8,128)S(1)}, f32[104,8,128]{2,1,0:T(8,128)S(1)}, u32[]{:S(2)}, u32[]{:S(2)}) collective-permute-start(f32[104,8,128]{2,1,0:T(8,128)S(1)} %get-tuple-element.24), channel_id=1, source_target_pairs={{1,0},{2,1},{3,2},{4,3},{5,4},{6,5},{7,6},{8,7},{9,8},{10,9},{11,1... | collective-permute-start | bytes 1277960 | tf_op jit(solution)/shard_map/ppermute | solution.py:617
  73.1 6.1 %collective-permute-start.7 = (f32[8,8,128]{2,1,0:T(8,128)S(1)}, f32[8,8,128]{2,1,0:T(8,128)S(1)}, u32[]{:S(2)}, u32[]{:S(2)}) collective-permute-start(f32[8,8,128]{2,1,0:T(8,128)S(1)} %slice_bitcast_fusion), channel_id=1, source_target_pairs={{32,0},{64,32},{96,64},{224,96},{192,224},{160,192},{128,160},{256... | collective-permute-start | bytes 98312 | tf_op jit(solution)/shard_map/ppermute | solution.py:617
  74.4 6.1 %collective-permute-start.6 = (f32[8,8,128]{2,1,0:T(8,128)S(1)}, f32[8,8,128]{2,1,0:T(8,128)S(1)}, u32[]{:S(2)}, u32[]{:S(2)}) collective-permute-start(f32[8,8,128]{2,1,0:T(8,128)S(1)} %slice_bitcast_fusion), channel_id=1, source_target_pairs={{0,32},{32,64},{64,96},{96,224},{224,192},{192,160},{160,128},{128... | collective-permute-start | bytes 98312 | tf_op jit(solution)/shard_map/ppermute | solution.py:617
  80.6 6.1 %collective-permute-start.9 = (f32[8,24,128]{2,1,0:T(8,128)S(1)}, f32[8,24,128]{2,1,0:T(8,128)S(1)}, u32[]{:S(2)}, u32[]{:S(2)}) collective-permute-start(f32[8,24,128]{2,1,0:T(8,128)S(1)} %pad_maximum_fusion.own_u), channel_id=1, source_target_pairs={{1,0},{2,1},{3,2},{4,3},{5,4},{6,5},{7,6},{8,7},{9,8},{10,9},{11,1... | collective-permute-start | bytes 294920 | tf_op jit(solution)/shard_map/ppermute | solution.py:617
  84.4 7.1 %collective-permute-start.8 = (f32[8,24,128]{2,1,0:T(8,128)S(1)}, f32[8,24,128]{2,1,0:T(8,128)S(1)}, u32[]{:S(2)}, u32[]{:S(2)}) collective-permute-start(f32[8,24,128]{2,1,0:T(8,128)S(1)} %pad_maximum_fusion.own_u), channel_id=1, source_target_pairs={{0,1},{1,2},{2,3},{3,4},{4,5},{5,6},{6,7},{7,8},{8,9},{9,10},{10,1... | collective-permute-start | bytes 294920 | tf_op jit(solution)/shard_map/ppermute | solution.py:617

commit v6 on v5

--- a/solution.py
+++ b/solution.py
@@ -118,6 +118,16 @@
     return below, above
 
 
+def is_mirrored():
+    return lax.rem(lax.axis_index("space"), 2) == 1
+
+
+def next_chip_exists():
+    index = lax.axis_index("space")
+    at_end = (index == 0) | (index == lax.axis_size("space") - 1)
+    return jnp.where(at_end, 0.0, 1.0).astype(jnp.float32)
+
+
 def one_trip():
     return jnp.where(lax.axis_index("space") < 0, 2, 1)
 
@@ -127,29 +137,32 @@
     small = pltpu.make_async_copy(resistivity, resistivity_s, sems.at[4])
     small.start()
     copies = []
+    odd = is_mirrored()
     for h in range(2):
-        part = pl.ds(h * HALF, HALF)
+        part = pl.ds(jnp.where(odd, 1 - h, h) * HALF, HALF)
         pair = (
-            pltpu.make_async_copy(start.at[part], start_v.at[part], sems.at[2 * h]),
-            pltpu.make_async_copy(regions.at[part], regions_v.at[part], sems.at[2 * h + 1]),
+            pltpu.make_async_copy(start.at[part], start_v.at[h], sems.at[2 * h]),
+            pltpu.make_async_copy(regions.at[part], regions_v.at[h], sems.at[2 * h + 1]),
         )
         for copy in pair:
             copy.start()
         copies.append(pair)
     small.wait()
     scaled = [resistivity_s[i] * jnp.float32(0.5 * fine_step) for i in range(REGIONS)]
+    once = one_trip()
     for h in range(2):
         for copy in copies[h]:
             copy.wait()
 
-        def planes(n, _, h=h):
-            for x in (2 * n, 2 * n + 1):
+        def planes(_, carry, h=h):
+            for x in range(HALF):
+                source = jnp.where(odd, HALF - 1 - x, x)
                 for ry in range(Q):
                     u, e = [], []
                     for g in range(Q):
                         where = rows_at(g, ry)
-                        u.append(start_v[h * HALF + x, where, :])
-                        region = regions_v[h * HALF + x, where, :]
+                        u.append(start_v[h, source, where, :])
+                        region = regions_v[h, source, where, :]
                         value = jnp.zeros((8, NZ), jnp.float32)
                         for i in range(REGIONS):
                             value = jnp.where(region == i, scaled[i], value)
@@ -158,9 +171,9 @@
                     for rz in range(Q):
                         outs[h][x, Q * ry + rz] = u[rz]
                         outs[h][HALF + x, Q * ry + rz] = e[rz]
-            return 0
-
-        lax.fori_loop(0, HALF // 2, planes, 0)
+            return carry
+
+        lax.fori_loop(0, once, planes, 0)
 
 
 def own_part(start, regions, resistivity):
@@ -172,8 +185,8 @@
         in_specs=[hbm] * 3,
         out_specs=(VMEM, VMEM),
         scratch_shapes=[
-            pltpu.VMEM((BX, NY, NZ), jnp.float32),
-            pltpu.VMEM((BX, NY, NZ), jnp.int32),
+            pltpu.VMEM((2, HALF, NY, NZ), jnp.float32),
+            pltpu.VMEM((2, HALF, NY, NZ), jnp.int32),
             pltpu.SMEM((REGIONS,), jnp.float32),
             pltpu.SemaphoreType.DMA((5,)),
         ],
@@ -185,20 +198,21 @@
 class Fine:
     def __init__(self, u_ref, k_ref, e_ref, f_ref):
         self.u, self.k, self.e, self.f = u_ref, k_ref, e_ref, f_ref
-        self.below, self.above = has_neighbours(lax.axis_index("space"), lax.axis_size("space"))
+        self.below = next_chip_exists()
         lane, sub = iotas()
         self.z_high, self.z_low = [(lane & (CHUNK - 1)) == v for v in (CHUNK - 1, 0)]
         self.y_high, self.y_low = sub == 7, sub == 0
         self.y_end = (sub == 7) & (lane >= NZ - CHUNK)
         self.y_start = (sub == 0) & (lane < CHUNK)
 
-    def stage(self, ref, base):
+    def stage(self, ref, base, turn=False):
         def one(x, _):
+            to = base + (HALF - 1 - x if turn else x)
             for r in range(PARTS):
                 u, e = ref[x, r], ref[HALF + x, r]
-                self.u[base + x, r] = u
-                self.e[base + x, r] = e
-                self.k[base + x, r] = coeff(e, u)
+                self.u[to, r] = u
+                self.e[to, r] = e
+                self.k[to, r] = coeff(e, u)
             return 0
 
         lax.fori_loop(0, HALF, one, 0)
@@ -271,7 +285,7 @@
         self.stretches(first, count, size, emit)
 
     def keep(self, x, r, u0, total):
-        inside = jnp.where(x < BX, self.below, jnp.where(x < 2 * BX, jnp.float32(1.0), self.above))
+        inside = jnp.where(x < BX, self.below, jnp.float32(1.0))
         new = inside * (u0 + total)
         self.u[x, r] = new
         self.k[x, r] = coeff(self.e[x, r], new)
@@ -288,7 +302,7 @@
     later = jnp.where(lax.axis_index("tm") == 0, 0.0, 1.0).astype(jnp.float32)
     fine = Fine(u_ref, k_ref, e_ref, f_ref)
     for n, ref in enumerate((low, own_a, own_b, high)):
-        fine.stage(ref, (n + 1) * HALF)
+        fine.stage(ref, (n + 1) * HALF, turn=n in (0, 3))
 
     def keep_first(x, r, u0, total):
         g_ref[x - HALF, r] = later * (u0 + STEPS * total)
@@ -308,8 +322,8 @@
 
 def outer_kernel(low, high, u_in, k_in, e_in, g_ref, save, out, u_ref, k_ref, e_ref, f_ref, s_ref):
     fine = Fine(u_ref, k_ref, e_ref, f_ref)
-    fine.stage(low, 0)
-    fine.stage(high, 5 * HALF)
+    fine.stage(low, 0, turn=True)
+    fine.stage(high, 5 * HALF, turn=True)
 
     once = one_trip()
 
@@ -337,11 +351,11 @@
     fine.step(BX, 2, HALF, keep_last)
 
     def natural(n, _):
-        for x in (2 * n, 2 * n + 1):
-            to_rows(u_ref.at[x], s_ref.at[x])
+        for q in range(HALF):
+            to_rows(u_ref.at[HALF * n + q], s_ref.at[HALF * n + q])
         return 0
 
-    lax.fori_loop(0, BX // 2, natural, 0)
+    lax.fori_loop(0, 2, natural, 0)
 
     def spread(x, _):
         for j in range(SLICES):
@@ -430,7 +444,8 @@
 
         def natural(m, _, n=n, ref=ref):
             for x in (2 * m, 2 * m + 1):
-                to_rows(ref.at[HALF + x], rows.at[n * HALF + x])
+                to = HALF - 1 - x if n in (0, 1, 4, 5) else x
+                to_rows(ref.at[HALF + x], rows.at[n * HALF + to])
             return 0
 
         lax.fori_loop(0, HALF // 2, natural, 0)
@@ -466,14 +481,14 @@
 
 def coarse_steps(count, base, eta, refs, u_ref, k_ref, f_ref, out):
     lane, row = iotas()
-    x_below, x_above = has_neighbours(lax.axis_index("space"), lax.axis_size("space"))
+    x_below = next_chip_exists()
     y_below, y_above = has_neighbours(strip_of(lax.axis_index("tm")), SLICES)
     once = one_trip()
 
     def mask(x, c):
         factors = []
-        if not BX <= x < 2 * BX:
-            factors.append(x_below if x < BX else x_above)
+        if x < BX:
+            factors.append(x_below)
         if c != 1:
             factors.append(y_below if c == 0 else y_above)
         return factors[0] * factors[1] if len(factors) == 2 else (factors or [None])[0]
@@ -526,7 +541,7 @@
                         u_ref[x, c] = new
                         k_ref[x, c] = coeff(eta[x, c], new)
                     if c == 1 and far == 0:
-                        out[base + n, x - BX] = new
+                        out(n, x - BX, new)
             for c in range(3):
                 if flux[c] is not None:
                     f_ref[c] = flux[c]
@@ -553,19 +568,33 @@
                 u_ref[x, c] = jnp.zeros((8, NZ), jnp.float32)
     for x in range(BX):
         out[0, x] = sent[0, x, ROWS : 2 * ROWS, :]
-    coarse_steps(FIRST, 0, eta, refs, u_ref, k_ref, f_ref, out)
+
+    def put(n, x, value):
+        out[n, x] = value
+
+    coarse_steps(FIRST, 0, eta, refs, u_ref, k_ref, f_ref, put)
 
 
 def second_kernel(eta, sent, below, above, low_u, own_u, high_u, done, out, u_ref, k_ref, f_ref):
+    odd = is_mirrored()
+
+    def true_plane(x):
+        return jnp.where(odd, BX - 1 - x, x)
+
     for b, ref in enumerate((low_u, own_u, high_u)):
         for x in range(BX):
             for c in range(3):
-                u_ref[b * BX + x, c] = ref[x, c * ROWS : (c + 1) * ROWS, :]
+                to = b * BX + (x if b == 1 else BX - 1 - x)
+                u_ref[to, c] = ref[x, c * ROWS : (c + 1) * ROWS, :]
     for i in range(FIRST + 1):
         for x in range(BX):
-            out[i, x] = done[i, x]
+            out[i, true_plane(x)] = done[i, x]
     refs = (sent, below, above)
-    coarse_steps(SLICES - 1 - FIRST, FIRST, eta, refs, u_ref, k_ref, f_ref, out)
+
+    def put(n, x, value):
+        out[FIRST + n, true_plane(x)] = value
+
+    coarse_steps(SLICES - 1 - FIRST, FIRST, eta, refs, u_ref, k_ref, f_ref, put)
 
 
 def coarse_call(kernel, name, count, *operands):
@@ -610,26 +639,40 @@
     )(strips)
 
 
-def both_ways(down, up, axis):
-    line = ORDER if axis == "tm" else range(lax.axis_size(axis))
-    forward = list(zip(line[:-1], line[1:]))
-    backward = [(b, a) for a, b in forward]
-    return lax.ppermute(up, axis, forward), lax.ppermute(down, axis, backward)
+def across(value):
+    count = lax.axis_size("space")
+    pairs = [(i, i + 1) for i in range(1, count - 1, 2)]
+    return lax.ppermute(value, "space", pairs + [(b, a) for a, b in pairs])
+
+
+def beside(value):
+    pairs = [(i, i + 1) for i in range(0, lax.axis_size("space"), 2)]
+    return lax.ppermute(value, "space", pairs + [(b, a) for a, b in pairs])
+
+
+def with_strips(state):
+    sides = []
+    for first in (0, 1):
+        pairs = [(ORDER[q], ORDER[q + 1]) for q in range(first, SLICES - 1, 2)]
+        sides.append(lax.ppermute(state, "tm", pairs + [(b, a) for a, b in pairs]))
+    even = lax.rem(strip_of(lax.axis_index("tm")), 2) == 0
+    low = jnp.where(even, sides[1], sides[0])
+    high = jnp.where(even, sides[0], sides[1])
+    return jnp.concatenate([low, state, high], axis=1)
 
 
 def per_device(start_values, regions, resistivity):
     own_a, own_b = own_part(start_values[0], regions, resistivity)
-    low_b, high_a = both_ways(own_a, own_b, "space")
-    low_a, high_b = both_ways(own_b, own_a, "space")
-    sent = outer(low_a, high_b, *inner(low_b, own_a, own_b, high_a))
+    low_near, high_near = across(own_a), beside(own_b)
+    low_far, high_far = across(own_b), beside(own_a)
+    sent = outer(low_far, high_far, *inner(low_near, own_a, own_b, high_near))
     sent = lax.all_to_all(sent, "tm", 0, 0)
-    below, above = both_ways(*pack(sent), "space")
-    eta = strip_part(low_a, low_b, own_a, own_b, high_a, high_b)
+    down, up = pack(sent)
+    below, above = across(down), beside(up)
+    eta = strip_part(low_far, low_near, own_a, own_b, high_near, high_far)
     done = coarse_call(first_kernel, "first", FIRST + 1, eta, sent, below, above)
-    state = done[FIRST]
-    y_low, y_high = both_ways(state, state, "tm")
-    strip = jnp.concatenate([y_low, state, y_high], axis=1)
-    x_low, x_high = both_ways(strip, strip, "space")
+    strip = with_strips(done[FIRST])
+    x_low, x_high = across(strip), beside(strip)
     ends = coarse_call(
         second_kernel, "second", SLICES, eta, sent, below, above, x_low, strip, x_high, done
     )

time: 110 us -> 107 us (0.973)
  the two profiles are of different devices: /device:TPU:128 before, /device:TPU:96 now
where the time goes in v6:
time: 107 us
  blocking collectives  48.3 us (45%)
  starting transfers between devices  29.4 us (27%)
  Pallas kernels  23.8 us (22%)
  waiting for transfers between devices  5.07 us (5%)
    all_to_all x1, blocking collectives, per_device(): sent = lax.all_to_all(sent, 'tm', 0, 0)  30.9 us
    all_to_all x1, blocking collectives, per_device(): result = lax.all_to_all(ends, 'tm', 0, 0)  17.3 us
    ppermute x4, starting transfers between devices, beside(): return lax.ppermute(value, 'space', pairs + [(b, a) for a, b in pairs])  16.9 us
    ppermute x4, starting transfers between devices, across(): return lax.ppermute(value, 'space', pairs + [(b, a) for a, b in pairs])  7.68 us
    pallas_call x1, Pallas kernels, outer(): pl.pallas_call(outer_kernel, out_shape=(jax.ShapeDtypeStruct((SLICES, BX,...  6.68 us
    pallas_call x2, Pallas kernels, coarse_call(): pl.pallas_call(kernel, out_shape=jax.ShapeDtypeStruct((count, BX, ROWS, N...  5.16 us
    ppermute x2, starting transfers between devices, with_strips(): sides.append(lax.ppermute(state, 'tm', pairs + [(b, a) for a, b in pairs]))  4.86 us
    pallas_call x1, Pallas kernels, own_part(): pl.pallas_call(own_kernel, out_shape=(shape, shape), in_specs=[hbm] * 3,...  4.49 us
  transfers between devices with their start and end apart: 10, of which 4 were waited for; matrix products, arithmetic and copies ran while one was open for 0% of the time, Pallas kernels for 6%

profile of v6, /device:TPU:96, one launch (start us, length us, event | category | flops | bytes accessed | tf_op | source)
XLA Modules:
  0.0 106.8 jit_solution(14269020330297423117)
XLA Ops:
  0.0 4.5 %own.1 = (f32[8,16,8,128]{3,2,1,0:T(8,128)S(1)}, f32[8,16,8,128]{3,2,1,0:T(8,128)S(1)}) custom-call(f32[8,128,128]{2,1,0:T(8,128)} %bitcast.4, s32[8,128,128]{2,1,0:T(8,128)} %regions.1, f32[4]{0:T(128)} %resistivity.1), custom_call_target="tpu_custom_call" | custom-call | tf_op jit(solution)/shard_map/own/pallas_call | solution.py:182
  4.5 1.9 %collective-permute-start.1 = (f32[8,16,8,128]{3,2,1,0:T(8,128)S(1)}, f32[8,16,8,128]{3,2,1,0:T(8,128)S(1)}, u32[]{:S(2)}, u32[]{:S(2)}) collective-permute-start(f32[8,16,8,128]{3,2,1,0:T(8,128)S(1)} %get-tuple-element.16.refs_2_.own_a), channel_id=1, source_target_pairs={{1,2},{3,4},{5,6},{7,8},{9,10},{11,12},{13,14},{15,16},{17,18},{19... | collective-permute-start | bytes 1572872 | tf_op jit(solution)/shard_map/ppermute | solution.py:645
  6.4 5.1 %collective-permute-start.2 = (f32[8,16,8,128]{3,2,1,0:T(8,128)S(1)}, f32[8,16,8,128]{3,2,1,0:T(8,128)S(1)}, u32[]{:S(2)}, u32[]{:S(2)}) collective-permute-start(f32[8,16,8,128]{3,2,1,0:T(8,128)S(1)} %get-tuple-element.15.refs_3_.own_b), channel_id=1, source_target_pairs={{0,1},{2,3},{4,5},{6,7},{8,9},{10,11},{12,13},{14,15},{16,17},{18,... | collective-permute-start | bytes 1572872 | tf_op jit(solution)/shard_map/ppermute | solution.py:650
  11.6 1.9 %collective-permute-start = (f32[8,16,8,128]{3,2,1,0:T(8,128)S(1)}, f32[8,16,8,128]{3,2,1,0:T(8,128)S(1)}, u32[]{:S(2)}, u32[]{:S(2)}) collective-permute-start(f32[8,16,8,128]{3,2,1,0:T(8,128)S(1)} %get-tuple-element.15.refs_3_.own_b), channel_id=1, source_target_pairs={{1,2},{3,4},{5,6},{7,8},{9,10},{11,12},{13,14},{15,16},{17,18},{19... | collective-permute-start | bytes 1572872 | tf_op jit(solution)/shard_map/ppermute | solution.py:645
  13.5 3.9 %collective-permute-start.3 = (f32[8,16,8,128]{3,2,1,0:T(8,128)S(1)}, f32[8,16,8,128]{3,2,1,0:T(8,128)S(1)}, u32[]{:S(2)}, u32[]{:S(2)}) collective-permute-start(f32[8,16,8,128]{3,2,1,0:T(8,128)S(1)} %get-tuple-element.16.refs_2_.own_a), channel_id=1, source_target_pairs={{0,1},{2,3},{4,5},{6,7},{8,9},{10,11},{12,13},{14,15},{16,17},{18,... | collective-permute-start | bytes 1572872 | tf_op jit(solution)/shard_map/ppermute | solution.py:650
  17.4 0.0 collective-permute-done.1.refs_1_.low
  17.4 0.0 collective-permute-done.2.refs_4_.high
  17.5 3.8 %inner.1 = (f32[25,16,8,128]{3,2,1,0:T(8,128)S(1)}, f32[25,16,8,128]{3,2,1,0:T(8,128)S(1)}, f32[25,16,8,128]{3,2,1,0:T(8,128)S(1)}, f32[16,16,8,128]{3,2,1,0:T(8,128)S(1)}, f32[4,5,16,8,128]{4,3,2,1,0:T(8,128)S(1)}) custom-call(f32[8,16,8,128]{3,2,1,0:T(8,128)S(1)} %collective-permute-done.1.refs_1_.low, ...), custom_call_target="tpu_custom_call" | custom-call | flops 100000000 | bytes 10000000 | tf_op jit(solution)/shard_map/inner/pallas_call | solution.py:379
  21.2 0.8 collective-permute-done.refs_0_.low
  22.1 0.0 collective-permute-done.3.refs_5_.high
  22.1 6.7 %outer.1 = (f32[16,8,24,128]{3,2,1,0:T(8,128)S(1)}, f32[25,16,8,128]{3,2,1,0:T(8,128)S(1)}, f32[25,16,8,128]{3,2,1,0:T(8,128)S(1)}, f32[25,16,8,128]{3,2,1,0:T(8,128)S(1)}) custom-call(f32[8,16,8,128]{3,2,1,0:T(8,128)S(1)} %collective-permute-done.refs_0_.low, ...), custom_call_target="tpu_custom_call", output_to_operand_aliasing={{1}: (2, {}), {2}: (3, {}), {3}: (4, {})} | custom-call | tf_op jit(solution)/shard_map/outer/pallas_call | solution.py:399
  28.8 30.9 %all_to_all.10.sent = f32[16,8,24,128]{3,2,1,0:T(8,128)S(1)} all-to-all(f32[16,8,24,128]{3,2,1,0:T(8,128)S(1)} %get-tuple-element.22), channel_id=1, replica_groups=mesh['tm'=16,'space'=32] {'tm'}, dimensions={0} | all-to-all | bytes 3145728 | tf_op jit(solution)/shard_map/all_to_all | solution.py:669
  59.7 0.1 pack.1
  59.8 1.9 %collective-permute-start.4 = (f32[104,8,128]{2,1,0:T(8,128)S(1)}, f32[104,8,128]{2,1,0:T(8,128)S(1)}, u32[]{:S(2)}, u32[]{:S(2)}) collective-permute-start(f32[104,8,128]{2,1,0:T(8,128)S(1)} %get-tuple-element.23), channel_id=1, source_target_pairs={{1,2},{3,4},{5,6},{7,8},{9,10},{11,12},{13,14},{15,16},{17,18},{19... | collective-permute-start | bytes 1277960 | tf_op jit(solution)/shard_map/ppermute | solution.py:645
  61.7 3.3 %collective-permute-start.5 = (f32[104,8,128]{2,1,0:T(8,128)S(1)}, f32[104,8,128]{2,1,0:T(8,128)S(1)}, u32[]{:S(2)}, u32[]{:S(2)}) collective-permute-start(f32[104,8,128]{2,1,0:T(8,128)S(1)} %get-tuple-element.24), channel_id=1, source_target_pairs={{0,1},{2,3},{4,5},{6,7},{8,9},{10,11},{12,13},{14,15},{16,17},{18,... | collective-permute-start | bytes 1277960 | tf_op jit(solution)/shard_map/ppermute | solution.py:650
  65.0 2.8 %strip.1.eta = f32[24,3,8,128]{3,2,1,0:T(8,128)S(1)} custom-call(f32[8,16,8,128]{3,2,1,0:T(8,128)S(1)} %collective-permute-done.refs_0_.low, f32[8,16,8,128]{3,2,1,0:T(8,128)S(1)} %collective-permute-done.1.refs_1_.low, f32[8,16,8,128]{3,2,1,0:T(8,128)S(1)} %get-tuple-element.16.refs_2_.own_a, f32[8,16,8,128]{3,2,1,0:T(8,128)S(1)} %get-tuple-element.15.refs_3_.own_b, ...), custom_call_target="tpu_custom_call" | custom-call | flops 1000000 | bytes 1000000 | tf_op jit(solution)/shard_map/strip/pallas_call | solution.py:461
  67.8 1.4 %collective-permute-done.4.below = f32[104,8,128]{2,1,0:T(8,128)S(1)} collective-permute-done((f32[104,8,128]{2,1,0:T(8,128)S(1)}, f32[104,8,128]{2,1,0:T(8,128)S(1)}, u32[]{:S(2)}, u32[]{:S(2)}) %collective-permute-start.4) | collective-permute-done | bytes 426016 | tf_op jit(solution)/shard_map/ppermute | solution.py:645
  69.2 0.0 collective-permute-done.5.above
  69.2 2.4 %first.1.done = f32[8,8,8,128]{3,2,1,0:T(8,128)S(1)} custom-call(f32[24,3,8,128]{3,2,1,0:T(8,128)S(1)} %strip.1.eta, f32[16,8,24,128]{3,2,1,0:T(8,128)S(1)} %all_to_all.10.sent, f32[104,8,128]{2,1,0:T(8,128)S(1)} %collective-permute-done.4.below, f32[104,8,128]{2,1,0:T(8,128)S(1)} %collective-permute-done.5.above), custom_call_target="tpu_custom_call" | custom-call | tf_op jit(solution)/shard_map/first/pallas_call | solution.py:602
  71.6 0.7 collective-permute-start.6
  72.3 4.2 %collective-permute-start.7 = (f32[8,8,128]{2,1,0:T(8,128)S(1)}, f32[8,8,128]{2,1,0:T(8,128)S(1)}, u32[]{:S(2)}, u32[]{:S(2)}) collective-permute-start(f32[8,8,128]{2,1,0:T(8,128)S(1)} %slice_bitcast_fusion), channel_id=1, source_target_pairs={{0,32},{64,96},{224,192},{160,128},{256,288},{320,352},{480,448},{... | collective-permute-start | bytes 98312 | tf_op jit(solution)/shard_map/ppermute | solution.py:657
  76.5 0.0 collective-permute-done.6
  76.5 1.9 %collective-permute-done.7 = f32[8,8,128]{2,1,0:T(8,128)S(1)} collective-permute-done((f32[8,8,128]{2,1,0:T(8,128)S(1)}, f32[8,8,128]{2,1,0:T(8,128)S(1)}, u32[]{:S(2)}, u32[]{:S(2)}) %collective-permute-start.7) | collective-permute-done | bytes 32800 | tf_op jit(solution)/shard_map/ppermute | solution.py:657
  78.4 1.9 %collective-permute-start.8 = (f32[8,24,128]{2,1,0:T(8,128)S(1)}, f32[8,24,128]{2,1,0:T(8,128)S(1)}, u32[]{:S(2)}, u32[]{:S(2)}) collective-permute-start(f32[8,24,128]{2,1,0:T(8,128)S(1)} %pad_maximum_fusion.own_u), channel_id=1, source_target_pairs={{1,2},{3,4},{5,6},{7,8},{9,10},{11,12},{13,14},{15,16},{17,18},{19... | collective-permute-start | bytes 294920 | tf_op jit(solution)/shard_map/ppermute | solution.py:645
  80.3 4.5 %collective-permute-start.9 = (f32[8,24,128]{2,1,0:T(8,128)S(1)}, f32[8,24,128]{2,1,0:T(8,128)S(1)}, u32[]{:S(2)}, u32[]{:S(2)}) collective-permute-start(f32[8,24,128]{2,1,0:T(8,128)S(1)} %pad_maximum_fusion.own_u), channel_id=1, source_target_pairs={{0,1},{2,3},{4,5},{6,7},{8,9},{10,11},{12,13},{14,15},{16,17},{18,... | collective-permute-start | bytes 294920 | tf_op jit(solution)/shard_map/ppermute | solution.py:650
  84.9 0.0 collective-permute-done.8.low_u
  84.9 0.9 collective-permute-done.9.high_u
  85.8 2.8 %second.1 = f32[16,8,8,128]{3,2,1,0:T(8,128)S(1)} custom-call(f32[24,3,8,128]{3,2,1,0:T(8,128)S(1)} %strip.1.eta, f32[16,8,24,128]{3,2,1,0:T(8,128)S(1)} %all_to_all.10.sent, f32[104,8,128]{2,1,0:T(8,128)S(1)} %collective-permute-done.4.below, f32[104,8,128]{2,1,0:T(8,128)S(1)} %collective-permute-done.5.above, ...), custom_call_target="tpu_custom_call" | custom-call | tf_op jit(solution)/shard_map/second/pallas_call | solution.py:602
  88.6 17.3 %all_to_all.11.strips = f32[16,8,8,128]{3,2,1,0:T(8,128)S(1)} all-to-all(f32[16,8,8,128]{3,2,1,0:T(8,128)S(1)} %second.1), channel_id=1, replica_groups=mesh['tm'=16,'space'=32] {'tm'}, dimensions={0} | all-to-all | bytes 1048576 | tf_op jit(solution)/shard_map/all_to_all | solution.py:679
  105.9 0.9 place.1
  (3 shorter events, 0.0 us)
Async XLA Ops:
  4.5 12.9 %collective-permute-start.1 = (f32[8,16,8,128]{3,2,1,0:T(8,128)S(1)}, f32[8,16,8,128]{3,2,1,0:T(8,128)S(1)}, u32[]{:S(2)}, u32[]{:S(2)}) collective-permute-start(f32[8,16,8,128]{3,2,1,0:T(8,128)S(1)} %get-tuple-element.16.refs_2_.own_a), channel_id=1, source_target_pairs={{1,2},{3,4},{5,6},{7,8},{9,10},{11,12},{13,14},{15,16},{17,18},{19... | collective-permute-start | bytes 1572872 | tf_op jit(solution)/shard_map/ppermute | solution.py:645
  6.4 11.0 %collective-permute-start.2 = (f32[8,16,8,128]{3,2,1,0:T(8,128)S(1)}, f32[8,16,8,128]{3,2,1,0:T(8,128)S(1)}, u32[]{:S(2)}, u32[]{:S(2)}) collective-permute-start(f32[8,16,8,128]{3,2,1,0:T(8,128)S(1)} %get-tuple-element.15.refs_3_.own_b), channel_id=1, source_target_pairs={{0,1},{2,3},{4,5},{6,7},{8,9},{10,11},{12,13},{14,15},{16,17},{18,... | collective-permute-start | bytes 1572872 | tf_op jit(solution)/shard_map/ppermute | solution.py:650
  11.6 10.5 %collective-permute-start = (f32[8,16,8,128]{3,2,1,0:T(8,128)S(1)}, f32[8,16,8,128]{3,2,1,0:T(8,128)S(1)}, u32[]{:S(2)}, u32[]{:S(2)}) collective-permute-start(f32[8,16,8,128]{3,2,1,0:T(8,128)S(1)} %get-tuple-element.15.refs_3_.own_b), channel_id=1, source_target_pairs={{1,2},{3,4},{5,6},{7,8},{9,10},{11,12},{13,14},{15,16},{17,18},{19... | collective-permute-start | bytes 1572872 | tf_op jit(solution)/shard_map/ppermute | solution.py:645
  13.5 8.6 %collective-permute-start.3 = (f32[8,16,8,128]{3,2,1,0:T(8,128)S(1)}, f32[8,16,8,128]{3,2,1,0:T(8,128)S(1)}, u32[]{:S(2)}, u32[]{:S(2)}) collective-permute-start(f32[8,16,8,128]{3,2,1,0:T(8,128)S(1)} %get-tuple-element.16.refs_2_.own_a), channel_id=1, source_target_pairs={{0,1},{2,3},{4,5},{6,7},{8,9},{10,11},{12,13},{14,15},{16,17},{18,... | collective-permute-start | bytes 1572872 | tf_op jit(solution)/shard_map/ppermute | solution.py:650
  59.8 9.4 %collective-permute-start.4 = (f32[104,8,128]{2,1,0:T(8,128)S(1)}, f32[104,8,128]{2,1,0:T(8,128)S(1)}, u32[]{:S(2)}, u32[]{:S(2)}) collective-permute-start(f32[104,8,128]{2,1,0:T(8,128)S(1)} %get-tuple-element.23), channel_id=1, source_target_pairs={{1,2},{3,4},{5,6},{7,8},{9,10},{11,12},{13,14},{15,16},{17,18},{19... | collective-permute-start | bytes 1277960 | tf_op jit(solution)/shard_map/ppermute | solution.py:645
  61.7 7.5 %collective-permute-start.5 = (f32[104,8,128]{2,1,0:T(8,128)S(1)}, f32[104,8,128]{2,1,0:T(8,128)S(1)}, u32[]{:S(2)}, u32[]{:S(2)}) collective-permute-start(f32[104,8,128]{2,1,0:T(8,128)S(1)} %get-tuple-element.24), channel_id=1, source_target_pairs={{0,1},{2,3},{4,5},{6,7},{8,9},{10,11},{12,13},{14,15},{16,17},{18,... | collective-permute-start | bytes 1277960 | tf_op jit(solution)/shard_map/ppermute | solution.py:650
  71.6 4.9 %collective-permute-start.6 = (f32[8,8,128]{2,1,0:T(8,128)S(1)}, f32[8,8,128]{2,1,0:T(8,128)S(1)}, u32[]{:S(2)}, u32[]{:S(2)}) collective-permute-start(f32[8,8,128]{2,1,0:T(8,128)S(1)} %slice_bitcast_fusion), channel_id=1, source_target_pairs={{32,64},{96,224},{192,160},{128,256},{288,320},{352,480},{448,416}... | collective-permute-start | bytes 98312 | tf_op jit(solution)/shard_map/ppermute | solution.py:657
  72.3 6.1 %collective-permute-start.7 = (f32[8,8,128]{2,1,0:T(8,128)S(1)}, f32[8,8,128]{2,1,0:T(8,128)S(1)}, u32[]{:S(2)}, u32[]{:S(2)}) collective-permute-start(f32[8,8,128]{2,1,0:T(8,128)S(1)} %slice_bitcast_fusion), channel_id=1, source_target_pairs={{0,32},{64,96},{224,192},{160,128},{256,288},{320,352},{480,448},{... | collective-permute-start | bytes 98312 | tf_op jit(solution)/shard_map/ppermute | solution.py:657
  78.4 6.5 %collective-permute-start.8 = (f32[8,24,128]{2,1,0:T(8,128)S(1)}, f32[8,24,128]{2,1,0:T(8,128)S(1)}, u32[]{:S(2)}, u32[]{:S(2)}) collective-permute-start(f32[8,24,128]{2,1,0:T(8,128)S(1)} %pad_maximum_fusion.own_u), channel_id=1, source_target_pairs={{1,2},{3,4},{5,6},{7,8},{9,10},{11,12},{13,14},{15,16},{17,18},{19... | collective-permute-start | bytes 294920 | tf_op jit(solution)/shard_map/ppermute | solution.py:645
  80.3 5.5 %collective-permute-start.9 = (f32[8,24,128]{2,1,0:T(8,128)S(1)}, f32[8,24,128]{2,1,0:T(8,128)S(1)}, u32[]{:S(2)}, u32[]{:S(2)}) collective-permute-start(f32[8,24,128]{2,1,0:T(8,128)S(1)} %pad_maximum_fusion.own_u), channel_id=1, source_target_pairs={{0,1},{2,3},{4,5},{6,7},{8,9},{10,11},{12,13},{14,15},{16,17},{18,... | collective-permute-start | bytes 294920 | tf_op jit(solution)/shard_map/ppermute | solution.py:650

commit v7 on v6

--- a/solution.py
+++ b/solution.py
@@ -49,6 +49,7 @@
     for _c in {"mid": (1,), "both": (0, 2), "low": (0,), "high": (2,)}[_kind]:
         PLACE[_i, _d, _c] = _n
 PARTS = NY // 8
+LOAD = 3 * BX - 2
 GROUP = 40
 
 
@@ -74,12 +75,14 @@
     return jnp.where(lane < 2 * CHUNK, low, jnp.where(lane < 3 * CHUNK, values[2], values[3]))
 
 
-def interleave(rows):
+def turn(h, rows):
     lane, _ = iotas()
-    turned = []
-    for h in range(Q):
-        source = Q * (lane & (CHUNK - 1)) + (((lane >> 5) - h) & (Q - 1))
-        turned.append(jnp.take_along_axis(rows[h], source, axis=1))
+    source = Q * (lane & (CHUNK - 1)) + (((lane >> 5) - h) & (Q - 1))
+    return jnp.take_along_axis(rows, source, axis=1)
+
+
+def gather_tiles(turned):
+    lane, _ = iotas()
     tiles = []
     for rz in range(Q):
         tile = by_chunk(lane, [turned[(c - rz) % Q] for c in range(Q)])
@@ -133,7 +136,7 @@
 
 
 def own_kernel(start, regions, resistivity, *refs):
-    outs, (start_v, regions_v, resistivity_s, sems) = refs[:2], refs[2:]
+    outs, (start_v, regions_v, half_v, resistivity_s, sems) = refs[:2], refs[2:]
     small = pltpu.make_async_copy(resistivity, resistivity_s, sems.at[4])
     small.start()
     copies = []
@@ -149,31 +152,34 @@
         copies.append(pair)
     small.wait()
     scaled = [resistivity_s[i] * jnp.float32(0.5 * fine_step) for i in range(REGIONS)]
-    once = one_trip()
     for h in range(2):
         for copy in copies[h]:
             copy.wait()
 
-        def planes(_, carry, h=h):
-            for x in range(HALF):
+        def first_pass(n, _, h=h):
+            for x in (2 * n, 2 * n + 1):
                 source = jnp.where(odd, HALF - 1 - x, x)
                 for ry in range(Q):
-                    u, e = [], []
                     for g in range(Q):
                         where = rows_at(g, ry)
-                        u.append(start_v[h, source, where, :])
                         region = regions_v[h, source, where, :]
                         value = jnp.zeros((8, NZ), jnp.float32)
                         for i in range(REGIONS):
                             value = jnp.where(region == i, scaled[i], value)
-                        e.append(value)
-                    u, e = interleave(u), interleave(e)
+                        half_v[x, Q * ry + g] = turn(g, start_v[h, source, where, :])
+                        half_v[HALF + x, Q * ry + g] = turn(g, value)
+            return 0
+
+        def second_pass(n, _, h=h):
+            for x in (2 * n, 2 * n + 1):
+                for ry in range(Q):
+                    tiles = gather_tiles([half_v[x, Q * ry + g] for g in range(Q)])
                     for rz in range(Q):
-                        outs[h][x, Q * ry + rz] = u[rz]
-                        outs[h][HALF + x, Q * ry + rz] = e[rz]
-            return carry
-
-        lax.fori_loop(0, once, planes, 0)
+                        outs[h][x, Q * ry + rz] = tiles[rz]
+            return 0
+
+        lax.fori_loop(0, HALF // 2, first_pass, 0)
+        lax.fori_loop(0, HALF, second_pass, 0)
 
 
 def own_part(start, regions, resistivity):
@@ -187,6 +193,7 @@
         scratch_shapes=[
             pltpu.VMEM((2, HALF, NY, NZ), jnp.float32),
             pltpu.VMEM((2, HALF, NY, NZ), jnp.int32),
+            pltpu.VMEM((2 * HALF, PARTS, 8, NZ), jnp.float32),
             pltpu.SMEM((REGIONS,), jnp.float32),
             pltpu.SemaphoreType.DMA((5,)),
         ],
@@ -357,18 +364,24 @@
 
     lax.fori_loop(0, 2, natural, 0)
 
-    def spread(x, _):
-        for j in range(SLICES):
-            for c in range(3):
-                strip = ORDER[j] + c - 1
-                if 0 <= strip < SLICES:
-                    tile = s_ref[x, strip * ROWS : (strip + 1) * ROWS, :]
-                else:
-                    tile = jnp.zeros((ROWS, NZ), jnp.float32)
-                out[j, x, c * ROWS : (c + 1) * ROWS, :] = tile
-        return 0
-
-    lax.fori_loop(0, BX, spread, 0)
+    row = lax.broadcasted_iota(jnp.int32, (ROWS, NZ), 0)
+    for j in range(SLICES):
+
+        def tile(x, c, j=j):
+            strip = ORDER[j] + c - 1
+            if 0 <= strip < SLICES:
+                return s_ref[x, strip * ROWS : (strip + 1) * ROWS, :]
+            return jnp.zeros((ROWS, NZ), jnp.float32)
+
+        low_end, high_end = tile(BX - 1, 0), tile(BX - 1, 2)
+        for x in range(BX):
+            out[j, x] = tile(x, 1)
+        for x in range(BX - 1):
+            shift = BX - 1 - x
+            low = pltpu.roll(low_end, shift, 0) if shift else low_end
+            high = pltpu.roll(high_end, shift, 0) if shift else high_end
+            out[j, BX + x] = jnp.where(row == 0, low, tile(x, 0))
+            out[j, 2 * BX - 1 + x] = jnp.where(row == ROWS - 1, high, tile(x, 2))
 
 
 GRID = jax.ShapeDtypeStruct((3 * BX + 1, PARTS, 8, NZ), jnp.float32)
@@ -398,7 +411,7 @@
     f32 = jnp.float32
     return pl.pallas_call(
         outer_kernel,
-        out_shape=(jax.ShapeDtypeStruct((SLICES, BX, EXT, NZ), f32), GRID, GRID, GRID),
+        out_shape=(jax.ShapeDtypeStruct((SLICES, LOAD, ROWS, NZ), f32), GRID, GRID, GRID),
         in_specs=[VMEM] * 7,
         out_specs=(VMEM,) * 4,
         scratch_shapes=[pltpu.VMEM((PARTS, 8, NZ), f32), pltpu.VMEM((BX, NY, NZ), f32)],
@@ -408,20 +421,37 @@
     )(low, high, u, k, e, g, save)[0]
 
 
-def pack_kernel(sent, down, up):
+def own_tile(sent, ends, i, x, c):
+    if c == 1:
+        return sent[i, x]
+    if x == BX - 1:
+        return ends[i, c // 2]
+    return sent[i, (BX if c == 0 else 2 * BX - 1) + x]
+
+
+def pack_kernel(sent, down, up, ends):
     row = lax.broadcasted_iota(jnp.int32, (ROWS, NZ), 0)
 
-    def tile(i, x, c):
-        return sent[i, x, c * ROWS : (c + 1) * ROWS, :]
-
+    def rebuild(i, _):
+        low, high = sent[i, 2 * BX - 2], sent[i, 3 * BX - 3]
+        low = pltpu.roll(low, BX - 1, 0)
+        for x in range(BX - 1):
+            low = jnp.where(row == x + 1, pltpu.roll(sent[i, BX + x], x + 1, 0), low)
+            high = jnp.where(row == x, pltpu.roll(sent[i, 2 * BX - 1 + x], (x + 1) % 8, 0), high)
+        ends[i, 0] = low
+        ends[i, 1] = high
+        return 0
+
+    lax.fori_loop(0, SLICES, rebuild, 0, unroll=4)
     for n, (i, d, kind) in enumerate(TILES):
         for ref, x in ((down, d - 1), (up, BX - d)):
             if kind == "mid":
-                value = tile(i, x, 1)
+                value = own_tile(sent, ends, i, x, 1)
             elif kind == "both":
-                value = jnp.where(row < 4, tile(i, x, 2), tile(i, x, 0))
+                high, low = own_tile(sent, ends, i, x, 2), own_tile(sent, ends, i, x, 0)
+                value = jnp.where(row < 4, high, low)
             else:
-                value = tile(i, x, 0 if kind == "low" else 2)
+                value = own_tile(sent, ends, i, x, 0 if kind == "low" else 2)
             ref[n] = value
 
 
@@ -429,9 +459,9 @@
     shape = jax.ShapeDtypeStruct((len(TILES), ROWS, NZ), jnp.float32)
     return pl.pallas_call(
         pack_kernel,
-        out_shape=(shape, shape),
+        out_shape=(shape, shape, jax.ShapeDtypeStruct((SLICES, 2, ROWS, NZ), jnp.float32)),
         in_specs=[VMEM],
-        out_specs=(VMEM, VMEM),
+        out_specs=(VMEM,) * 3,
         compiler_params=pltpu.CompilerParams(vmem_limit_bytes=8 << 20),
         name="pack",
     )(sent)
@@ -471,12 +501,12 @@
 
 
 def sent_tile(refs, i, x, c):
-    sent, below, above = refs
+    sent, ends, below, above = refs
     if x < BX:
         return below[PLACE[i, BX - x, c]]
     if x >= 2 * BX:
         return above[PLACE[i, x - 2 * BX + 1, c]]
-    return sent[i, x - BX, c * ROWS : (c + 1) * ROWS, :]
+    return own_tile(sent, ends, i, x - BX, c)
 
 
 def coarse_steps(count, base, eta, refs, u_ref, k_ref, f_ref, out):
@@ -558,8 +588,8 @@
             stretch(n, left, planes[a : a + size])
 
 
-def first_kernel(eta, sent, below, above, out, u_ref, k_ref, f_ref):
-    refs = (sent, below, above)
+def first_kernel(eta, sent, ends, below, above, out, u_ref, k_ref, f_ref):
+    refs = (sent, ends, below, above)
     for x in range(BX - FIRST, 2 * BX + FIRST):
         for c in range(3):
             if BX <= x < 2 * BX or c == 1 or max(BX - x, x - 2 * BX + 1) < FIRST:
@@ -567,7 +597,7 @@
             else:
                 u_ref[x, c] = jnp.zeros((8, NZ), jnp.float32)
     for x in range(BX):
-        out[0, x] = sent[0, x, ROWS : 2 * ROWS, :]
+        out[0, x] = sent[0, x]
 
     def put(n, x, value):
         out[n, x] = value
@@ -575,7 +605,9 @@
     coarse_steps(FIRST, 0, eta, refs, u_ref, k_ref, f_ref, put)
 
 
-def second_kernel(eta, sent, below, above, low_u, own_u, high_u, done, out, u_ref, k_ref, f_ref):
+def second_kernel(
+    eta, sent, ends, below, above, low_u, own_u, high_u, done, out, u_ref, k_ref, f_ref
+):
     odd = is_mirrored()
 
     def true_plane(x):
@@ -589,7 +621,7 @@
     for i in range(FIRST + 1):
         for x in range(BX):
             out[i, true_plane(x)] = done[i, x]
-    refs = (sent, below, above)
+    refs = (sent, ends, below, above)
 
     def put(n, x, value):
         out[FIRST + n, true_plane(x)] = value
@@ -667,14 +699,14 @@
     low_far, high_far = across(own_b), beside(own_a)
     sent = outer(low_far, high_far, *inner(low_near, own_a, own_b, high_near))
     sent = lax.all_to_all(sent, "tm", 0, 0)
-    down, up = pack(sent)
+    down, up, ends = pack(sent)
     below, above = across(down), beside(up)
     eta = strip_part(low_far, low_near, own_a, own_b, high_near, high_far)
-    done = coarse_call(first_kernel, "first", FIRST + 1, eta, sent, below, above)
+    done = coarse_call(first_kernel, "first", FIRST + 1, eta, sent, ends, below, above)
     strip = with_strips(done[FIRST])
     x_low, x_high = across(strip), beside(strip)
     ends = coarse_call(
-        second_kernel, "second", SLICES, eta, sent, below, above, x_low, strip, x_high, done
+        second_kernel, "second", SLICES, eta, sent, ends, below, above, x_low, strip, x_high, done
     )
     result = lax.all_to_all(ends, "tm", 0, 0)
     return place(result)[None]

time: 107 us -> 104 us (0.972)
  Pallas kernels: 23.8 us -> 22.1 us
  blocking collectives: 48.3 us -> 46.7 us
    pallas_call x1, Pallas kernels: 4.49 us -> 2.72 us  [own_part(): pl.pallas_call(own_kernel, out_shape=(shape, shape), in_specs=[hbm] * 3,...]
    all_to_all x1, blocking collectives: 30.9 us -> 29.5 us  [per_device(): sent = lax.all_to_all(sent, 'tm', 0, 0)]
where the time goes in v7:
time: 104 us
  blocking collectives  46.7 us (45%)
  starting transfers between devices  29.3 us (28%)
  Pallas kernels  22.1 us (21%)
  waiting for transfers between devices  5.34 us (5%)
    all_to_all x1, blocking collectives, per_device(): sent = lax.all_to_all(sent, 'tm', 0, 0)  29.5 us
    all_to_all x1, blocking collectives, per_device(): result = lax.all_to_all(ends, 'tm', 0, 0)  17.2 us
    ppermute x4, starting transfers between devices, beside(): return lax.ppermute(value, 'space', pairs + [(b, a) for a, b in pairs])  16.6 us
    ppermute x4, starting transfers between devices, across(): return lax.ppermute(value, 'space', pairs + [(b, a) for a, b in pairs])  7.68 us
    pallas_call x1, Pallas kernels, outer(): pl.pallas_call(outer_kernel, out_shape=(jax.ShapeDtypeStruct((SLICES, LOA...  6.68 us
    pallas_call x2, Pallas kernels, coarse_call(): pl.pallas_call(kernel, out_shape=jax.ShapeDtypeStruct((count, BX, ROWS, N...  5.16 us
    ppermute x2, starting transfers between devices, with_strips(): sides.append(lax.ppermute(state, 'tm', pairs + [(b, a) for a, b in pairs]))  4.97 us
    pallas_call x1, Pallas kernels, inner(): pl.pallas_call(inner_kernel, out_shape=(GRID, GRID, GRID, jax.ShapeDtypeS...  3.77 us
  transfers between devices with their start and end apart: 10, of which 4 were waited for; matrix products, arithmetic and copies ran while one was open for 0% of the time, Pallas kernels for 6%

profile of v7, /device:TPU:96, one launch (start us, length us, event | category | flops | bytes accessed | tf_op | source)
XLA Modules:
  0.0 103.7 jit_solution(3202170311016466375)
XLA Ops:
  0.0 2.7 %own.1 = (f32[8,16,8,128]{3,2,1,0:T(8,128)S(1)}, f32[8,16,8,128]{3,2,1,0:T(8,128)S(1)}) custom-call(f32[8,128,128]{2,1,0:T(8,128)} %bitcast.4, s32[8,128,128]{2,1,0:T(8,128)} %regions.1, f32[4]{0:T(128)} %resistivity.1), custom_call_target="tpu_custom_call" | custom-call | tf_op jit(solution)/shard_map/own/pallas_call | solution.py:188
  2.7 1.9 %collective-permute-start.1 = (f32[8,16,8,128]{3,2,1,0:T(8,128)S(1)}, f32[8,16,8,128]{3,2,1,0:T(8,128)S(1)}, u32[]{:S(2)}, u32[]{:S(2)}) collective-permute-start(f32[8,16,8,128]{3,2,1,0:T(8,128)S(1)} %get-tuple-element.17.refs_2_.own_a), channel_id=1, source_target_pairs={{1,2},{3,4},{5,6},{7,8},{9,10},{11,12},{13,14},{15,16},{17,18},{19... | collective-permute-start | bytes 1572872 | tf_op jit(solution)/shard_map/ppermute | solution.py:677
  4.7 5.1 %collective-permute-start.2 = (f32[8,16,8,128]{3,2,1,0:T(8,128)S(1)}, f32[8,16,8,128]{3,2,1,0:T(8,128)S(1)}, u32[]{:S(2)}, u32[]{:S(2)}) collective-permute-start(f32[8,16,8,128]{3,2,1,0:T(8,128)S(1)} %get-tuple-element.16.refs_3_.own_b), channel_id=1, source_target_pairs={{0,1},{2,3},{4,5},{6,7},{8,9},{10,11},{12,13},{14,15},{16,17},{18,... | collective-permute-start | bytes 1572872 | tf_op jit(solution)/shard_map/ppermute | solution.py:682
  9.8 1.9 %collective-permute-start = (f32[8,16,8,128]{3,2,1,0:T(8,128)S(1)}, f32[8,16,8,128]{3,2,1,0:T(8,128)S(1)}, u32[]{:S(2)}, u32[]{:S(2)}) collective-permute-start(f32[8,16,8,128]{3,2,1,0:T(8,128)S(1)} %get-tuple-element.16.refs_3_.own_b), channel_id=1, source_target_pairs={{1,2},{3,4},{5,6},{7,8},{9,10},{11,12},{13,14},{15,16},{17,18},{19... | collective-permute-start | bytes 1572872 | tf_op jit(solution)/shard_map/ppermute | solution.py:677
  11.7 3.9 %collective-permute-start.3 = (f32[8,16,8,128]{3,2,1,0:T(8,128)S(1)}, f32[8,16,8,128]{3,2,1,0:T(8,128)S(1)}, u32[]{:S(2)}, u32[]{:S(2)}) collective-permute-start(f32[8,16,8,128]{3,2,1,0:T(8,128)S(1)} %get-tuple-element.17.refs_2_.own_a), channel_id=1, source_target_pairs={{0,1},{2,3},{4,5},{6,7},{8,9},{10,11},{12,13},{14,15},{16,17},{18,... | collective-permute-start | bytes 1572872 | tf_op jit(solution)/shard_map/ppermute | solution.py:682
  15.7 0.0 collective-permute-done.1.refs_1_.low
  15.7 0.0 collective-permute-done.2.refs_4_.high
  15.7 3.8 %inner.1 = (f32[25,16,8,128]{3,2,1,0:T(8,128)S(1)}, f32[25,16,8,128]{3,2,1,0:T(8,128)S(1)}, f32[25,16,8,128]{3,2,1,0:T(8,128)S(1)}, f32[16,16,8,128]{3,2,1,0:T(8,128)S(1)}, f32[4,5,16,8,128]{4,3,2,1,0:T(8,128)S(1)}) custom-call(f32[8,16,8,128]{3,2,1,0:T(8,128)S(1)} %collective-permute-done.1.refs_1_.low, ...), custom_call_target="tpu_custom_call" | custom-call | flops 100000000 | bytes 10000000 | tf_op jit(solution)/shard_map/inner/pallas_call | solution.py:392
  19.5 0.8 collective-permute-done.refs_0_.low
  20.3 0.0 collective-permute-done.3.refs_5_.high
  20.3 6.7 %outer.1 = (f32[16,22,8,128]{3,2,1,0:T(8,128)S(1)}, f32[25,16,8,128]{3,2,1,0:T(8,128)S(1)}, f32[25,16,8,128]{3,2,1,0:T(8,128)S(1)}, f32[25,16,8,128]{3,2,1,0:T(8,128)S(1)}) custom-call(f32[8,16,8,128]{3,2,1,0:T(8,128)S(1)} %collective-permute-done.refs_0_.low, ...), custom_call_target="tpu_custom_call", output_to_operand_aliasing={{1}: (2, {}), {2}: (3, {}), {3}: (4, {})} | custom-call | tf_op jit(solution)/shard_map/outer/pallas_call | solution.py:412
  27.0 29.5 %all_to_all.10.sent = f32[16,22,8,128]{3,2,1,0:T(8,128)S(1)} all-to-all(f32[16,22,8,128]{3,2,1,0:T(8,128)S(1)} %get-tuple-element.23), channel_id=1, replica_groups=mesh['tm'=16,'space'=32] {'tm'}, dimensions={0} | all-to-all | bytes 2883584 | tf_op jit(solution)/shard_map/all_to_all | solution.py:701
  56.5 0.1 pack.1
  56.7 1.9 %collective-permute-start.4 = (f32[104,8,128]{2,1,0:T(8,128)S(1)}, f32[104,8,128]{2,1,0:T(8,128)S(1)}, u32[]{:S(2)}, u32[]{:S(2)}) collective-permute-start(f32[104,8,128]{2,1,0:T(8,128)S(1)} %get-tuple-element.25), channel_id=1, source_target_pairs={{1,2},{3,4},{5,6},{7,8},{9,10},{11,12},{13,14},{15,16},{17,18},{19... | collective-permute-start | bytes 1277960 | tf_op jit(solution)/shard_map/ppermute | solution.py:677
  58.6 3.1 %collective-permute-start.5 = (f32[104,8,128]{2,1,0:T(8,128)S(1)}, f32[104,8,128]{2,1,0:T(8,128)S(1)}, u32[]{:S(2)}, u32[]{:S(2)}) collective-permute-start(f32[104,8,128]{2,1,0:T(8,128)S(1)} %get-tuple-element.26), channel_id=1, source_target_pairs={{0,1},{2,3},{4,5},{6,7},{8,9},{10,11},{12,13},{14,15},{16,17},{18,... | collective-permute-start | bytes 1277960 | tf_op jit(solution)/shard_map/ppermute | solution.py:682
  61.7 2.8 %strip.1.eta = f32[24,3,8,128]{3,2,1,0:T(8,128)S(1)} custom-call(f32[8,16,8,128]{3,2,1,0:T(8,128)S(1)} %collective-permute-done.refs_0_.low, f32[8,16,8,128]{3,2,1,0:T(8,128)S(1)} %collective-permute-done.1.refs_1_.low, f32[8,16,8,128]{3,2,1,0:T(8,128)S(1)} %get-tuple-element.17.refs_2_.own_a, f32[8,16,8,128]{3,2,1,0:T(8,128)S(1)} %get-tuple-element.16.refs_3_.own_b, ...), custom_call_target="tpu_custom_call" | custom-call | flops 1000000 | bytes 1000000 | tf_op jit(solution)/shard_map/strip/pallas_call | solution.py:491
  64.4 1.7 %collective-permute-done.4.below = f32[104,8,128]{2,1,0:T(8,128)S(1)} collective-permute-done((f32[104,8,128]{2,1,0:T(8,128)S(1)}, f32[104,8,128]{2,1,0:T(8,128)S(1)}, u32[]{:S(2)}, u32[]{:S(2)}) %collective-permute-start.4) | collective-permute-done | bytes 426016 | tf_op jit(solution)/shard_map/ppermute | solution.py:677
  66.1 0.0 collective-permute-done.5.above
  66.1 2.4 %first.1.done = f32[8,8,8,128]{3,2,1,0:T(8,128)S(1)} custom-call(f32[24,3,8,128]{3,2,1,0:T(8,128)S(1)} %strip.1.eta, f32[16,22,8,128]{3,2,1,0:T(8,128)S(1)} %all_to_all.10.sent, f32[16,2,8,128]{3,2,1,0:T(8,128)S(1)} %get-tuple-element.24.ends, f32[104,8,128]{2,1,0:T(8,128)S(1)} %collective-permute-done.4.below, f32[104,8,128]{2,1,0:T(8,128)S(1)} %collective-permute-done.5.above), custom_call_target="tpu_custom_call" | custom-call | tf_op jit(solution)/shard_map/first/pallas_call | solution.py:634
  68.5 0.7 collective-permute-start.6
  69.2 4.3 %collective-permute-start.7 = (f32[8,8,128]{2,1,0:T(8,128)S(1)}, f32[8,8,128]{2,1,0:T(8,128)S(1)}, u32[]{:S(2)}, u32[]{:S(2)}) collective-permute-start(f32[8,8,128]{2,1,0:T(8,128)S(1)} %slice_bitcast_fusion), channel_id=1, source_target_pairs={{0,32},{64,96},{224,192},{160,128},{256,288},{320,352},{480,448},{... | collective-permute-start | bytes 98312 | tf_op jit(solution)/shard_map/ppermute | solution.py:689
  73.5 0.0 collective-permute-done.6
  73.5 1.9 %collective-permute-done.7 = f32[8,8,128]{2,1,0:T(8,128)S(1)} collective-permute-done((f32[8,8,128]{2,1,0:T(8,128)S(1)}, f32[8,8,128]{2,1,0:T(8,128)S(1)}, u32[]{:S(2)}, u32[]{:S(2)}) %collective-permute-start.7) | collective-permute-done | bytes 32800 | tf_op jit(solution)/shard_map/ppermute | solution.py:689
  75.4 1.9 %collective-permute-start.8 = (f32[8,24,128]{2,1,0:T(8,128)S(1)}, f32[8,24,128]{2,1,0:T(8,128)S(1)}, u32[]{:S(2)}, u32[]{:S(2)}) collective-permute-start(f32[8,24,128]{2,1,0:T(8,128)S(1)} %pad_maximum_fusion.own_u), channel_id=1, source_target_pairs={{1,2},{3,4},{5,6},{7,8},{9,10},{11,12},{13,14},{15,16},{17,18},{19... | collective-permute-start | bytes 294920 | tf_op jit(solution)/shard_map/ppermute | solution.py:677
  77.4 4.5 %collective-permute-start.9 = (f32[8,24,128]{2,1,0:T(8,128)S(1)}, f32[8,24,128]{2,1,0:T(8,128)S(1)}, u32[]{:S(2)}, u32[]{:S(2)}) collective-permute-start(f32[8,24,128]{2,1,0:T(8,128)S(1)} %pad_maximum_fusion.own_u), channel_id=1, source_target_pairs={{0,1},{2,3},{4,5},{6,7},{8,9},{10,11},{12,13},{14,15},{16,17},{18,... | collective-permute-start | bytes 294920 | tf_op jit(solution)/shard_map/ppermute | solution.py:682
  81.8 0.0 collective-permute-done.8.low_u
  81.9 0.9 collective-permute-done.9.high_u
  82.8 2.8 %second.1 = f32[16,8,8,128]{3,2,1,0:T(8,128)S(1)} custom-call(f32[24,3,8,128]{3,2,1,0:T(8,128)S(1)} %strip.1.eta, f32[16,22,8,128]{3,2,1,0:T(8,128)S(1)} %all_to_all.10.sent, f32[16,2,8,128]{3,2,1,0:T(8,128)S(1)} %get-tuple-element.24.ends, f32[104,8,128]{2,1,0:T(8,128)S(1)} %collective-permute-done.4.below, ...), custom_call_target="tpu_custom_call" | custom-call | tf_op jit(solution)/shard_map/second/pallas_call | solution.py:634
  85.6 17.2 %all_to_all.11.strips = f32[16,8,8,128]{3,2,1,0:T(8,128)S(1)} all-to-all(f32[16,8,8,128]{3,2,1,0:T(8,128)S(1)} %second.1), channel_id=1, replica_groups=mesh['tm'=16,'space'=32] {'tm'}, dimensions={0} | all-to-all | bytes 1048576 | tf_op jit(solution)/shard_map/all_to_all | solution.py:711
  102.7 0.9 place.1
  (3 shorter events, 0.0 us)
Async XLA Ops:
  2.7 12.9 %collective-permute-start.1 = (f32[8,16,8,128]{3,2,1,0:T(8,128)S(1)}, f32[8,16,8,128]{3,2,1,0:T(8,128)S(1)}, u32[]{:S(2)}, u32[]{:S(2)}) collective-permute-start(f32[8,16,8,128]{3,2,1,0:T(8,128)S(1)} %get-tuple-element.17.refs_2_.own_a), channel_id=1, source_target_pairs={{1,2},{3,4},{5,6},{7,8},{9,10},{11,12},{13,14},{15,16},{17,18},{19... | collective-permute-start | bytes 1572872 | tf_op jit(solution)/shard_map/ppermute | solution.py:677
  4.7 11.0 %collective-permute-start.2 = (f32[8,16,8,128]{3,2,1,0:T(8,128)S(1)}, f32[8,16,8,128]{3,2,1,0:T(8,128)S(1)}, u32[]{:S(2)}, u32[]{:S(2)}) collective-permute-start(f32[8,16,8,128]{3,2,1,0:T(8,128)S(1)} %get-tuple-element.16.refs_3_.own_b), channel_id=1, source_target_pairs={{0,1},{2,3},{4,5},{6,7},{8,9},{10,11},{12,13},{14,15},{16,17},{18,... | collective-permute-start | bytes 1572872 | tf_op jit(solution)/shard_map/ppermute | solution.py:682
  9.8 10.5 %collective-permute-start = (f32[8,16,8,128]{3,2,1,0:T(8,128)S(1)}, f32[8,16,8,128]{3,2,1,0:T(8,128)S(1)}, u32[]{:S(2)}, u32[]{:S(2)}) collective-permute-start(f32[8,16,8,128]{3,2,1,0:T(8,128)S(1)} %get-tuple-element.16.refs_3_.own_b), channel_id=1, source_target_pairs={{1,2},{3,4},{5,6},{7,8},{9,10},{11,12},{13,14},{15,16},{17,18},{19... | collective-permute-start | bytes 1572872 | tf_op jit(solution)/shard_map/ppermute | solution.py:677
  11.7 8.6 %collective-permute-start.3 = (f32[8,16,8,128]{3,2,1,0:T(8,128)S(1)}, f32[8,16,8,128]{3,2,1,0:T(8,128)S(1)}, u32[]{:S(2)}, u32[]{:S(2)}) collective-permute-start(f32[8,16,8,128]{3,2,1,0:T(8,128)S(1)} %get-tuple-element.17.refs_2_.own_a), channel_id=1, source_target_pairs={{0,1},{2,3},{4,5},{6,7},{8,9},{10,11},{12,13},{14,15},{16,17},{18,... | collective-permute-start | bytes 1572872 | tf_op jit(solution)/shard_map/ppermute | solution.py:682
  56.7 9.4 %collective-permute-start.4 = (f32[104,8,128]{2,1,0:T(8,128)S(1)}, f32[104,8,128]{2,1,0:T(8,128)S(1)}, u32[]{:S(2)}, u32[]{:S(2)}) collective-permute-start(f32[104,8,128]{2,1,0:T(8,128)S(1)} %get-tuple-element.25), channel_id=1, source_target_pairs={{1,2},{3,4},{5,6},{7,8},{9,10},{11,12},{13,14},{15,16},{17,18},{19... | collective-permute-start | bytes 1277960 | tf_op jit(solution)/shard_map/ppermute | solution.py:677
  58.6 7.5 %collective-permute-start.5 = (f32[104,8,128]{2,1,0:T(8,128)S(1)}, f32[104,8,128]{2,1,0:T(8,128)S(1)}, u32[]{:S(2)}, u32[]{:S(2)}) collective-permute-start(f32[104,8,128]{2,1,0:T(8,128)S(1)} %get-tuple-element.26), channel_id=1, source_target_pairs={{0,1},{2,3},{4,5},{6,7},{8,9},{10,11},{12,13},{14,15},{16,17},{18,... | collective-permute-start | bytes 1277960 | tf_op jit(solution)/shard_map/ppermute | solution.py:682
  68.5 5.0 %collective-permute-start.6 = (f32[8,8,128]{2,1,0:T(8,128)S(1)}, f32[8,8,128]{2,1,0:T(8,128)S(1)}, u32[]{:S(2)}, u32[]{:S(2)}) collective-permute-start(f32[8,8,128]{2,1,0:T(8,128)S(1)} %slice_bitcast_fusion), channel_id=1, source_target_pairs={{32,64},{96,224},{192,160},{128,256},{288,320},{352,480},{448,416}... | collective-permute-start | bytes 98312 | tf_op jit(solution)/shard_map/ppermute | solution.py:689
  69.2 6.2 %collective-permute-start.7 = (f32[8,8,128]{2,1,0:T(8,128)S(1)}, f32[8,8,128]{2,1,0:T(8,128)S(1)}, u32[]{:S(2)}, u32[]{:S(2)}) collective-permute-start(f32[8,8,128]{2,1,0:T(8,128)S(1)} %slice_bitcast_fusion), channel_id=1, source_target_pairs={{0,32},{64,96},{224,192},{160,128},{256,288},{320,352},{480,448},{... | collective-permute-start | bytes 98312 | tf_op jit(solution)/shard_map/ppermute | solution.py:689
  75.4 6.4 %collective-permute-start.8 = (f32[8,24,128]{2,1,0:T(8,128)S(1)}, f32[8,24,128]{2,1,0:T(8,128)S(1)}, u32[]{:S(2)}, u32[]{:S(2)}) collective-permute-start(f32[8,24,128]{2,1,0:T(8,128)S(1)} %pad_maximum_fusion.own_u), channel_id=1, source_target_pairs={{1,2},{3,4},{5,6},{7,8},{9,10},{11,12},{13,14},{15,16},{17,18},{19... | collective-permute-start | bytes 294920 | tf_op jit(solution)/shard_map/ppermute | solution.py:677
  77.4 5.4 %collective-permute-start.9 = (f32[8,24,128]{2,1,0:T(8,128)S(1)}, f32[8,24,128]{2,1,0:T(8,128)S(1)}, u32[]{:S(2)}, u32[]{:S(2)}) collective-permute-start(f32[8,24,128]{2,1,0:T(8,128)S(1)} %pad_maximum_fusion.own_u), channel_id=1, source_target_pairs={{0,1},{2,3},{4,5},{6,7},{8,9},{10,11},{12,13},{14,15},{16,17},{18,... | collective-permute-start | bytes 294920 | tf_op jit(solution)/shard_map/ppermute | solution.py:682

commit v8 on v7

--- a/solution.py
+++ b/solution.py
@@ -29,25 +29,32 @@
 
 
 def packed_tiles():
-    tiles = []
+    tiles, groups = [], []
     for i in range(SLICES):
         depth = halo_depth(i)
         for d in range(1, depth + 1):
-            tiles.append((i, d, "mid"))
-            beyond = depth - d
-            if 1 <= beyond <= 4:
-                tiles.append((i, d, "both"))
-            elif beyond > 4:
-                tiles.append((i, d, "low"))
-                tiles.append((i, d, "high"))
-    return tiles
+            tiles.append([(i, d, 1, ROWS, 0)])
+            if depth > d:
+                groups += [(depth - d, i, d, 0), (depth - d, i, d, 2)]
+    used = []
+    for rows, i, d, part in sorted(groups, reverse=True):
+        for tile in used:
+            start = sum(entry[3] for entry in tile)
+            if start + rows <= ROWS:
+                break
+        else:
+            tile, start = [], 0
+            used.append(tile)
+        tile.append((i, d, part, rows, start))
+    return tiles + used
 
 
 TILES = packed_tiles()
-PLACE = {}
-for _n, (_i, _d, _kind) in enumerate(TILES):
-    for _c in {"mid": (1,), "both": (0, 2), "low": (0,), "high": (2,)}[_kind]:
-        PLACE[_i, _d, _c] = _n
+PLACE = {
+    (i, d, part): (n, (start if part else start + rows) % ROWS)
+    for n, tile in enumerate(TILES)
+    for i, d, part, rows, start in tile
+}
 PARTS = NY // 8
 LOAD = 3 * BX - 2
 GROUP = 40
@@ -152,12 +159,13 @@
         copies.append(pair)
     small.wait()
     scaled = [resistivity_s[i] * jnp.float32(0.5 * fine_step) for i in range(REGIONS)]
+    once = one_trip()
     for h in range(2):
         for copy in copies[h]:
             copy.wait()
 
-        def first_pass(n, _, h=h):
-            for x in (2 * n, 2 * n + 1):
+        def first_pass(_, carry, h=h):
+            for x in range(HALF):
                 source = jnp.where(odd, HALF - 1 - x, x)
                 for ry in range(Q):
                     for g in range(Q):
@@ -168,18 +176,18 @@
                             value = jnp.where(region == i, scaled[i], value)
                         half_v[x, Q * ry + g] = turn(g, start_v[h, source, where, :])
                         half_v[HALF + x, Q * ry + g] = turn(g, value)
-            return 0
+            return carry
 
         def second_pass(n, _, h=h):
-            for x in (2 * n, 2 * n + 1):
+            for x in [HALF * n + q for q in range(HALF)]:
                 for ry in range(Q):
                     tiles = gather_tiles([half_v[x, Q * ry + g] for g in range(Q)])
                     for rz in range(Q):
                         outs[h][x, Q * ry + rz] = tiles[rz]
             return 0
 
-        lax.fori_loop(0, HALF // 2, first_pass, 0)
-        lax.fori_loop(0, HALF, second_pass, 0)
+        lax.fori_loop(0, once, first_pass, 0)
+        lax.fori_loop(0, 2, second_pass, 0)
 
 
 def own_part(start, regions, resistivity):
@@ -213,16 +221,17 @@
         self.y_start = (sub == 0) & (lane < CHUNK)
 
     def stage(self, ref, base, turn=False):
-        def one(x, _):
-            to = base + (HALF - 1 - x if turn else x)
-            for r in range(PARTS):
-                u, e = ref[x, r], ref[HALF + x, r]
-                self.u[to, r] = u
-                self.e[to, r] = e
-                self.k[to, r] = coeff(e, u)
+        def two(n, _):
+            for x in (2 * n, 2 * n + 1):
+                to = base + (HALF - 1 - x if turn else x)
+                for r in range(PARTS):
+                    u, e = ref[x, r], ref[HALF + x, r]
+                    self.u[to, r] = u
+                    self.e[to, r] = e
+                    self.k[to, r] = coeff(e, u)
             return 0
 
-        lax.fori_loop(0, HALF, one, 0)
+        lax.fori_loop(0, HALF // 2, two, 0)
 
     def above_y(self, v):
         turned = pltpu.roll(pltpu.roll(v, NZ - CHUNK, 1), 7, 0)
@@ -443,15 +452,15 @@
         return 0
 
     lax.fori_loop(0, SLICES, rebuild, 0, unroll=4)
-    for n, (i, d, kind) in enumerate(TILES):
-        for ref, x in ((down, d - 1), (up, BX - d)):
-            if kind == "mid":
-                value = own_tile(sent, ends, i, x, 1)
-            elif kind == "both":
-                high, low = own_tile(sent, ends, i, x, 2), own_tile(sent, ends, i, x, 0)
-                value = jnp.where(row < 4, high, low)
-            else:
-                value = own_tile(sent, ends, i, x, 0 if kind == "low" else 2)
+    for n, tile in enumerate(TILES):
+        for ref, near in ((down, True), (up, False)):
+            value = None
+            for i, d, part, rows, start in tile:
+                part_of = own_tile(sent, ends, i, d - 1 if near else BX - d, part)
+                shift = PLACE[i, d, part][1]
+                if shift:
+                    part_of = pltpu.roll(part_of, shift, 0)
+                value = part_of if value is None else jnp.where(row >= start, part_of, value)
             ref[n] = value
 
 
@@ -502,10 +511,10 @@
 
 def sent_tile(refs, i, x, c):
     sent, ends, below, above = refs
-    if x < BX:
-        return below[PLACE[i, BX - x, c]]
-    if x >= 2 * BX:
-        return above[PLACE[i, x - 2 * BX + 1, c]]
+    if x < BX or x >= 2 * BX:
+        ref, d = (below, BX - x) if x < BX else (above, x - 2 * BX + 1)
+        n, shift = PLACE[i, d, c]
+        return pltpu.roll(ref[n], ROWS - shift, 0) if shift else ref[n]
     return own_tile(sent, ends, i, x - BX, c)
 
 

time: 104 us -> 103 us (level)
  no operation moved by 1% of the time
where the time goes in v8:
time: 103 us; the launch traced here: 102 us
  blocking collectives  46.7 us (45%)
  starting transfers between devices  29.3 us (28%)
  Pallas kernels  21.6 us (21%)
  waiting for transfers between devices  4.52 us (4%)
    all_to_all x1, blocking collectives, per_device(): sent = lax.all_to_all(sent, 'tm', 0, 0)  29.5 us
    all_to_all x1, blocking collectives, per_device(): result = lax.all_to_all(ends, 'tm', 0, 0)  17.2 us
    ppermute x4, starting transfers between devices, beside(): return lax.ppermute(value, 'space', pairs + [(b, a) for a, b in pairs])  16.6 us
    ppermute x4, starting transfers between devices, across(): return lax.ppermute(value, 'space', pairs + [(b, a) for a, b in pairs])  7.68 us
    pallas_call x1, Pallas kernels, outer(): pl.pallas_call(outer_kernel, out_shape=(jax.ShapeDtypeStruct((SLICES, LOA...  6.66 us
    pallas_call x2, Pallas kernels, coarse_call(): pl.pallas_call(kernel, out_shape=jax.ShapeDtypeStruct((count, BX, ROWS, N...  5.15 us
    ppermute x2, starting transfers between devices, with_strips(): sides.append(lax.ppermute(state, 'tm', pairs + [(b, a) for a, b in pairs]))  4.97 us
    pallas_call x1, Pallas kernels, inner(): pl.pallas_call(inner_kernel, out_shape=(GRID, GRID, GRID, jax.ShapeDtypeS...  3.71 us
  transfers between devices with their start and end apart: 10, of which 4 were waited for; matrix products, arithmetic and copies ran while one was open for 0% of the time, Pallas kernels for 6%

profile of v8, /device:TPU:96, one launch (start us, length us, event | category | flops | bytes accessed | tf_op | source)
XLA Modules:
  0.0 102.3 jit_solution(6343274033683746509)
XLA Ops:
  0.0 2.3 %own.1 = (f32[8,16,8,128]{3,2,1,0:T(8,128)S(1)}, f32[8,16,8,128]{3,2,1,0:T(8,128)S(1)}) custom-call(f32[8,128,128]{2,1,0:T(8,128)} %bitcast.4, s32[8,128,128]{2,1,0:T(8,128)} %regions.1, f32[4]{0:T(128)} %resistivity.1), custom_call_target="tpu_custom_call" | custom-call | tf_op jit(solution)/shard_map/own/pallas_call | solution.py:196
  2.3 1.9 %collective-permute-start.1 = (f32[8,16,8,128]{3,2,1,0:T(8,128)S(1)}, f32[8,16,8,128]{3,2,1,0:T(8,128)S(1)}, u32[]{:S(2)}, u32[]{:S(2)}) collective-permute-start(f32[8,16,8,128]{3,2,1,0:T(8,128)S(1)} %get-tuple-element.17.refs_2_.own_a), channel_id=1, source_target_pairs={{1,2},{3,4},{5,6},{7,8},{9,10},{11,12},{13,14},{15,16},{17,18},{19... | collective-permute-start | bytes 1572872 | tf_op jit(solution)/shard_map/ppermute | solution.py:686
  4.2 5.1 %collective-permute-start.2 = (f32[8,16,8,128]{3,2,1,0:T(8,128)S(1)}, f32[8,16,8,128]{3,2,1,0:T(8,128)S(1)}, u32[]{:S(2)}, u32[]{:S(2)}) collective-permute-start(f32[8,16,8,128]{3,2,1,0:T(8,128)S(1)} %get-tuple-element.16.refs_3_.own_b), channel_id=1, source_target_pairs={{0,1},{2,3},{4,5},{6,7},{8,9},{10,11},{12,13},{14,15},{16,17},{18,... | collective-permute-start | bytes 1572872 | tf_op jit(solution)/shard_map/ppermute | solution.py:691
  9.4 1.9 %collective-permute-start = (f32[8,16,8,128]{3,2,1,0:T(8,128)S(1)}, f32[8,16,8,128]{3,2,1,0:T(8,128)S(1)}, u32[]{:S(2)}, u32[]{:S(2)}) collective-permute-start(f32[8,16,8,128]{3,2,1,0:T(8,128)S(1)} %get-tuple-element.16.refs_3_.own_b), channel_id=1, source_target_pairs={{1,2},{3,4},{5,6},{7,8},{9,10},{11,12},{13,14},{15,16},{17,18},{19... | collective-permute-start | bytes 1572872 | tf_op jit(solution)/shard_map/ppermute | solution.py:686
  11.3 3.9 %collective-permute-start.3 = (f32[8,16,8,128]{3,2,1,0:T(8,128)S(1)}, f32[8,16,8,128]{3,2,1,0:T(8,128)S(1)}, u32[]{:S(2)}, u32[]{:S(2)}) collective-permute-start(f32[8,16,8,128]{3,2,1,0:T(8,128)S(1)} %get-tuple-element.17.refs_2_.own_a), channel_id=1, source_target_pairs={{0,1},{2,3},{4,5},{6,7},{8,9},{10,11},{12,13},{14,15},{16,17},{18,... | collective-permute-start | bytes 1572872 | tf_op jit(solution)/shard_map/ppermute | solution.py:691
  15.3 0.0 collective-permute-done.1.refs_1_.low
  15.3 0.0 collective-permute-done.2.refs_4_.high
  15.3 3.7 %inner.1 = (f32[25,16,8,128]{3,2,1,0:T(8,128)S(1)}, f32[25,16,8,128]{3,2,1,0:T(8,128)S(1)}, f32[25,16,8,128]{3,2,1,0:T(8,128)S(1)}, f32[16,16,8,128]{3,2,1,0:T(8,128)S(1)}, f32[4,5,16,8,128]{4,3,2,1,0:T(8,128)S(1)}) custom-call(f32[8,16,8,128]{3,2,1,0:T(8,128)S(1)} %collective-permute-done.1.refs_1_.low, ...), custom_call_target="tpu_custom_call" | custom-call | flops 100000000 | bytes 10000000 | tf_op jit(solution)/shard_map/inner/pallas_call | solution.py:401
  19.0 0.9 collective-permute-done.refs_0_.low
  19.9 0.0 collective-permute-done.3.refs_5_.high
  19.9 6.7 %outer.1 = (f32[16,22,8,128]{3,2,1,0:T(8,128)S(1)}, f32[25,16,8,128]{3,2,1,0:T(8,128)S(1)}, f32[25,16,8,128]{3,2,1,0:T(8,128)S(1)}, f32[25,16,8,128]{3,2,1,0:T(8,128)S(1)}) custom-call(f32[8,16,8,128]{3,2,1,0:T(8,128)S(1)} %collective-permute-done.refs_0_.low, ...), custom_call_target="tpu_custom_call", output_to_operand_aliasing={{1}: (2, {}), {2}: (3, {}), {3}: (4, {})} | custom-call | tf_op jit(solution)/shard_map/outer/pallas_call | solution.py:421
  26.6 29.5 %all_to_all.10.sent = f32[16,22,8,128]{3,2,1,0:T(8,128)S(1)} all-to-all(f32[16,22,8,128]{3,2,1,0:T(8,128)S(1)} %get-tuple-element.23), channel_id=1, replica_groups=mesh['tm'=16,'space'=32] {'tm'}, dimensions={0} | all-to-all | bytes 2883584 | tf_op jit(solution)/shard_map/all_to_all | solution.py:710
  56.1 0.1 pack.1
  56.2 1.9 %collective-permute-start.4 = (f32[84,8,128]{2,1,0:T(8,128)S(1)}, f32[84,8,128]{2,1,0:T(8,128)S(1)}, u32[]{:S(2)}, u32[]{:S(2)}) collective-permute-start(f32[84,8,128]{2,1,0:T(8,128)S(1)} %get-tuple-element.25), channel_id=1, source_target_pairs={{1,2},{3,4},{5,6},{7,8},{9,10},{11,12},{13,14},{15,16},{17,18},{19... | collective-permute-start | bytes 1032200 | tf_op jit(solution)/shard_map/ppermute | solution.py:686
  58.2 3.1 %collective-permute-start.5 = (f32[84,8,128]{2,1,0:T(8,128)S(1)}, f32[84,8,128]{2,1,0:T(8,128)S(1)}, u32[]{:S(2)}, u32[]{:S(2)}) collective-permute-start(f32[84,8,128]{2,1,0:T(8,128)S(1)} %get-tuple-element.26), channel_id=1, source_target_pairs={{0,1},{2,3},{4,5},{6,7},{8,9},{10,11},{12,13},{14,15},{16,17},{18,... | collective-permute-start | bytes 1032200 | tf_op jit(solution)/shard_map/ppermute | solution.py:691
  61.2 2.8 %strip.1.eta = f32[24,3,8,128]{3,2,1,0:T(8,128)S(1)} custom-call(f32[8,16,8,128]{3,2,1,0:T(8,128)S(1)} %collective-permute-done.refs_0_.low, f32[8,16,8,128]{3,2,1,0:T(8,128)S(1)} %collective-permute-done.1.refs_1_.low, f32[8,16,8,128]{3,2,1,0:T(8,128)S(1)} %get-tuple-element.17.refs_2_.own_a, f32[8,16,8,128]{3,2,1,0:T(8,128)S(1)} %get-tuple-element.16.refs_3_.own_b, ...), custom_call_target="tpu_custom_call" | custom-call | flops 1000000 | bytes 1000000 | tf_op jit(solution)/shard_map/strip/pallas_call | solution.py:500
  64.0 0.8 collective-permute-done.4.below
  64.8 0.0 collective-permute-done.5.above
  64.8 2.3 %first.1.done = f32[8,8,8,128]{3,2,1,0:T(8,128)S(1)} custom-call(f32[24,3,8,128]{3,2,1,0:T(8,128)S(1)} %strip.1.eta, f32[16,22,8,128]{3,2,1,0:T(8,128)S(1)} %all_to_all.10.sent, f32[16,2,8,128]{3,2,1,0:T(8,128)S(1)} %get-tuple-element.24.ends, f32[84,8,128]{2,1,0:T(8,128)S(1)} %collective-permute-done.4.below, f32[84,8,128]{2,1,0:T(8,128)S(1)} %collective-permute-done.5.above), custom_call_target="tpu_custom_call" | custom-call | tf_op jit(solution)/shard_map/first/pallas_call | solution.py:643
  67.2 0.7 collective-permute-start.6
  67.8 4.3 %collective-permute-start.7 = (f32[8,8,128]{2,1,0:T(8,128)S(1)}, f32[8,8,128]{2,1,0:T(8,128)S(1)}, u32[]{:S(2)}, u32[]{:S(2)}) collective-permute-start(f32[8,8,128]{2,1,0:T(8,128)S(1)} %slice_bitcast_fusion), channel_id=1, source_target_pairs={{0,32},{64,96},{224,192},{160,128},{256,288},{320,352},{480,448},{... | collective-permute-start | bytes 98312 | tf_op jit(solution)/shard_map/ppermute | solution.py:698
  72.2 0.0 collective-permute-done.6
  72.2 1.9 %collective-permute-done.7 = f32[8,8,128]{2,1,0:T(8,128)S(1)} collective-permute-done((f32[8,8,128]{2,1,0:T(8,128)S(1)}, f32[8,8,128]{2,1,0:T(8,128)S(1)}, u32[]{:S(2)}, u32[]{:S(2)}) %collective-permute-start.7) | collective-permute-done | bytes 32800 | tf_op jit(solution)/shard_map/ppermute | solution.py:698
  74.1 1.9 %collective-permute-start.8 = (f32[8,24,128]{2,1,0:T(8,128)S(1)}, f32[8,24,128]{2,1,0:T(8,128)S(1)}, u32[]{:S(2)}, u32[]{:S(2)}) collective-permute-start(f32[8,24,128]{2,1,0:T(8,128)S(1)} %pad_maximum_fusion.own_u), channel_id=1, source_target_pairs={{1,2},{3,4},{5,6},{7,8},{9,10},{11,12},{13,14},{15,16},{17,18},{19... | collective-permute-start | bytes 294920 | tf_op jit(solution)/shard_map/ppermute | solution.py:686
  76.0 4.5 %collective-permute-start.9 = (f32[8,24,128]{2,1,0:T(8,128)S(1)}, f32[8,24,128]{2,1,0:T(8,128)S(1)}, u32[]{:S(2)}, u32[]{:S(2)}) collective-permute-start(f32[8,24,128]{2,1,0:T(8,128)S(1)} %pad_maximum_fusion.own_u), channel_id=1, source_target_pairs={{0,1},{2,3},{4,5},{6,7},{8,9},{10,11},{12,13},{14,15},{16,17},{18,... | collective-permute-start | bytes 294920 | tf_op jit(solution)/shard_map/ppermute | solution.py:691
  80.5 0.0 collective-permute-done.8.low_u
  80.5 0.9 collective-permute-done.9.high_u
  81.5 2.8 %second.1 = f32[16,8,8,128]{3,2,1,0:T(8,128)S(1)} custom-call(f32[24,3,8,128]{3,2,1,0:T(8,128)S(1)} %strip.1.eta, f32[16,22,8,128]{3,2,1,0:T(8,128)S(1)} %all_to_all.10.sent, f32[16,2,8,128]{3,2,1,0:T(8,128)S(1)} %get-tuple-element.24.ends, f32[84,8,128]{2,1,0:T(8,128)S(1)} %collective-permute-done.4.below, f32[84,8,128]{2,1,0:T(8,128)S(1)} %collective-permute-done.5.above, ...), custom_call_target="tpu_custom_call" | custom-call | tf_op jit(solution)/shard_map/second/pallas_call | solution.py:643
  84.3 17.2 %all_to_all.11.strips = f32[16,8,8,128]{3,2,1,0:T(8,128)S(1)} all-to-all(f32[16,8,8,128]{3,2,1,0:T(8,128)S(1)} %second.1), channel_id=1, replica_groups=mesh['tm'=16,'space'=32] {'tm'}, dimensions={0} | all-to-all | bytes 1048576 | tf_op jit(solution)/shard_map/all_to_all | solution.py:720
  101.4 0.9 place.1
  (3 shorter events, 0.0 us)
Async XLA Ops:
  2.3 12.9 %collective-permute-start.1 = (f32[8,16,8,128]{3,2,1,0:T(8,128)S(1)}, f32[8,16,8,128]{3,2,1,0:T(8,128)S(1)}, u32[]{:S(2)}, u32[]{:S(2)}) collective-permute-start(f32[8,16,8,128]{3,2,1,0:T(8,128)S(1)} %get-tuple-element.17.refs_2_.own_a), channel_id=1, source_target_pairs={{1,2},{3,4},{5,6},{7,8},{9,10},{11,12},{13,14},{15,16},{17,18},{19... | collective-permute-start | bytes 1572872 | tf_op jit(solution)/shard_map/ppermute | solution.py:686
  4.2 11.0 %collective-permute-start.2 = (f32[8,16,8,128]{3,2,1,0:T(8,128)S(1)}, f32[8,16,8,128]{3,2,1,0:T(8,128)S(1)}, u32[]{:S(2)}, u32[]{:S(2)}) collective-permute-start(f32[8,16,8,128]{3,2,1,0:T(8,128)S(1)} %get-tuple-element.16.refs_3_.own_b), channel_id=1, source_target_pairs={{0,1},{2,3},{4,5},{6,7},{8,9},{10,11},{12,13},{14,15},{16,17},{18,... | collective-permute-start | bytes 1572872 | tf_op jit(solution)/shard_map/ppermute | solution.py:691
  9.4 10.5 %collective-permute-start = (f32[8,16,8,128]{3,2,1,0:T(8,128)S(1)}, f32[8,16,8,128]{3,2,1,0:T(8,128)S(1)}, u32[]{:S(2)}, u32[]{:S(2)}) collective-permute-start(f32[8,16,8,128]{3,2,1,0:T(8,128)S(1)} %get-tuple-element.16.refs_3_.own_b), channel_id=1, source_target_pairs={{1,2},{3,4},{5,6},{7,8},{9,10},{11,12},{13,14},{15,16},{17,18},{19... | collective-permute-start | bytes 1572872 | tf_op jit(solution)/shard_map/ppermute | solution.py:686
  11.3 8.6 %collective-permute-start.3 = (f32[8,16,8,128]{3,2,1,0:T(8,128)S(1)}, f32[8,16,8,128]{3,2,1,0:T(8,128)S(1)}, u32[]{:S(2)}, u32[]{:S(2)}) collective-permute-start(f32[8,16,8,128]{3,2,1,0:T(8,128)S(1)} %get-tuple-element.17.refs_2_.own_a), channel_id=1, source_target_pairs={{0,1},{2,3},{4,5},{6,7},{8,9},{10,11},{12,13},{14,15},{16,17},{18,... | collective-permute-start | bytes 1572872 | tf_op jit(solution)/shard_map/ppermute | solution.py:691
  56.2 8.6 %collective-permute-start.4 = (f32[84,8,128]{2,1,0:T(8,128)S(1)}, f32[84,8,128]{2,1,0:T(8,128)S(1)}, u32[]{:S(2)}, u32[]{:S(2)}) collective-permute-start(f32[84,8,128]{2,1,0:T(8,128)S(1)} %get-tuple-element.25), channel_id=1, source_target_pairs={{1,2},{3,4},{5,6},{7,8},{9,10},{11,12},{13,14},{15,16},{17,18},{19... | collective-permute-start | bytes 1032200 | tf_op jit(solution)/shard_map/ppermute | solution.py:686
  58.2 6.6 %collective-permute-start.5 = (f32[84,8,128]{2,1,0:T(8,128)S(1)}, f32[84,8,128]{2,1,0:T(8,128)S(1)}, u32[]{:S(2)}, u32[]{:S(2)}) collective-permute-start(f32[84,8,128]{2,1,0:T(8,128)S(1)} %get-tuple-element.26), channel_id=1, source_target_pairs={{0,1},{2,3},{4,5},{6,7},{8,9},{10,11},{12,13},{14,15},{16,17},{18,... | collective-permute-start | bytes 1032200 | tf_op jit(solution)/shard_map/ppermute | solution.py:691
  67.2 5.0 %collective-permute-start.6 = (f32[8,8,128]{2,1,0:T(8,128)S(1)}, f32[8,8,128]{2,1,0:T(8,128)S(1)}, u32[]{:S(2)}, u32[]{:S(2)}) collective-permute-start(f32[8,8,128]{2,1,0:T(8,128)S(1)} %slice_bitcast_fusion), channel_id=1, source_target_pairs={{32,64},{96,224},{192,160},{128,256},{288,320},{352,480},{448,416}... | collective-permute-start | bytes 98312 | tf_op jit(solution)/shard_map/ppermute | solution.py:698
  67.8 6.2 %collective-permute-start.7 = (f32[8,8,128]{2,1,0:T(8,128)S(1)}, f32[8,8,128]{2,1,0:T(8,128)S(1)}, u32[]{:S(2)}, u32[]{:S(2)}) collective-permute-start(f32[8,8,128]{2,1,0:T(8,128)S(1)} %slice_bitcast_fusion), channel_id=1, source_target_pairs={{0,32},{64,96},{224,192},{160,128},{256,288},{320,352},{480,448},{... | collective-permute-start | bytes 98312 | tf_op jit(solution)/shard_map/ppermute | solution.py:698
  74.1 6.4 %collective-permute-start.8 = (f32[8,24,128]{2,1,0:T(8,128)S(1)}, f32[8,24,128]{2,1,0:T(8,128)S(1)}, u32[]{:S(2)}, u32[]{:S(2)}) collective-permute-start(f32[8,24,128]{2,1,0:T(8,128)S(1)} %pad_maximum_fusion.own_u), channel_id=1, source_target_pairs={{1,2},{3,4},{5,6},{7,8},{9,10},{11,12},{13,14},{15,16},{17,18},{19... | collective-permute-start | bytes 294920 | tf_op jit(solution)/shard_map/ppermute | solution.py:686
  76.0 5.4 %collective-permute-start.9 = (f32[8,24,128]{2,1,0:T(8,128)S(1)}, f32[8,24,128]{2,1,0:T(8,128)S(1)}, u32[]{:S(2)}, u32[]{:S(2)}) collective-permute-start(f32[8,24,128]{2,1,0:T(8,128)S(1)} %pad_maximum_fusion.own_u), channel_id=1, source_target_pairs={{0,1},{2,3},{4,5},{6,7},{8,9},{10,11},{12,13},{14,15},{16,17},{18,... | collective-permute-start | bytes 294920 | tf_op jit(solution)/shard_map/ppermute | solution.py:691

commit v9 on v8

--- a/solution.py
+++ b/solution.py
@@ -478,35 +478,42 @@
 
 def strip_kernel(*refs):
     own = strip_of(lax.axis_index("tm"))
-    parts, (out, rows) = refs[:-2], refs[-2:]
-    for n, ref in enumerate(parts):
-
-        def natural(m, _, n=n, ref=ref):
-            for x in (2 * m, 2 * m + 1):
-                to = HALF - 1 - x if n in (0, 1, 4, 5) else x
-                to_rows(ref.at[HALF + x], rows.at[n * HALF + to])
-            return 0
-
-        lax.fori_loop(0, HALF // 2, natural, 0)
+    parts, out = refs[:-1], refs[-1]
+    lane, _ = iotas()
     for c in range(3):
         strip = own + (c - 1)
         scale = jnp.where((strip >= 0) & (strip < SLICES), float(STEPS), 0.0).astype(jnp.float32)
-        start = pl.multiple_of(jnp.clip(strip, 0, SLICES - 1) * ROWS, ROWS)
-        for x in range(3 * BX):
-            out[x, c] = scale * rows[x, pl.ds(start, ROWS), :]
+        strip = jnp.clip(strip, 0, SLICES - 1)
+        h, s0 = lax.div(strip, Q), 2 * lax.rem(strip, Q)
+        source = CHUNK * h + (lane >> 2)
+        for n, ref in enumerate(parts):
+            for x in range(HALF):
+                turned = []
+                for rz in range(Q):
+                    halves = [
+                        ref[HALF + x, pl.ds(8 * rz + s0 + ds, Q, stride=8 * Q), :]
+                        for ds in range(2)
+                    ]
+                    both = jnp.concatenate(halves, axis=0)
+                    turned.append(jnp.take_along_axis(both, source, axis=1))
+                low = jnp.where((lane & 3) == 0, turned[0], turned[1])
+                high = jnp.where((lane & 3) == 2, turned[2], turned[3])
+                value = jnp.where((lane & 3) < 2, low, high)
+                to = HALF - 1 - x if n in (0, 1, 4, 5) else x
+                out[n * HALF + to, c] = scale * value
 
 
 def strip_part(*parts):
+    flat = [a.reshape(2 * HALF, NY, NZ) for a in parts]
     return pl.pallas_call(
         strip_kernel,
         out_shape=jax.ShapeDtypeStruct((3 * BX, 3, 8, NZ), jnp.float32),
         in_specs=[VMEM] * len(parts),
         out_specs=VMEM,
-        scratch_shapes=[pltpu.VMEM((3 * BX, NY, NZ), jnp.float32)],
         compiler_params=pltpu.CompilerParams(vmem_limit_bytes=8 << 20),
         cost_estimate=pl.CostEstimate(flops=10**6, bytes_accessed=10**6, transcendentals=0),
         name="strip",
-    )(*parts)
+    )(*flat)
 
 
 def sent_tile(refs, i, x, c):

time: 103 us -> 103 us (level)
  waiting for transfers between devices: 4.52 us -> 6.51 us
  Pallas kernels: 21.6 us -> 19.7 us
    ppermute x4, waiting for transfers between devices: 1.71 us -> 3.7 us  [across(): return lax.ppermute(value, 'space', pairs + [(b, a) for a, b in pairs])]
    pallas_call x1, Pallas kernels: 2.76 us -> 0.78 us  [strip_part(): pl.pallas_call(strip_kernel, out_shape=jax.ShapeDtypeStruct((3 * BX, 3, 8...]
  transfers between devices with their start and end apart: 10 -> 10, of which waited for: 4 -> 4; matrix products, arithmetic and copies ran while one was open for 0% -> 0% of each run, Pallas kernels for 6% -> 4%
where the time goes in v9:
time: 103 us; the launch traced here: 102 us
  blocking collectives  46.7 us (45%)
  starting transfers between devices  29.3 us (28%)
  Pallas kernels  19.7 us (19%)
  waiting for transfers between devices  6.51 us (6%)
    all_to_all x1, blocking collectives, per_device(): sent = lax.all_to_all(sent, 'tm', 0, 0)  29.5 us
    all_to_all x1, blocking collectives, per_device(): result = lax.all_to_all(ends, 'tm', 0, 0)  17.2 us
    ppermute x4, starting transfers between devices, beside(): return lax.ppermute(value, 'space', pairs + [(b, a) for a, b in pairs])  16.6 us
    ppermute x4, starting transfers between devices, across(): return lax.ppermute(value, 'space', pairs + [(b, a) for a, b in pairs])  7.68 us
    pallas_call x1, Pallas kernels, outer(): pl.pallas_call(outer_kernel, out_shape=(jax.ShapeDtypeStruct((SLICES, LOA...  6.66 us
    pallas_call x2, Pallas kernels, coarse_call(): pl.pallas_call(kernel, out_shape=jax.ShapeDtypeStruct((count, BX, ROWS, N...  5.15 us
    ppermute x2, starting transfers between devices, with_strips(): sides.append(lax.ppermute(state, 'tm', pairs + [(b, a) for a, b in pairs]))  4.97 us
    pallas_call x1, Pallas kernels, inner(): pl.pallas_call(inner_kernel, out_shape=(GRID, GRID, GRID, jax.ShapeDtypeS...  3.71 us
  transfers between devices with their start and end apart: 10, of which 4 were waited for; matrix products, arithmetic and copies ran while one was open for 0% of the time, Pallas kernels for 4%

profile of v9, /device:TPU:96, one launch (start us, length us, event | category | flops | bytes accessed | tf_op | source)
XLA Modules:
  0.0 102.3 jit_solution(16568905034850838517)
XLA Ops:
  0.0 2.3 %own.1 = (f32[8,16,8,128]{3,2,1,0:T(8,128)S(1)}, f32[8,16,8,128]{3,2,1,0:T(8,128)S(1)}) custom-call(f32[8,128,128]{2,1,0:T(8,128)} %bitcast.16, s32[8,128,128]{2,1,0:T(8,128)} %regions.1, f32[4]{0:T(128)} %resistivity.1), custom_call_target="tpu_custom_call" | custom-call | tf_op jit(solution)/shard_map/own/pallas_call | solution.py:196
  2.3 1.9 %collective-permute-start.1 = (f32[8,16,8,128]{3,2,1,0:T(8,128)S(1)}, f32[8,16,8,128]{3,2,1,0:T(8,128)S(1)}, u32[]{:S(2)}, u32[]{:S(2)}) collective-permute-start(f32[8,16,8,128]{3,2,1,0:T(8,128)S(1)} %get-tuple-element.17.own_a), channel_id=1, source_target_pairs={{1,2},{3,4},{5,6},{7,8},{9,10},{11,12},{13,14},{15,16},{17,18},{19... | collective-permute-start | bytes 1572872 | tf_op jit(solution)/shard_map/ppermute | solution.py:693
  4.2 5.1 %collective-permute-start.2 = (f32[8,16,8,128]{3,2,1,0:T(8,128)S(1)}, f32[8,16,8,128]{3,2,1,0:T(8,128)S(1)}, u32[]{:S(2)}, u32[]{:S(2)}) collective-permute-start(f32[8,16,8,128]{3,2,1,0:T(8,128)S(1)} %get-tuple-element.16.own_b), channel_id=1, source_target_pairs={{0,1},{2,3},{4,5},{6,7},{8,9},{10,11},{12,13},{14,15},{16,17},{18,... | collective-permute-start | bytes 1572872 | tf_op jit(solution)/shard_map/ppermute | solution.py:698
  9.4 1.9 %collective-permute-start = (f32[8,16,8,128]{3,2,1,0:T(8,128)S(1)}, f32[8,16,8,128]{3,2,1,0:T(8,128)S(1)}, u32[]{:S(2)}, u32[]{:S(2)}) collective-permute-start(f32[8,16,8,128]{3,2,1,0:T(8,128)S(1)} %get-tuple-element.16.own_b), channel_id=1, source_target_pairs={{1,2},{3,4},{5,6},{7,8},{9,10},{11,12},{13,14},{15,16},{17,18},{19... | collective-permute-start | bytes 1572872 | tf_op jit(solution)/shard_map/ppermute | solution.py:693
  11.3 3.9 %collective-permute-start.3 = (f32[8,16,8,128]{3,2,1,0:T(8,128)S(1)}, f32[8,16,8,128]{3,2,1,0:T(8,128)S(1)}, u32[]{:S(2)}, u32[]{:S(2)}) collective-permute-start(f32[8,16,8,128]{3,2,1,0:T(8,128)S(1)} %get-tuple-element.17.own_a), channel_id=1, source_target_pairs={{0,1},{2,3},{4,5},{6,7},{8,9},{10,11},{12,13},{14,15},{16,17},{18,... | collective-permute-start | bytes 1572872 | tf_op jit(solution)/shard_map/ppermute | solution.py:698
  15.3 0.0 collective-permute-done.1.low
  15.3 0.0 collective-permute-done.2.high
  15.3 3.7 %inner.1 = (f32[25,16,8,128]{3,2,1,0:T(8,128)S(1)}, f32[25,16,8,128]{3,2,1,0:T(8,128)S(1)}, f32[25,16,8,128]{3,2,1,0:T(8,128)S(1)}, f32[16,16,8,128]{3,2,1,0:T(8,128)S(1)}, f32[4,5,16,8,128]{4,3,2,1,0:T(8,128)S(1)}) custom-call(f32[8,16,8,128]{3,2,1,0:T(8,128)S(1)} %collective-permute-done.1.low, f32[8,16,8,128]{3,2,1,0:T(8,128)S(1)} %get-tuple-element.17.own_a, ...), custom_call_target="tpu_custom_call" | custom-call | flops 100000000 | bytes 10000000 | tf_op jit(solution)/shard_map/inner/pallas_call | solution.py:401
  19.0 0.9 collective-permute-done.low
  19.9 0.0 collective-permute-done.3.high
  19.9 6.7 %outer.1 = (f32[16,22,8,128]{3,2,1,0:T(8,128)S(1)}, f32[25,16,8,128]{3,2,1,0:T(8,128)S(1)}, f32[25,16,8,128]{3,2,1,0:T(8,128)S(1)}, f32[25,16,8,128]{3,2,1,0:T(8,128)S(1)}) custom-call(f32[8,16,8,128]{3,2,1,0:T(8,128)S(1)} %collective-permute-done.low, ...), custom_call_target="tpu_custom_call", output_to_operand_aliasing={{1}: (2, {}), {2}: (3, {}), {3}: (4, {})} | custom-call | tf_op jit(solution)/shard_map/outer/pallas_call | solution.py:421
  26.6 29.5 %all_to_all.10.sent = f32[16,22,8,128]{3,2,1,0:T(8,128)S(1)} all-to-all(f32[16,22,8,128]{3,2,1,0:T(8,128)S(1)} %get-tuple-element.23), channel_id=1, replica_groups=mesh['tm'=16,'space'=32] {'tm'}, dimensions={0} | all-to-all | bytes 2883584 | tf_op jit(solution)/shard_map/all_to_all | solution.py:717
  56.1 0.1 pack.1
  56.2 1.9 %collective-permute-start.4 = (f32[84,8,128]{2,1,0:T(8,128)S(1)}, f32[84,8,128]{2,1,0:T(8,128)S(1)}, u32[]{:S(2)}, u32[]{:S(2)}) collective-permute-start(f32[84,8,128]{2,1,0:T(8,128)S(1)} %get-tuple-element.25), channel_id=1, source_target_pairs={{1,2},{3,4},{5,6},{7,8},{9,10},{11,12},{13,14},{15,16},{17,18},{19... | collective-permute-start | bytes 1032200 | tf_op jit(solution)/shard_map/ppermute | solution.py:693
  58.2 3.1 %collective-permute-start.5 = (f32[84,8,128]{2,1,0:T(8,128)S(1)}, f32[84,8,128]{2,1,0:T(8,128)S(1)}, u32[]{:S(2)}, u32[]{:S(2)}) collective-permute-start(f32[84,8,128]{2,1,0:T(8,128)S(1)} %get-tuple-element.26), channel_id=1, source_target_pairs={{0,1},{2,3},{4,5},{6,7},{8,9},{10,11},{12,13},{14,15},{16,17},{18,... | collective-permute-start | bytes 1032200 | tf_op jit(solution)/shard_map/ppermute | solution.py:698
  61.2 0.8 strip.1.eta
  62.0 2.8 %collective-permute-done.4.below = f32[84,8,128]{2,1,0:T(8,128)S(1)} collective-permute-done((f32[84,8,128]{2,1,0:T(8,128)S(1)}, f32[84,8,128]{2,1,0:T(8,128)S(1)}, u32[]{:S(2)}, u32[]{:S(2)}) %collective-permute-start.4) | collective-permute-done | bytes 344096 | tf_op jit(solution)/shard_map/ppermute | solution.py:693
  64.8 0.0 collective-permute-done.5.above
  64.8 2.3 %first.1.done = f32[8,8,8,128]{3,2,1,0:T(8,128)S(1)} custom-call(f32[24,3,8,128]{3,2,1,0:T(8,128)S(1)} %strip.1.eta, f32[16,22,8,128]{3,2,1,0:T(8,128)S(1)} %all_to_all.10.sent, f32[16,2,8,128]{3,2,1,0:T(8,128)S(1)} %get-tuple-element.24.ends, f32[84,8,128]{2,1,0:T(8,128)S(1)} %collective-permute-done.4.below, f32[84,8,128]{2,1,0:T(8,128)S(1)} %collective-permute-done.5.above), custom_call_target="tpu_custom_call" | custom-call | tf_op jit(solution)/shard_map/first/pallas_call | solution.py:650
  67.2 0.7 collective-permute-start.6
  67.8 4.3 %collective-permute-start.7 = (f32[8,8,128]{2,1,0:T(8,128)S(1)}, f32[8,8,128]{2,1,0:T(8,128)S(1)}, u32[]{:S(2)}, u32[]{:S(2)}) collective-permute-start(f32[8,8,128]{2,1,0:T(8,128)S(1)} %slice_bitcast_fusion), channel_id=1, source_target_pairs={{0,32},{64,96},{224,192},{160,128},{256,288},{320,352},{480,448},{... | collective-permute-start | bytes 98312 | tf_op jit(solution)/shard_map/ppermute | solution.py:705
  72.2 0.0 collective-permute-done.6
  72.2 1.9 %collective-permute-done.7 = f32[8,8,128]{2,1,0:T(8,128)S(1)} collective-permute-done((f32[8,8,128]{2,1,0:T(8,128)S(1)}, f32[8,8,128]{2,1,0:T(8,128)S(1)}, u32[]{:S(2)}, u32[]{:S(2)}) %collective-permute-start.7) | collective-permute-done | bytes 32800 | tf_op jit(solution)/shard_map/ppermute | solution.py:705
  74.1 1.9 %collective-permute-start.8 = (f32[8,24,128]{2,1,0:T(8,128)S(1)}, f32[8,24,128]{2,1,0:T(8,128)S(1)}, u32[]{:S(2)}, u32[]{:S(2)}) collective-permute-start(f32[8,24,128]{2,1,0:T(8,128)S(1)} %pad_maximum_fusion.own_u), channel_id=1, source_target_pairs={{1,2},{3,4},{5,6},{7,8},{9,10},{11,12},{13,14},{15,16},{17,18},{19... | collective-permute-start | bytes 294920 | tf_op jit(solution)/shard_map/ppermute | solution.py:693
  76.0 4.5 %collective-permute-start.9 = (f32[8,24,128]{2,1,0:T(8,128)S(1)}, f32[8,24,128]{2,1,0:T(8,128)S(1)}, u32[]{:S(2)}, u32[]{:S(2)}) collective-permute-start(f32[8,24,128]{2,1,0:T(8,128)S(1)} %pad_maximum_fusion.own_u), channel_id=1, source_target_pairs={{0,1},{2,3},{4,5},{6,7},{8,9},{10,11},{12,13},{14,15},{16,17},{18,... | collective-permute-start | bytes 294920 | tf_op jit(solution)/shard_map/ppermute | solution.py:698
  80.5 0.0 collective-permute-done.8.low_u
  80.5 0.9 collective-permute-done.9.high_u
  81.5 2.8 %second.1 = f32[16,8,8,128]{3,2,1,0:T(8,128)S(1)} custom-call(f32[24,3,8,128]{3,2,1,0:T(8,128)S(1)} %strip.1.eta, f32[16,22,8,128]{3,2,1,0:T(8,128)S(1)} %all_to_all.10.sent, f32[16,2,8,128]{3,2,1,0:T(8,128)S(1)} %get-tuple-element.24.ends, f32[84,8,128]{2,1,0:T(8,128)S(1)} %collective-permute-done.4.below, f32[84,8,128]{2,1,0:T(8,128)S(1)} %collective-permute-done.5.above, ...), custom_call_target="tpu_custom_call" | custom-call | tf_op jit(solution)/shard_map/second/pallas_call | solution.py:650
  84.3 17.2 %all_to_all.11.strips = f32[16,8,8,128]{3,2,1,0:T(8,128)S(1)} all-to-all(f32[16,8,8,128]{3,2,1,0:T(8,128)S(1)} %second.1), channel_id=1, replica_groups=mesh['tm'=16,'space'=32] {'tm'}, dimensions={0} | all-to-all | bytes 1048576 | tf_op jit(solution)/shard_map/all_to_all | solution.py:727
  101.4 0.9 place.1
  (3 shorter events, 0.0 us)
Async XLA Ops:
  2.3 12.9 %collective-permute-start.1 = (f32[8,16,8,128]{3,2,1,0:T(8,128)S(1)}, f32[8,16,8,128]{3,2,1,0:T(8,128)S(1)}, u32[]{:S(2)}, u32[]{:S(2)}) collective-permute-start(f32[8,16,8,128]{3,2,1,0:T(8,128)S(1)} %get-tuple-element.17.own_a), channel_id=1, source_target_pairs={{1,2},{3,4},{5,6},{7,8},{9,10},{11,12},{13,14},{15,16},{17,18},{19... | collective-permute-start | bytes 1572872 | tf_op jit(solution)/shard_map/ppermute | solution.py:693
  4.2 11.0 %collective-permute-start.2 = (f32[8,16,8,128]{3,2,1,0:T(8,128)S(1)}, f32[8,16,8,128]{3,2,1,0:T(8,128)S(1)}, u32[]{:S(2)}, u32[]{:S(2)}) collective-permute-start(f32[8,16,8,128]{3,2,1,0:T(8,128)S(1)} %get-tuple-element.16.own_b), channel_id=1, source_target_pairs={{0,1},{2,3},{4,5},{6,7},{8,9},{10,11},{12,13},{14,15},{16,17},{18,... | collective-permute-start | bytes 1572872 | tf_op jit(solution)/shard_map/ppermute | solution.py:698
  9.4 10.5 %collective-permute-start = (f32[8,16,8,128]{3,2,1,0:T(8,128)S(1)}, f32[8,16,8,128]{3,2,1,0:T(8,128)S(1)}, u32[]{:S(2)}, u32[]{:S(2)}) collective-permute-start(f32[8,16,8,128]{3,2,1,0:T(8,128)S(1)} %get-tuple-element.16.own_b), channel_id=1, source_target_pairs={{1,2},{3,4},{5,6},{7,8},{9,10},{11,12},{13,14},{15,16},{17,18},{19... | collective-permute-start | bytes 1572872 | tf_op jit(solution)/shard_map/ppermute | solution.py:693
  11.3 8.6 %collective-permute-start.3 = (f32[8,16,8,128]{3,2,1,0:T(8,128)S(1)}, f32[8,16,8,128]{3,2,1,0:T(8,128)S(1)}, u32[]{:S(2)}, u32[]{:S(2)}) collective-permute-start(f32[8,16,8,128]{3,2,1,0:T(8,128)S(1)} %get-tuple-element.17.own_a), channel_id=1, source_target_pairs={{0,1},{2,3},{4,5},{6,7},{8,9},{10,11},{12,13},{14,15},{16,17},{18,... | collective-permute-start | bytes 1572872 | tf_op jit(solution)/shard_map/ppermute | solution.py:698
  56.2 8.6 %collective-permute-start.4 = (f32[84,8,128]{2,1,0:T(8,128)S(1)}, f32[84,8,128]{2,1,0:T(8,128)S(1)}, u32[]{:S(2)}, u32[]{:S(2)}) collective-permute-start(f32[84,8,128]{2,1,0:T(8,128)S(1)} %get-tuple-element.25), channel_id=1, source_target_pairs={{1,2},{3,4},{5,6},{7,8},{9,10},{11,12},{13,14},{15,16},{17,18},{19... | collective-permute-start | bytes 1032200 | tf_op jit(solution)/shard_map/ppermute | solution.py:693
  58.2 6.6 %collective-permute-start.5 = (f32[84,8,128]{2,1,0:T(8,128)S(1)}, f32[84,8,128]{2,1,0:T(8,128)S(1)}, u32[]{:S(2)}, u32[]{:S(2)}) collective-permute-start(f32[84,8,128]{2,1,0:T(8,128)S(1)} %get-tuple-element.26), channel_id=1, source_target_pairs={{0,1},{2,3},{4,5},{6,7},{8,9},{10,11},{12,13},{14,15},{16,17},{18,... | collective-permute-start | bytes 1032200 | tf_op jit(solution)/shard_map/ppermute | solution.py:698
  67.2 5.0 %collective-permute-start.6 = (f32[8,8,128]{2,1,0:T(8,128)S(1)}, f32[8,8,128]{2,1,0:T(8,128)S(1)}, u32[]{:S(2)}, u32[]{:S(2)}) collective-permute-start(f32[8,8,128]{2,1,0:T(8,128)S(1)} %slice_bitcast_fusion), channel_id=1, source_target_pairs={{32,64},{96,224},{192,160},{128,256},{288,320},{352,480},{448,416}... | collective-permute-start | bytes 98312 | tf_op jit(solution)/shard_map/ppermute | solution.py:705
  67.8 6.2 %collective-permute-start.7 = (f32[8,8,128]{2,1,0:T(8,128)S(1)}, f32[8,8,128]{2,1,0:T(8,128)S(1)}, u32[]{:S(2)}, u32[]{:S(2)}) collective-permute-start(f32[8,8,128]{2,1,0:T(8,128)S(1)} %slice_bitcast_fusion), channel_id=1, source_target_pairs={{0,32},{64,96},{224,192},{160,128},{256,288},{320,352},{480,448},{... | collective-permute-start | bytes 98312 | tf_op jit(solution)/shard_map/ppermute | solution.py:705
  74.1 6.4 %collective-permute-start.8 = (f32[8,24,128]{2,1,0:T(8,128)S(1)}, f32[8,24,128]{2,1,0:T(8,128)S(1)}, u32[]{:S(2)}, u32[]{:S(2)}) collective-permute-start(f32[8,24,128]{2,1,0:T(8,128)S(1)} %pad_maximum_fusion.own_u), channel_id=1, source_target_pairs={{1,2},{3,4},{5,6},{7,8},{9,10},{11,12},{13,14},{15,16},{17,18},{19... | collective-permute-start | bytes 294920 | tf_op jit(solution)/shard_map/ppermute | solution.py:693
  76.0 5.4 %collective-permute-start.9 = (f32[8,24,128]{2,1,0:T(8,128)S(1)}, f32[8,24,128]{2,1,0:T(8,128)S(1)}, u32[]{:S(2)}, u32[]{:S(2)}) collective-permute-start(f32[8,24,128]{2,1,0:T(8,128)S(1)} %pad_maximum_fusion.own_u), channel_id=1, source_target_pairs={{0,1},{2,3},{4,5},{6,7},{8,9},{10,11},{12,13},{14,15},{16,17},{18,... | collective-permute-start | bytes 294920 | tf_op jit(solution)/shard_map/ppermute | solution.py:698

commit v10 on v9

--- a/solution.py
+++ b/solution.py
@@ -17,7 +17,6 @@
 SLICES = 16
 REGIONS = 4
 ROWS = 8
-EXT = 3 * ROWS
 SMEM = pl.BlockSpec(memory_space=pltpu.SMEM)
 FIRST = 7
 VMEM = pl.BlockSpec(memory_space=pltpu.VMEM)
@@ -645,7 +644,7 @@
     coarse_steps(SLICES - 1 - FIRST, FIRST, eta, refs, u_ref, k_ref, f_ref, put)
 
 
-def coarse_call(kernel, name, count, *operands):
+def coarse_call(kernel, count, *operands):
     f32 = jnp.float32
     return pl.pallas_call(
         kernel,
@@ -658,7 +657,6 @@
             pltpu.VMEM((3, 8, NZ), f32),
         ],
         compiler_params=pltpu.CompilerParams(vmem_limit_bytes=8 << 20),
-        name=name,
     )(*operands)
 
 
@@ -711,18 +709,20 @@
 
 def per_device(start_values, regions, resistivity):
     own_a, own_b = own_part(start_values[0], regions, resistivity)
-    low_near, high_near = across(own_a), beside(own_b)
-    low_far, high_far = across(own_b), beside(own_a)
+    low_near = across(own_a)
+    low_far = across(own_b)
+    high_near = beside(own_b)
+    high_far = beside(own_a)
     sent = outer(low_far, high_far, *inner(low_near, own_a, own_b, high_near))
     sent = lax.all_to_all(sent, "tm", 0, 0)
     down, up, ends = pack(sent)
     below, above = across(down), beside(up)
     eta = strip_part(low_far, low_near, own_a, own_b, high_near, high_far)
-    done = coarse_call(first_kernel, "first", FIRST + 1, eta, sent, ends, below, above)
+    done = coarse_call(first_kernel, FIRST + 1, eta, sent, ends, below, above)
     strip = with_strips(done[FIRST])
     x_low, x_high = across(strip), beside(strip)
     ends = coarse_call(
-        second_kernel, "second", SLICES, eta, sent, ends, below, above, x_low, strip, x_high, done
+        second_kernel, SLICES, eta, sent, ends, below, above, x_low, strip, x_high, done
     )
     result = lax.all_to_all(ends, "tm", 0, 0)
     return place(result)[None]

time: 103 us -> 103 us (level)
  no operation moved by 1% of the time
where the time goes in v10:
time: 103 us; the launch traced here: 102 us
  blocking collectives  46.7 us (45%)
  starting transfers between devices  29.3 us (28%)
  Pallas kernels  19.7 us (19%)
  waiting for transfers between devices  6.51 us (6%)
    all_to_all x1, blocking collectives, per_device(): sent = lax.all_to_all(sent, 'tm', 0, 0)  29.5 us
    all_to_all x1, blocking collectives, per_device(): result = lax.all_to_all(ends, 'tm', 0, 0)  17.2 us
    ppermute x4, starting transfers between devices, beside(): return lax.ppermute(value, 'space', pairs + [(b, a) for a, b in pairs])  16.6 us
    ppermute x4, starting transfers between devices, across(): return lax.ppermute(value, 'space', pairs + [(b, a) for a, b in pairs])  7.68 us
    pallas_call x1, Pallas kernels, outer(): pl.pallas_call(outer_kernel, out_shape=(jax.ShapeDtypeStruct((SLICES, LOA...  6.66 us
    pallas_call x2, Pallas kernels, coarse_call(): pl.pallas_call(kernel, out_shape=jax.ShapeDtypeStruct((count, BX, ROWS, N...  5.15 us
    ppermute x2, starting transfers between devices, with_strips(): sides.append(lax.ppermute(state, 'tm', pairs + [(b, a) for a, b in pairs]))  4.97 us
    pallas_call x1, Pallas kernels, inner(): pl.pallas_call(inner_kernel, out_shape=(GRID, GRID, GRID, jax.ShapeDtypeS...  3.71 us
  transfers between devices with their start and end apart: 10, of which 4 were waited for; matrix products, arithmetic and copies ran while one was open for 0% of the time, Pallas kernels for 4%

profile of v10, /device:TPU:96, one launch (start us, length us, event | category | flops | bytes accessed | tf_op | source)
XLA Modules:
  0.0 102.3 jit_solution(16568905034850838517)
XLA Ops:
  0.0 2.3 %own.1 = (f32[8,16,8,128]{3,2,1,0:T(8,128)S(1)}, f32[8,16,8,128]{3,2,1,0:T(8,128)S(1)}) custom-call(f32[8,128,128]{2,1,0:T(8,128)} %bitcast.16, s32[8,128,128]{2,1,0:T(8,128)} %regions.1, f32[4]{0:T(128)} %resistivity.1), custom_call_target="tpu_custom_call" | custom-call | tf_op jit(solution)/shard_map/own/pallas_call | solution.py:195
  2.3 1.9 %collective-permute-start.1 = (f32[8,16,8,128]{3,2,1,0:T(8,128)S(1)}, f32[8,16,8,128]{3,2,1,0:T(8,128)S(1)}, u32[]{:S(2)}, u32[]{:S(2)}) collective-permute-start(f32[8,16,8,128]{3,2,1,0:T(8,128)S(1)} %get-tuple-element.17.own_a), channel_id=1, source_target_pairs={{1,2},{3,4},{5,6},{7,8},{9,10},{11,12},{13,14},{15,16},{17,18},{19... | collective-permute-start | bytes 1572872 | tf_op jit(solution)/shard_map/ppermute | solution.py:691
  4.2 5.1 %collective-permute-start.2 = (f32[8,16,8,128]{3,2,1,0:T(8,128)S(1)}, f32[8,16,8,128]{3,2,1,0:T(8,128)S(1)}, u32[]{:S(2)}, u32[]{:S(2)}) collective-permute-start(f32[8,16,8,128]{3,2,1,0:T(8,128)S(1)} %get-tuple-element.16.own_b), channel_id=1, source_target_pairs={{0,1},{2,3},{4,5},{6,7},{8,9},{10,11},{12,13},{14,15},{16,17},{18,... | collective-permute-start | bytes 1572872 | tf_op jit(solution)/shard_map/ppermute | solution.py:696
  9.4 1.9 %collective-permute-start = (f32[8,16,8,128]{3,2,1,0:T(8,128)S(1)}, f32[8,16,8,128]{3,2,1,0:T(8,128)S(1)}, u32[]{:S(2)}, u32[]{:S(2)}) collective-permute-start(f32[8,16,8,128]{3,2,1,0:T(8,128)S(1)} %get-tuple-element.16.own_b), channel_id=1, source_target_pairs={{1,2},{3,4},{5,6},{7,8},{9,10},{11,12},{13,14},{15,16},{17,18},{19... | collective-permute-start | bytes 1572872 | tf_op jit(solution)/shard_map/ppermute | solution.py:691
  11.3 3.9 %collective-permute-start.3 = (f32[8,16,8,128]{3,2,1,0:T(8,128)S(1)}, f32[8,16,8,128]{3,2,1,0:T(8,128)S(1)}, u32[]{:S(2)}, u32[]{:S(2)}) collective-permute-start(f32[8,16,8,128]{3,2,1,0:T(8,128)S(1)} %get-tuple-element.17.own_a), channel_id=1, source_target_pairs={{0,1},{2,3},{4,5},{6,7},{8,9},{10,11},{12,13},{14,15},{16,17},{18,... | collective-permute-start | bytes 1572872 | tf_op jit(solution)/shard_map/ppermute | solution.py:696
  15.3 0.0 collective-permute-done.1.low
  15.3 0.0 collective-permute-done.2.high
  15.3 3.7 %inner.1 = (f32[25,16,8,128]{3,2,1,0:T(8,128)S(1)}, f32[25,16,8,128]{3,2,1,0:T(8,128)S(1)}, f32[25,16,8,128]{3,2,1,0:T(8,128)S(1)}, f32[16,16,8,128]{3,2,1,0:T(8,128)S(1)}, f32[4,5,16,8,128]{4,3,2,1,0:T(8,128)S(1)}) custom-call(f32[8,16,8,128]{3,2,1,0:T(8,128)S(1)} %collective-permute-done.1.low, f32[8,16,8,128]{3,2,1,0:T(8,128)S(1)} %get-tuple-element.17.own_a, ...), custom_call_target="tpu_custom_call" | custom-call | flops 100000000 | bytes 10000000 | tf_op jit(solution)/shard_map/inner/pallas_call | solution.py:400
  19.0 0.9 collective-permute-done.low
  19.9 0.0 collective-permute-done.3.high
  19.9 6.7 %outer.1 = (f32[16,22,8,128]{3,2,1,0:T(8,128)S(1)}, f32[25,16,8,128]{3,2,1,0:T(8,128)S(1)}, f32[25,16,8,128]{3,2,1,0:T(8,128)S(1)}, f32[25,16,8,128]{3,2,1,0:T(8,128)S(1)}) custom-call(f32[8,16,8,128]{3,2,1,0:T(8,128)S(1)} %collective-permute-done.low, ...), custom_call_target="tpu_custom_call", output_to_operand_aliasing={{1}: (2, {}), {2}: (3, {}), {3}: (4, {})} | custom-call | tf_op jit(solution)/shard_map/outer/pallas_call | solution.py:420
  26.6 29.5 %all_to_all.10.sent = f32[16,22,8,128]{3,2,1,0:T(8,128)S(1)} all-to-all(f32[16,22,8,128]{3,2,1,0:T(8,128)S(1)} %get-tuple-element.23), channel_id=1, replica_groups=mesh['tm'=16,'space'=32] {'tm'}, dimensions={0} | all-to-all | bytes 2883584 | tf_op jit(solution)/shard_map/all_to_all | solution.py:717
  56.1 0.1 pack.1
  56.2 1.9 %collective-permute-start.4 = (f32[84,8,128]{2,1,0:T(8,128)S(1)}, f32[84,8,128]{2,1,0:T(8,128)S(1)}, u32[]{:S(2)}, u32[]{:S(2)}) collective-permute-start(f32[84,8,128]{2,1,0:T(8,128)S(1)} %get-tuple-element.25), channel_id=1, source_target_pairs={{1,2},{3,4},{5,6},{7,8},{9,10},{11,12},{13,14},{15,16},{17,18},{19... | collective-permute-start | bytes 1032200 | tf_op jit(solution)/shard_map/ppermute | solution.py:691
  58.2 3.1 %collective-permute-start.5 = (f32[84,8,128]{2,1,0:T(8,128)S(1)}, f32[84,8,128]{2,1,0:T(8,128)S(1)}, u32[]{:S(2)}, u32[]{:S(2)}) collective-permute-start(f32[84,8,128]{2,1,0:T(8,128)S(1)} %get-tuple-element.26), channel_id=1, source_target_pairs={{0,1},{2,3},{4,5},{6,7},{8,9},{10,11},{12,13},{14,15},{16,17},{18,... | collective-permute-start | bytes 1032200 | tf_op jit(solution)/shard_map/ppermute | solution.py:696
  61.2 0.8 strip.1.eta
  62.0 2.8 %collective-permute-done.4.below = f32[84,8,128]{2,1,0:T(8,128)S(1)} collective-permute-done((f32[84,8,128]{2,1,0:T(8,128)S(1)}, f32[84,8,128]{2,1,0:T(8,128)S(1)}, u32[]{:S(2)}, u32[]{:S(2)}) %collective-permute-start.4) | collective-permute-done | bytes 344096 | tf_op jit(solution)/shard_map/ppermute | solution.py:691
  64.8 0.0 collective-permute-done.5.above
  64.8 2.3 %shard_map.37.done = f32[8,8,8,128]{3,2,1,0:T(8,128)S(1)} custom-call(f32[24,3,8,128]{3,2,1,0:T(8,128)S(1)} %strip.1.eta, f32[16,22,8,128]{3,2,1,0:T(8,128)S(1)} %all_to_all.10.sent, f32[16,2,8,128]{3,2,1,0:T(8,128)S(1)} %get-tuple-element.24.ends, f32[84,8,128]{2,1,0:T(8,128)S(1)} %collective-permute-done.4.below, ...), custom_call_target="tpu_custom_call" | custom-call | tf_op jit(solution)/shard_map/pallas_call | solution.py:649
  67.2 0.7 collective-permute-start.6
  67.8 4.3 %collective-permute-start.7 = (f32[8,8,128]{2,1,0:T(8,128)S(1)}, f32[8,8,128]{2,1,0:T(8,128)S(1)}, u32[]{:S(2)}, u32[]{:S(2)}) collective-permute-start(f32[8,8,128]{2,1,0:T(8,128)S(1)} %slice_bitcast_fusion), channel_id=1, source_target_pairs={{0,32},{64,96},{224,192},{160,128},{256,288},{320,352},{480,448},{... | collective-permute-start | bytes 98312 | tf_op jit(solution)/shard_map/ppermute | solution.py:703
  72.2 0.0 collective-permute-done.6
  72.2 1.9 %collective-permute-done.7 = f32[8,8,128]{2,1,0:T(8,128)S(1)} collective-permute-done((f32[8,8,128]{2,1,0:T(8,128)S(1)}, f32[8,8,128]{2,1,0:T(8,128)S(1)}, u32[]{:S(2)}, u32[]{:S(2)}) %collective-permute-start.7) | collective-permute-done | bytes 32800 | tf_op jit(solution)/shard_map/ppermute | solution.py:703
  74.1 1.9 %collective-permute-start.8 = (f32[8,24,128]{2,1,0:T(8,128)S(1)}, f32[8,24,128]{2,1,0:T(8,128)S(1)}, u32[]{:S(2)}, u32[]{:S(2)}) collective-permute-start(f32[8,24,128]{2,1,0:T(8,128)S(1)} %pad_maximum_fusion.own_u), channel_id=1, source_target_pairs={{1,2},{3,4},{5,6},{7,8},{9,10},{11,12},{13,14},{15,16},{17,18},{19... | collective-permute-start | bytes 294920 | tf_op jit(solution)/shard_map/ppermute | solution.py:691
  76.0 4.5 %collective-permute-start.9 = (f32[8,24,128]{2,1,0:T(8,128)S(1)}, f32[8,24,128]{2,1,0:T(8,128)S(1)}, u32[]{:S(2)}, u32[]{:S(2)}) collective-permute-start(f32[8,24,128]{2,1,0:T(8,128)S(1)} %pad_maximum_fusion.own_u), channel_id=1, source_target_pairs={{0,1},{2,3},{4,5},{6,7},{8,9},{10,11},{12,13},{14,15},{16,17},{18,... | collective-permute-start | bytes 294920 | tf_op jit(solution)/shard_map/ppermute | solution.py:696
  80.5 0.0 collective-permute-done.8.low_u
  80.5 0.9 collective-permute-done.9.high_u
  81.5 2.8 %shard_map.38 = f32[16,8,8,128]{3,2,1,0:T(8,128)S(1)} custom-call(f32[24,3,8,128]{3,2,1,0:T(8,128)S(1)} %strip.1.eta, f32[16,22,8,128]{3,2,1,0:T(8,128)S(1)} %all_to_all.10.sent, f32[16,2,8,128]{3,2,1,0:T(8,128)S(1)} %get-tuple-element.24.ends, f32[84,8,128]{2,1,0:T(8,128)S(1)} %collective-permute-done.4.below, ...), custom_call_target="tpu_custom_call" | custom-call | tf_op jit(solution)/shard_map/pallas_call | solution.py:649
  84.3 17.2 %all_to_all.11.strips = f32[16,8,8,128]{3,2,1,0:T(8,128)S(1)} all-to-all(f32[16,8,8,128]{3,2,1,0:T(8,128)S(1)} %shard_map.38), channel_id=1, replica_groups=mesh['tm'=16,'space'=32] {'tm'}, dimensions={0} | all-to-all | bytes 1048576 | tf_op jit(solution)/shard_map/all_to_all | solution.py:727
  101.4 0.9 place.1
  (3 shorter events, 0.0 us)
Async XLA Ops:
  2.3 12.9 %collective-permute-start.1 = (f32[8,16,8,128]{3,2,1,0:T(8,128)S(1)}, f32[8,16,8,128]{3,2,1,0:T(8,128)S(1)}, u32[]{:S(2)}, u32[]{:S(2)}) collective-permute-start(f32[8,16,8,128]{3,2,1,0:T(8,128)S(1)} %get-tuple-element.17.own_a), channel_id=1, source_target_pairs={{1,2},{3,4},{5,6},{7,8},{9,10},{11,12},{13,14},{15,16},{17,18},{19... | collective-permute-start | bytes 1572872 | tf_op jit(solution)/shard_map/ppermute | solution.py:691
  4.2 11.0 %collective-permute-start.2 = (f32[8,16,8,128]{3,2,1,0:T(8,128)S(1)}, f32[8,16,8,128]{3,2,1,0:T(8,128)S(1)}, u32[]{:S(2)}, u32[]{:S(2)}) collective-permute-start(f32[8,16,8,128]{3,2,1,0:T(8,128)S(1)} %get-tuple-element.16.own_b), channel_id=1, source_target_pairs={{0,1},{2,3},{4,5},{6,7},{8,9},{10,11},{12,13},{14,15},{16,17},{18,... | collective-permute-start | bytes 1572872 | tf_op jit(solution)/shard_map/ppermute | solution.py:696
  9.4 10.5 %collective-permute-start = (f32[8,16,8,128]{3,2,1,0:T(8,128)S(1)}, f32[8,16,8,128]{3,2,1,0:T(8,128)S(1)}, u32[]{:S(2)}, u32[]{:S(2)}) collective-permute-start(f32[8,16,8,128]{3,2,1,0:T(8,128)S(1)} %get-tuple-element.16.own_b), channel_id=1, source_target_pairs={{1,2},{3,4},{5,6},{7,8},{9,10},{11,12},{13,14},{15,16},{17,18},{19... | collective-permute-start | bytes 1572872 | tf_op jit(solution)/shard_map/ppermute | solution.py:691
  11.3 8.6 %collective-permute-start.3 = (f32[8,16,8,128]{3,2,1,0:T(8,128)S(1)}, f32[8,16,8,128]{3,2,1,0:T(8,128)S(1)}, u32[]{:S(2)}, u32[]{:S(2)}) collective-permute-start(f32[8,16,8,128]{3,2,1,0:T(8,128)S(1)} %get-tuple-element.17.own_a), channel_id=1, source_target_pairs={{0,1},{2,3},{4,5},{6,7},{8,9},{10,11},{12,13},{14,15},{16,17},{18,... | collective-permute-start | bytes 1572872 | tf_op jit(solution)/shard_map/ppermute | solution.py:696
  56.2 8.6 %collective-permute-start.4 = (f32[84,8,128]{2,1,0:T(8,128)S(1)}, f32[84,8,128]{2,1,0:T(8,128)S(1)}, u32[]{:S(2)}, u32[]{:S(2)}) collective-permute-start(f32[84,8,128]{2,1,0:T(8,128)S(1)} %get-tuple-element.25), channel_id=1, source_target_pairs={{1,2},{3,4},{5,6},{7,8},{9,10},{11,12},{13,14},{15,16},{17,18},{19... | collective-permute-start | bytes 1032200 | tf_op jit(solution)/shard_map/ppermute | solution.py:691
  58.2 6.6 %collective-permute-start.5 = (f32[84,8,128]{2,1,0:T(8,128)S(1)}, f32[84,8,128]{2,1,0:T(8,128)S(1)}, u32[]{:S(2)}, u32[]{:S(2)}) collective-permute-start(f32[84,8,128]{2,1,0:T(8,128)S(1)} %get-tuple-element.26), channel_id=1, source_target_pairs={{0,1},{2,3},{4,5},{6,7},{8,9},{10,11},{12,13},{14,15},{16,17},{18,... | collective-permute-start | bytes 1032200 | tf_op jit(solution)/shard_map/ppermute | solution.py:696
  67.2 5.0 %collective-permute-start.6 = (f32[8,8,128]{2,1,0:T(8,128)S(1)}, f32[8,8,128]{2,1,0:T(8,128)S(1)}, u32[]{:S(2)}, u32[]{:S(2)}) collective-permute-start(f32[8,8,128]{2,1,0:T(8,128)S(1)} %slice_bitcast_fusion), channel_id=1, source_target_pairs={{32,64},{96,224},{192,160},{128,256},{288,320},{352,480},{448,416}... | collective-permute-start | bytes 98312 | tf_op jit(solution)/shard_map/ppermute | solution.py:703
  67.8 6.2 %collective-permute-start.7 = (f32[8,8,128]{2,1,0:T(8,128)S(1)}, f32[8,8,128]{2,1,0:T(8,128)S(1)}, u32[]{:S(2)}, u32[]{:S(2)}) collective-permute-start(f32[8,8,128]{2,1,0:T(8,128)S(1)} %slice_bitcast_fusion), channel_id=1, source_target_pairs={{0,32},{64,96},{224,192},{160,128},{256,288},{320,352},{480,448},{... | collective-permute-start | bytes 98312 | tf_op jit(solution)/shard_map/ppermute | solution.py:703
  74.1 6.4 %collective-permute-start.8 = (f32[8,24,128]{2,1,0:T(8,128)S(1)}, f32[8,24,128]{2,1,0:T(8,128)S(1)}, u32[]{:S(2)}, u32[]{:S(2)}) collective-permute-start(f32[8,24,128]{2,1,0:T(8,128)S(1)} %pad_maximum_fusion.own_u), channel_id=1, source_target_pairs={{1,2},{3,4},{5,6},{7,8},{9,10},{11,12},{13,14},{15,16},{17,18},{19... | collective-permute-start | bytes 294920 | tf_op jit(solution)/shard_map/ppermute | solution.py:691
  76.0 5.4 %collective-permute-start.9 = (f32[8,24,128]{2,1,0:T(8,128)S(1)}, f32[8,24,128]{2,1,0:T(8,128)S(1)}, u32[]{:S(2)}, u32[]{:S(2)}) collective-permute-start(f32[8,24,128]{2,1,0:T(8,128)S(1)} %pad_maximum_fusion.own_u), channel_id=1, source_target_pairs={{0,1},{2,3},{4,5},{6,7},{8,9},{10,11},{12,13},{14,15},{16,17},{18,... | collective-permute-start | bytes 294920 | tf_op jit(solution)/shard_map/ppermute | solution.py:696

commit v11 on v10

--- a/solution.py
+++ b/solution.py
@@ -1,3 +1,5 @@
+import functools
+
 import jax
 import jax.numpy as jnp
 from jax import lax
@@ -141,71 +143,63 @@
     return jnp.where(lax.axis_index("space") < 0, 2, 1)
 
 
-def own_kernel(start, regions, resistivity, *refs):
-    outs, (start_v, regions_v, half_v, resistivity_s, sems) = refs[:2], refs[2:]
-    small = pltpu.make_async_copy(resistivity, resistivity_s, sems.at[4])
-    small.start()
-    copies = []
+def own_kernel(h, start, regions, resistivity, out, *refs):
+    start_v, regions_v, half_v, resistivity_s, sems = refs
     odd = is_mirrored()
-    for h in range(2):
-        part = pl.ds(jnp.where(odd, 1 - h, h) * HALF, HALF)
-        pair = (
-            pltpu.make_async_copy(start.at[part], start_v.at[h], sems.at[2 * h]),
-            pltpu.make_async_copy(regions.at[part], regions_v.at[h], sems.at[2 * h + 1]),
-        )
-        for copy in pair:
-            copy.start()
-        copies.append(pair)
-    small.wait()
+    part = pl.ds(jnp.where(odd, 1 - h, h) * HALF, HALF)
+    copies = (
+        pltpu.make_async_copy(resistivity, resistivity_s, sems.at[0]),
+        pltpu.make_async_copy(start.at[part], start_v, sems.at[1]),
+        pltpu.make_async_copy(regions.at[part], regions_v, sems.at[2]),
+    )
+    for copy in copies:
+        copy.start()
+    for copy in copies:
+        copy.wait()
     scaled = [resistivity_s[i] * jnp.float32(0.5 * fine_step) for i in range(REGIONS)]
-    once = one_trip()
-    for h in range(2):
-        for copy in copies[h]:
-            copy.wait()
-
-        def first_pass(_, carry, h=h):
-            for x in range(HALF):
-                source = jnp.where(odd, HALF - 1 - x, x)
-                for ry in range(Q):
-                    for g in range(Q):
-                        where = rows_at(g, ry)
-                        region = regions_v[h, source, where, :]
-                        value = jnp.zeros((8, NZ), jnp.float32)
-                        for i in range(REGIONS):
-                            value = jnp.where(region == i, scaled[i], value)
-                        half_v[x, Q * ry + g] = turn(g, start_v[h, source, where, :])
-                        half_v[HALF + x, Q * ry + g] = turn(g, value)
-            return carry
-
-        def second_pass(n, _, h=h):
-            for x in [HALF * n + q for q in range(HALF)]:
-                for ry in range(Q):
-                    tiles = gather_tiles([half_v[x, Q * ry + g] for g in range(Q)])
-                    for rz in range(Q):
-                        outs[h][x, Q * ry + rz] = tiles[rz]
-            return 0
-
-        lax.fori_loop(0, once, first_pass, 0)
-        lax.fori_loop(0, 2, second_pass, 0)
-
-
-def own_part(start, regions, resistivity):
+
+    def first_pass(_, carry):
+        for x in range(HALF):
+            source = jnp.where(odd, HALF - 1 - x, x)
+            for ry in range(Q):
+                for g in range(Q):
+                    where = rows_at(g, ry)
+                    region = regions_v[source, where, :]
+                    value = jnp.zeros((8, NZ), jnp.float32)
+                    for i in range(REGIONS):
+                        value = jnp.where(region == i, scaled[i], value)
+                    half_v[x, Q * ry + g] = turn(g, start_v[source, where, :])
+                    half_v[HALF + x, Q * ry + g] = turn(g, value)
+        return carry
+
+    def second_pass(n, _):
+        for x in [HALF * n + q for q in range(HALF)]:
+            for ry in range(Q):
+                tiles = gather_tiles([half_v[x, Q * ry + g] for g in range(Q)])
+                for rz in range(Q):
+                    out[x, Q * ry + rz] = tiles[rz]
+        return 0
+
+    lax.fori_loop(0, one_trip(), first_pass, 0)
+    lax.fori_loop(0, 2, second_pass, 0)
+
+
+def own_part(h, start, regions, resistivity):
     hbm = pl.BlockSpec(memory_space=HBM)
-    shape = jax.ShapeDtypeStruct((2 * HALF, PARTS, 8, NZ), jnp.float32)
     return pl.pallas_call(
-        own_kernel,
-        out_shape=(shape, shape),
+        functools.partial(own_kernel, h),
+        out_shape=jax.ShapeDtypeStruct((2 * HALF, PARTS, 8, NZ), jnp.float32),
         in_specs=[hbm] * 3,
-        out_specs=(VMEM, VMEM),
+        out_specs=VMEM,
         scratch_shapes=[
-            pltpu.VMEM((2, HALF, NY, NZ), jnp.float32),
-            pltpu.VMEM((2, HALF, NY, NZ), jnp.int32),
+            pltpu.VMEM((HALF, NY, NZ), jnp.float32),
+            pltpu.VMEM((HALF, NY, NZ), jnp.int32),
             pltpu.VMEM((2 * HALF, PARTS, 8, NZ), jnp.float32),
             pltpu.SMEM((REGIONS,), jnp.float32),
-            pltpu.SemaphoreType.DMA((5,)),
+            pltpu.SemaphoreType.DMA((3,)),
         ],
         compiler_params=pltpu.CompilerParams(vmem_limit_bytes=8 << 20),
-        name="own",
+        cost_estimate=pl.CostEstimate(flops=10**6, bytes_accessed=10**6, transcendentals=0),
     )(*(pltpu.with_memory_space_constraint(a, HBM) for a in (start, regions, resistivity)))
 
 
@@ -543,7 +537,7 @@
             k_ref[x, c] = coeff(eta[x, c], u_ref[x, c])
         return 0
 
-    lax.fori_loop(BX - count, 2 * BX + count, begin, 0, unroll=4)
+    lax.fori_loop(BX - count, 2 * BX + count, begin, 0, unroll=BX // 2 + count)
 
     def stretch(n, left, planes):
         def body(_, carry):
@@ -708,8 +702,10 @@
 
 
 def per_device(start_values, regions, resistivity):
-    own_a, own_b = own_part(start_values[0], regions, resistivity)
+    args = (start_values[0], regions, resistivity)
+    own_a = own_part(0, *args)
     low_near = across(own_a)
+    own_b = own_part(1, *args)
     low_far = across(own_b)
     high_near = beside(own_b)
     high_far = beside(own_a)

time: 103 us -> 104 us (level)
  the two profiles are of different devices: /device:TPU:96 before, /device:TPU:225 now
where the time goes in v11:
time: 104 us; the launch traced here: 103 us
  blocking collectives  44.8 us (43%)
  starting transfers between devices  27.5 us (26%)
  Pallas kernels  20.6 us (20%)
  waiting for transfers between devices  10.3 us (10%)
    all_to_all x1, blocking collectives, per_device(): sent = lax.all_to_all(sent, 'tm', 0, 0)  27.6 us
    all_to_all x1, blocking collectives, per_device(): result = lax.all_to_all(ends, 'tm', 0, 0)  17.2 us
    ppermute x4, starting transfers between devices, across(): return lax.ppermute(value, 'space', pairs + [(b, a) for a, b in pairs])  14.1 us
    ppermute x4, waiting for transfers between devices, across(): return lax.ppermute(value, 'space', pairs + [(b, a) for a, b in pairs])  9 us
    ppermute x4, starting transfers between devices, beside(): return lax.ppermute(value, 'space', pairs + [(b, a) for a, b in pairs])  8.22 us
    pallas_call x1, Pallas kernels, outer(): pl.pallas_call(outer_kernel, out_shape=(jax.ShapeDtypeStruct((SLICES, LOA...  6.66 us
    ppermute x2, starting transfers between devices, with_strips(): sides.append(lax.ppermute(state, 'tm', pairs + [(b, a) for a, b in pairs]))  5.15 us
    pallas_call x2, Pallas kernels, coarse_call(): pl.pallas_call(kernel, out_shape=jax.ShapeDtypeStruct((count, BX, ROWS, N...  5.05 us
  transfers between devices with their start and end apart: 10, of which 4 were waited for; matrix products, arithmetic and copies ran while one was open for 0% of the time, Pallas kernels for 6%

profile of v11, /device:TPU:225, one launch (start us, length us, event | category | flops | bytes accessed | tf_op | source)
XLA Modules:
  0.0 103.4 jit_solution(159641094597521913)
XLA Ops:
  0.0 1.7 %shard_map.38.own_a = f32[8,16,8,128]{3,2,1,0:T(8,128)S(1)} custom-call(f32[8,128,128]{2,1,0:T(8,128)} %bitcast.16, s32[8,128,128]{2,1,0:T(8,128)} %regions.3, f32[4]{0:T(128)} %resistivity.3), custom_call_target="tpu_custom_call" | custom-call | flops 1000000 | bytes 1000000 | tf_op jit(solution)/shard_map/pallas_call | solution.py:189
  1.7 5.3 %collective-permute-start.1 = (f32[8,16,8,128]{3,2,1,0:T(8,128)S(1)}, f32[8,16,8,128]{3,2,1,0:T(8,128)S(1)}, u32[]{:S(2)}, u32[]{:S(2)}) collective-permute-start(f32[8,16,8,128]{3,2,1,0:T(8,128)S(1)} %shard_map.38.own_a), channel_id=1, source_target_pairs={{1,2},{3,4},{5,6},{7,8},{9,10},{11,12},{13,14},{15,16},{17,18},{19... | collective-permute-start | bytes 1572872 | tf_op jit(solution)/shard_map/ppermute | solution.py:685
  7.0 1.7 %shard_map.37.own_b = f32[8,16,8,128]{3,2,1,0:T(8,128)S(1)} custom-call(f32[8,128,128]{2,1,0:T(8,128)} %bitcast.17, s32[8,128,128]{2,1,0:T(8,128)} %regions.3, f32[4]{0:T(128)} %resistivity.3), custom_call_target="tpu_custom_call" | custom-call | flops 1000000 | bytes 1000000 | tf_op jit(solution)/shard_map/pallas_call | solution.py:189
  8.7 1.9 %collective-permute-start.2 = (f32[8,16,8,128]{3,2,1,0:T(8,128)S(1)}, f32[8,16,8,128]{3,2,1,0:T(8,128)S(1)}, u32[]{:S(2)}, u32[]{:S(2)}) collective-permute-start(f32[8,16,8,128]{3,2,1,0:T(8,128)S(1)} %shard_map.37.own_b), channel_id=1, source_target_pairs={{0,1},{2,3},{4,5},{6,7},{8,9},{10,11},{12,13},{14,15},{16,17},{18,... | collective-permute-start | bytes 1572872 | tf_op jit(solution)/shard_map/ppermute | solution.py:690
  10.6 3.0 %collective-permute-start = (f32[8,16,8,128]{3,2,1,0:T(8,128)S(1)}, f32[8,16,8,128]{3,2,1,0:T(8,128)S(1)}, u32[]{:S(2)}, u32[]{:S(2)}) collective-permute-start(f32[8,16,8,128]{3,2,1,0:T(8,128)S(1)} %shard_map.37.own_b), channel_id=1, source_target_pairs={{1,2},{3,4},{5,6},{7,8},{9,10},{11,12},{13,14},{15,16},{17,18},{19... | collective-permute-start | bytes 1572872 | tf_op jit(solution)/shard_map/ppermute | solution.py:685
  13.7 1.9 %collective-permute-start.3 = (f32[8,16,8,128]{3,2,1,0:T(8,128)S(1)}, f32[8,16,8,128]{3,2,1,0:T(8,128)S(1)}, u32[]{:S(2)}, u32[]{:S(2)}) collective-permute-start(f32[8,16,8,128]{3,2,1,0:T(8,128)S(1)} %shard_map.38.own_a), channel_id=1, source_target_pairs={{0,1},{2,3},{4,5},{6,7},{8,9},{10,11},{12,13},{14,15},{16,17},{18,... | collective-permute-start | bytes 1572872 | tf_op jit(solution)/shard_map/ppermute | solution.py:690
  15.6 0.0 collective-permute-done.1.low
  15.6 0.0 collective-permute-done.2.high
  15.6 3.7 %inner.1 = (f32[25,16,8,128]{3,2,1,0:T(8,128)S(1)}, f32[25,16,8,128]{3,2,1,0:T(8,128)S(1)}, f32[25,16,8,128]{3,2,1,0:T(8,128)S(1)}, f32[16,16,8,128]{3,2,1,0:T(8,128)S(1)}, f32[4,5,16,8,128]{4,3,2,1,0:T(8,128)S(1)}) custom-call(f32[8,16,8,128]{3,2,1,0:T(8,128)S(1)} %collective-permute-done.1.low, f32[8,16,8,128]{3,2,1,0:T(8,128)S(1)} %shard_map.38.own_a, ...), custom_call_target="tpu_custom_call" | custom-call | flops 100000000 | bytes 10000000 | tf_op jit(solution)/shard_map/inner/pallas_call | solution.py:394
  19.3 3.0 %collective-permute-done.low = f32[8,16,8,128]{3,2,1,0:T(8,128)S(1)} collective-permute-done((f32[8,16,8,128]{3,2,1,0:T(8,128)S(1)}, f32[8,16,8,128]{3,2,1,0:T(8,128)S(1)}, u32[]{:S(2)}, u32[]{:S(2)}) %collective-permute-start) | collective-permute-done | bytes 524320 | tf_op jit(solution)/shard_map/ppermute | solution.py:685
  22.3 0.0 collective-permute-done.3.high
  22.4 6.7 %outer.1 = (f32[16,22,8,128]{3,2,1,0:T(8,128)S(1)}, f32[25,16,8,128]{3,2,1,0:T(8,128)S(1)}, f32[25,16,8,128]{3,2,1,0:T(8,128)S(1)}, f32[25,16,8,128]{3,2,1,0:T(8,128)S(1)}) custom-call(f32[8,16,8,128]{3,2,1,0:T(8,128)S(1)} %collective-permute-done.low, ...), custom_call_target="tpu_custom_call", output_to_operand_aliasing={{1}: (2, {}), {2}: (3, {}), {3}: (4, {})} | custom-call | tf_op jit(solution)/shard_map/outer/pallas_call | solution.py:414
  29.0 27.6 %all_to_all.10.sent = f32[16,22,8,128]{3,2,1,0:T(8,128)S(1)} all-to-all(f32[16,22,8,128]{3,2,1,0:T(8,128)S(1)} %get-tuple-element.19), channel_id=1, replica_groups=mesh['tm'=16,'space'=32] {'tm'}, dimensions={0} | all-to-all | bytes 2883584 | tf_op jit(solution)/shard_map/all_to_all | solution.py:713
  56.7 0.1 pack.1
  56.8 2.6 %collective-permute-start.4 = (f32[84,8,128]{2,1,0:T(8,128)S(1)}, f32[84,8,128]{2,1,0:T(8,128)S(1)}, u32[]{:S(2)}, u32[]{:S(2)}) collective-permute-start(f32[84,8,128]{2,1,0:T(8,128)S(1)} %get-tuple-element.21), channel_id=1, source_target_pairs={{1,2},{3,4},{5,6},{7,8},{9,10},{11,12},{13,14},{15,16},{17,18},{19... | collective-permute-start | bytes 1032200 | tf_op jit(solution)/shard_map/ppermute | solution.py:685
  59.4 2.5 %collective-permute-start.5 = (f32[84,8,128]{2,1,0:T(8,128)S(1)}, f32[84,8,128]{2,1,0:T(8,128)S(1)}, u32[]{:S(2)}, u32[]{:S(2)}) collective-permute-start(f32[84,8,128]{2,1,0:T(8,128)S(1)} %get-tuple-element.22), channel_id=1, source_target_pairs={{0,1},{2,3},{4,5},{6,7},{8,9},{10,11},{12,13},{14,15},{16,17},{18,... | collective-permute-start | bytes 1032200 | tf_op jit(solution)/shard_map/ppermute | solution.py:690
  61.8 0.8 strip.1.eta
  62.6 4.0 %collective-permute-done.4.below = f32[84,8,128]{2,1,0:T(8,128)S(1)} collective-permute-done((f32[84,8,128]{2,1,0:T(8,128)S(1)}, f32[84,8,128]{2,1,0:T(8,128)S(1)}, u32[]{:S(2)}, u32[]{:S(2)}) %collective-permute-start.4) | collective-permute-done | bytes 344096 | tf_op jit(solution)/shard_map/ppermute | solution.py:685
  66.6 0.0 collective-permute-done.5.above
  66.6 2.3 %shard_map.39.done = f32[8,8,8,128]{3,2,1,0:T(8,128)S(1)} custom-call(f32[24,3,8,128]{3,2,1,0:T(8,128)S(1)} %strip.1.eta, f32[16,22,8,128]{3,2,1,0:T(8,128)S(1)} %all_to_all.10.sent, f32[16,2,8,128]{3,2,1,0:T(8,128)S(1)} %get-tuple-element.20.ends, f32[84,8,128]{2,1,0:T(8,128)S(1)} %collective-permute-done.4.below, ...), custom_call_target="tpu_custom_call" | custom-call | tf_op jit(solution)/shard_map/pallas_call | solution.py:643
  68.9 0.7 collective-permute-start.6
  69.6 4.5 %collective-permute-start.7 = (f32[8,8,128]{2,1,0:T(8,128)S(1)}, f32[8,8,128]{2,1,0:T(8,128)S(1)}, u32[]{:S(2)}, u32[]{:S(2)}) collective-permute-start(f32[8,8,128]{2,1,0:T(8,128)S(1)} %slice_bitcast_fusion), channel_id=1, source_target_pairs={{0,32},{64,96},{224,192},{160,128},{256,288},{320,352},{480,448},{... | collective-permute-start | bytes 98312 | tf_op jit(solution)/shard_map/ppermute | solution.py:697
  74.1 0.0 collective-permute-done.6
  74.1 1.3 %collective-permute-done.7 = f32[8,8,128]{2,1,0:T(8,128)S(1)} collective-permute-done((f32[8,8,128]{2,1,0:T(8,128)S(1)}, f32[8,8,128]{2,1,0:T(8,128)S(1)}, u32[]{:S(2)}, u32[]{:S(2)}) %collective-permute-start.7) | collective-permute-done | bytes 32800 | tf_op jit(solution)/shard_map/ppermute | solution.py:697
  75.4 3.2 %collective-permute-start.8 = (f32[8,24,128]{2,1,0:T(8,128)S(1)}, f32[8,24,128]{2,1,0:T(8,128)S(1)}, u32[]{:S(2)}, u32[]{:S(2)}) collective-permute-start(f32[8,24,128]{2,1,0:T(8,128)S(1)} %pad_maximum_fusion.own_u), channel_id=1, source_target_pairs={{1,2},{3,4},{5,6},{7,8},{9,10},{11,12},{13,14},{15,16},{17,18},{19... | collective-permute-start | bytes 294920 | tf_op jit(solution)/shard_map/ppermute | solution.py:685
  78.6 1.9 %collective-permute-start.9 = (f32[8,24,128]{2,1,0:T(8,128)S(1)}, f32[8,24,128]{2,1,0:T(8,128)S(1)}, u32[]{:S(2)}, u32[]{:S(2)}) collective-permute-start(f32[8,24,128]{2,1,0:T(8,128)S(1)} %pad_maximum_fusion.own_u), channel_id=1, source_target_pairs={{0,1},{2,3},{4,5},{6,7},{8,9},{10,11},{12,13},{14,15},{16,17},{18,... | collective-permute-start | bytes 294920 | tf_op jit(solution)/shard_map/ppermute | solution.py:690
  80.5 2.0 %collective-permute-done.8.low_u = f32[8,24,128]{2,1,0:T(8,128)S(1)} collective-permute-done((f32[8,24,128]{2,1,0:T(8,128)S(1)}, f32[8,24,128]{2,1,0:T(8,128)S(1)}, u32[]{:S(2)}, u32[]{:S(2)}) %collective-permute-start.8) | collective-permute-done | bytes 98336 | tf_op jit(solution)/shard_map/ppermute | solution.py:685
  82.6 0.0 collective-permute-done.9.high_u
  82.6 2.8 %shard_map.40 = f32[16,8,8,128]{3,2,1,0:T(8,128)S(1)} custom-call(f32[24,3,8,128]{3,2,1,0:T(8,128)S(1)} %strip.1.eta, f32[16,22,8,128]{3,2,1,0:T(8,128)S(1)} %all_to_all.10.sent, f32[16,2,8,128]{3,2,1,0:T(8,128)S(1)} %get-tuple-element.20.ends, f32[84,8,128]{2,1,0:T(8,128)S(1)} %collective-permute-done.4.below, ...), custom_call_target="tpu_custom_call" | custom-call | tf_op jit(solution)/shard_map/pallas_call | solution.py:643
  85.3 17.2 %all_to_all.11.strips = f32[16,8,8,128]{3,2,1,0:T(8,128)S(1)} all-to-all(f32[16,8,8,128]{3,2,1,0:T(8,128)S(1)} %shard_map.40), channel_id=1, replica_groups=mesh['tm'=16,'space'=32] {'tm'}, dimensions={0} | all-to-all | bytes 1048576 | tf_op jit(solution)/shard_map/all_to_all | solution.py:723
  102.5 0.9 place.1
  (3 shorter events, 0.0 us)
Async XLA Ops:
  1.7 13.9 %collective-permute-start.1 = (f32[8,16,8,128]{3,2,1,0:T(8,128)S(1)}, f32[8,16,8,128]{3,2,1,0:T(8,128)S(1)}, u32[]{:S(2)}, u32[]{:S(2)}) collective-permute-start(f32[8,16,8,128]{3,2,1,0:T(8,128)S(1)} %shard_map.38.own_a), channel_id=1, source_target_pairs={{1,2},{3,4},{5,6},{7,8},{9,10},{11,12},{13,14},{15,16},{17,18},{19... | collective-permute-start | bytes 1572872 | tf_op jit(solution)/shard_map/ppermute | solution.py:685
  8.7 6.9 %collective-permute-start.2 = (f32[8,16,8,128]{3,2,1,0:T(8,128)S(1)}, f32[8,16,8,128]{3,2,1,0:T(8,128)S(1)}, u32[]{:S(2)}, u32[]{:S(2)}) collective-permute-start(f32[8,16,8,128]{3,2,1,0:T(8,128)S(1)} %shard_map.37.own_b), channel_id=1, source_target_pairs={{0,1},{2,3},{4,5},{6,7},{8,9},{10,11},{12,13},{14,15},{16,17},{18,... | collective-permute-start | bytes 1572872 | tf_op jit(solution)/shard_map/ppermute | solution.py:690
  10.6 11.7 %collective-permute-start = (f32[8,16,8,128]{3,2,1,0:T(8,128)S(1)}, f32[8,16,8,128]{3,2,1,0:T(8,128)S(1)}, u32[]{:S(2)}, u32[]{:S(2)}) collective-permute-start(f32[8,16,8,128]{3,2,1,0:T(8,128)S(1)} %shard_map.37.own_b), channel_id=1, source_target_pairs={{1,2},{3,4},{5,6},{7,8},{9,10},{11,12},{13,14},{15,16},{17,18},{19... | collective-permute-start | bytes 1572872 | tf_op jit(solution)/shard_map/ppermute | solution.py:685
  13.7 8.7 %collective-permute-start.3 = (f32[8,16,8,128]{3,2,1,0:T(8,128)S(1)}, f32[8,16,8,128]{3,2,1,0:T(8,128)S(1)}, u32[]{:S(2)}, u32[]{:S(2)}) collective-permute-start(f32[8,16,8,128]{3,2,1,0:T(8,128)S(1)} %shard_map.38.own_a), channel_id=1, source_target_pairs={{0,1},{2,3},{4,5},{6,7},{8,9},{10,11},{12,13},{14,15},{16,17},{18,... | collective-permute-start | bytes 1572872 | tf_op jit(solution)/shard_map/ppermute | solution.py:690
  56.8 9.8 %collective-permute-start.4 = (f32[84,8,128]{2,1,0:T(8,128)S(1)}, f32[84,8,128]{2,1,0:T(8,128)S(1)}, u32[]{:S(2)}, u32[]{:S(2)}) collective-permute-start(f32[84,8,128]{2,1,0:T(8,128)S(1)} %get-tuple-element.21), channel_id=1, source_target_pairs={{1,2},{3,4},{5,6},{7,8},{9,10},{11,12},{13,14},{15,16},{17,18},{19... | collective-permute-start | bytes 1032200 | tf_op jit(solution)/shard_map/ppermute | solution.py:685
  59.4 7.2 %collective-permute-start.5 = (f32[84,8,128]{2,1,0:T(8,128)S(1)}, f32[84,8,128]{2,1,0:T(8,128)S(1)}, u32[]{:S(2)}, u32[]{:S(2)}) collective-permute-start(f32[84,8,128]{2,1,0:T(8,128)S(1)} %get-tuple-element.22), channel_id=1, source_target_pairs={{0,1},{2,3},{4,5},{6,7},{8,9},{10,11},{12,13},{14,15},{16,17},{18,... | collective-permute-start | bytes 1032200 | tf_op jit(solution)/shard_map/ppermute | solution.py:690
  68.9 5.2 %collective-permute-start.6 = (f32[8,8,128]{2,1,0:T(8,128)S(1)}, f32[8,8,128]{2,1,0:T(8,128)S(1)}, u32[]{:S(2)}, u32[]{:S(2)}) collective-permute-start(f32[8,8,128]{2,1,0:T(8,128)S(1)} %slice_bitcast_fusion), channel_id=1, source_target_pairs={{32,64},{96,224},{192,160},{128,256},{288,320},{352,480},{448,416}... | collective-permute-start | bytes 98312 | tf_op jit(solution)/shard_map/ppermute | solution.py:697
  69.6 5.8 %collective-permute-start.7 = (f32[8,8,128]{2,1,0:T(8,128)S(1)}, f32[8,8,128]{2,1,0:T(8,128)S(1)}, u32[]{:S(2)}, u32[]{:S(2)}) collective-permute-start(f32[8,8,128]{2,1,0:T(8,128)S(1)} %slice_bitcast_fusion), channel_id=1, source_target_pairs={{0,32},{64,96},{224,192},{160,128},{256,288},{320,352},{480,448},{... | collective-permute-start | bytes 98312 | tf_op jit(solution)/shard_map/ppermute | solution.py:697
  75.4 7.1 %collective-permute-start.8 = (f32[8,24,128]{2,1,0:T(8,128)S(1)}, f32[8,24,128]{2,1,0:T(8,128)S(1)}, u32[]{:S(2)}, u32[]{:S(2)}) collective-permute-start(f32[8,24,128]{2,1,0:T(8,128)S(1)} %pad_maximum_fusion.own_u), channel_id=1, source_target_pairs={{1,2},{3,4},{5,6},{7,8},{9,10},{11,12},{13,14},{15,16},{17,18},{19... | collective-permute-start | bytes 294920 | tf_op jit(solution)/shard_map/ppermute | solution.py:685
  78.6 4.0 %collective-permute-start.9 = (f32[8,24,128]{2,1,0:T(8,128)S(1)}, f32[8,24,128]{2,1,0:T(8,128)S(1)}, u32[]{:S(2)}, u32[]{:S(2)}) collective-permute-start(f32[8,24,128]{2,1,0:T(8,128)S(1)} %pad_maximum_fusion.own_u), channel_id=1, source_target_pairs={{0,1},{2,3},{4,5},{6,7},{8,9},{10,11},{12,13},{14,15},{16,17},{18,... | collective-permute-start | bytes 294920 | tf_op jit(solution)/shard_map/ppermute | solution.py:690

commit v12 on v11

--- a/solution.py
+++ b/solution.py
@@ -1,5 +1,3 @@
-import functools
-
 import jax
 import jax.numpy as jnp
 from jax import lax
@@ -143,20 +141,8 @@
     return jnp.where(lax.axis_index("space") < 0, 2, 1)
 
 
-def own_kernel(h, start, regions, resistivity, out, *refs):
-    start_v, regions_v, half_v, resistivity_s, sems = refs
+def convert(start_v, regions_v, scaled, half_v, out):
     odd = is_mirrored()
-    part = pl.ds(jnp.where(odd, 1 - h, h) * HALF, HALF)
-    copies = (
-        pltpu.make_async_copy(resistivity, resistivity_s, sems.at[0]),
-        pltpu.make_async_copy(start.at[part], start_v, sems.at[1]),
-        pltpu.make_async_copy(regions.at[part], regions_v, sems.at[2]),
-    )
-    for copy in copies:
-        copy.start()
-    for copy in copies:
-        copy.wait()
-    scaled = [resistivity_s[i] * jnp.float32(0.5 * fine_step) for i in range(REGIONS)]
 
     def first_pass(_, carry):
         for x in range(HALF):
@@ -184,23 +170,74 @@
     lax.fori_loop(0, 2, second_pass, 0)
 
 
-def own_part(h, start, regions, resistivity):
-    hbm = pl.BlockSpec(memory_space=HBM)
+def near_kernel(
+    start, regions, resistivity, out, start_far, regions_far, table,
+    start_v, regions_v, half_v, resistivity_s, sems,
+):
+    odd = is_mirrored()
+    near, far = [pl.ds(jnp.where(odd, 1 - h, h) * HALF, HALF) for h in range(2)]
+    copies = (
+        pltpu.make_async_copy(resistivity, resistivity_s, sems.at[0]),
+        pltpu.make_async_copy(start.at[near], start_v, sems.at[1]),
+        pltpu.make_async_copy(regions.at[near], regions_v, sems.at[2]),
+        pltpu.make_async_copy(start.at[far], start_far, sems.at[3]),
+        pltpu.make_async_copy(regions.at[far], regions_far, sems.at[4]),
+    )
+    for copy in copies:
+        copy.start()
+    for copy in copies[:3]:
+        copy.wait()
+    scaled = [resistivity_s[i] * jnp.float32(0.5 * fine_step) for i in range(REGIONS)]
+    for i in range(REGIONS):
+        table[i] = jnp.full((8, NZ), scaled[i], jnp.float32)
+    convert(start_v, regions_v, scaled, half_v, out)
+    for copy in copies[3:]:
+        copy.wait()
+
+
+def far_kernel(start_v, regions_v, table, out, half_v):
+    convert(start_v, regions_v, [table[i] for i in range(REGIONS)], half_v, out)
+
+
+TILED = jax.ShapeDtypeStruct((2 * HALF, PARTS, 8, NZ), jnp.float32)
+
+
+def near_half(start, regions, resistivity):
+    f32 = jnp.float32
+    shape = (HALF, NY, NZ)
     return pl.pallas_call(
-        functools.partial(own_kernel, h),
-        out_shape=jax.ShapeDtypeStruct((2 * HALF, PARTS, 8, NZ), jnp.float32),
-        in_specs=[hbm] * 3,
-        out_specs=VMEM,
+        near_kernel,
+        out_shape=(
+            TILED,
+            jax.ShapeDtypeStruct(shape, f32),
+            jax.ShapeDtypeStruct(shape, jnp.int32),
+            jax.ShapeDtypeStruct((REGIONS, 8, NZ), f32),
+        ),
+        in_specs=[pl.BlockSpec(memory_space=HBM)] * 3,
+        out_specs=(VMEM,) * 4,
         scratch_shapes=[
-            pltpu.VMEM((HALF, NY, NZ), jnp.float32),
-            pltpu.VMEM((HALF, NY, NZ), jnp.int32),
-            pltpu.VMEM((2 * HALF, PARTS, 8, NZ), jnp.float32),
-            pltpu.SMEM((REGIONS,), jnp.float32),
-            pltpu.SemaphoreType.DMA((3,)),
+            pltpu.VMEM(shape, f32),
+            pltpu.VMEM(shape, jnp.int32),
+            pltpu.VMEM(TILED.shape, f32),
+            pltpu.SMEM((REGIONS,), f32),
+            pltpu.SemaphoreType.DMA((5,)),
         ],
         compiler_params=pltpu.CompilerParams(vmem_limit_bytes=8 << 20),
+        name="near",
+    )(*(pltpu.with_memory_space_constraint(a, HBM) for a in (start, regions, resistivity)))
+
+
+def far_half(start, regions, table):
+    return pl.pallas_call(
+        far_kernel,
+        out_shape=TILED,
+        in_specs=[VMEM] * 3,
+        out_specs=VMEM,
+        scratch_shapes=[pltpu.VMEM(TILED.shape, jnp.float32)],
+        compiler_params=pltpu.CompilerParams(vmem_limit_bytes=8 << 20),
         cost_estimate=pl.CostEstimate(flops=10**6, bytes_accessed=10**6, transcendentals=0),
-    )(*(pltpu.with_memory_space_constraint(a, HBM) for a in (start, regions, resistivity)))
+        name="far",
+    )(start, regions, table)
 
 
 class Fine:
@@ -702,10 +739,9 @@
 
 
 def per_device(start_values, regions, resistivity):
-    args = (start_values[0], regions, resistivity)
-    own_a = own_part(0, *args)
+    own_a, *rest = near_half(start_values[0], regions, resistivity)
     low_near = across(own_a)
-    own_b = own_part(1, *args)
+    own_b = far_half(*rest)
     low_far = across(own_b)
     high_near = beside(own_b)
     high_far = beside(own_a)

time: 104 us -> 103 us (level)
    pallas_call x2, Pallas kernels: 3.37 us -> 2.32 us  [the longest x1 1.7 us: near_half(): pl.pallas_call(near_kernel, out_shape=(TILED, jax.ShapeDtypeStruct(shape,...]
  transfers between devices with their start and end apart: 10 -> 10, of which waited for: 4 -> 4; matrix products, arithmetic and copies ran while one was open for 0% -> 0% of each run, Pallas kernels for 6% -> 5%
where the time goes in v12:
time: 103 us; the launch traced here: 102 us
  blocking collectives  44.8 us (43%)
  starting transfers between devices  27.5 us (27%)
  Pallas kernels  19.6 us (19%)
  waiting for transfers between devices  10.3 us (10%)
    all_to_all x1, blocking collectives, per_device(): sent = lax.all_to_all(sent, 'tm', 0, 0)  27.6 us
    all_to_all x1, blocking collectives, per_device(): result = lax.all_to_all(ends, 'tm', 0, 0)  17.2 us
    ppermute x4, starting transfers between devices, across(): return lax.ppermute(value, 'space', pairs + [(b, a) for a, b in pairs])  14.1 us
    ppermute x4, waiting for transfers between devices, across(): return lax.ppermute(value, 'space', pairs + [(b, a) for a, b in pairs])  9 us
    ppermute x4, starting transfers between devices, beside(): return lax.ppermute(value, 'space', pairs + [(b, a) for a, b in pairs])  8.22 us
    pallas_call x1, Pallas kernels, outer(): pl.pallas_call(outer_kernel, out_shape=(jax.ShapeDtypeStruct((SLICES, LOA...  6.66 us
    ppermute x2, starting transfers between devices, with_strips(): sides.append(lax.ppermute(state, 'tm', pairs + [(b, a) for a, b in pairs]))  5.15 us
    pallas_call x2, Pallas kernels, coarse_call(): pl.pallas_call(kernel, out_shape=jax.ShapeDtypeStruct((count, BX, ROWS, N...  5.05 us
  transfers between devices with their start and end apart: 10, of which 4 were waited for; matrix products, arithmetic and copies ran while one was open for 0% of the time, Pallas kernels for 5%

profile of v12, /device:TPU:225, one launch (start us, length us, event | category | flops | bytes accessed | tf_op | source)
XLA Modules:
  0.0 102.4 jit_solution(17740826257731043894)
XLA Ops:
  0.0 1.7 %near.1 = (f32[8,16,8,128]{3,2,1,0:T(8,128)S(1)}, f32[4,128,128]{2,1,0:T(8,128)S(1)}, s32[4,128,128]{2,1,0:T(8,128)S(1)}, f32[4,8,128]{2,1,0:T(8,128)S(1)}) custom-call(f32[8,128,128]{2,1,0:T(8,128)} %bitcast.16, s32[8,128,128]{2,1,0:T(8,128)} %regions.1, f32[4]{0:T(128)} %resistivity.1), custom_call_target="tpu_custom_call" | custom-call | tf_op jit(solution)/shard_map/near/pallas_call | solution.py:208
  1.7 5.3 %collective-permute-start.1 = (f32[8,16,8,128]{3,2,1,0:T(8,128)S(1)}, f32[8,16,8,128]{3,2,1,0:T(8,128)S(1)}, u32[]{:S(2)}, u32[]{:S(2)}) collective-permute-start(f32[8,16,8,128]{3,2,1,0:T(8,128)S(1)} %get-tuple-element.21.own_a), channel_id=1, source_target_pairs={{1,2},{3,4},{5,6},{7,8},{9,10},{11,12},{13,14},{15,16},{17,18},{19... | collective-permute-start | bytes 1572872 | tf_op jit(solution)/shard_map/ppermute | solution.py:722
  7.0 0.6 far.1.own_b
  7.7 1.9 %collective-permute-start.2 = (f32[8,16,8,128]{3,2,1,0:T(8,128)S(1)}, f32[8,16,8,128]{3,2,1,0:T(8,128)S(1)}, u32[]{:S(2)}, u32[]{:S(2)}) collective-permute-start(f32[8,16,8,128]{3,2,1,0:T(8,128)S(1)} %far.1.own_b), channel_id=1, source_target_pairs={{0,1},{2,3},{4,5},{6,7},{8,9},{10,11},{12,13},{14,15},{16,17},{18,... | collective-permute-start | bytes 1572872 | tf_op jit(solution)/shard_map/ppermute | solution.py:727
  9.6 3.0 %collective-permute-start = (f32[8,16,8,128]{3,2,1,0:T(8,128)S(1)}, f32[8,16,8,128]{3,2,1,0:T(8,128)S(1)}, u32[]{:S(2)}, u32[]{:S(2)}) collective-permute-start(f32[8,16,8,128]{3,2,1,0:T(8,128)S(1)} %far.1.own_b), channel_id=1, source_target_pairs={{1,2},{3,4},{5,6},{7,8},{9,10},{11,12},{13,14},{15,16},{17,18},{19... | collective-permute-start | bytes 1572872 | tf_op jit(solution)/shard_map/ppermute | solution.py:722
  12.6 1.9 %collective-permute-start.3 = (f32[8,16,8,128]{3,2,1,0:T(8,128)S(1)}, f32[8,16,8,128]{3,2,1,0:T(8,128)S(1)}, u32[]{:S(2)}, u32[]{:S(2)}) collective-permute-start(f32[8,16,8,128]{3,2,1,0:T(8,128)S(1)} %get-tuple-element.21.own_a), channel_id=1, source_target_pairs={{0,1},{2,3},{4,5},{6,7},{8,9},{10,11},{12,13},{14,15},{16,17},{18,... | collective-permute-start | bytes 1572872 | tf_op jit(solution)/shard_map/ppermute | solution.py:727
  14.6 0.0 collective-permute-done.1.low
  14.6 0.0 collective-permute-done.2.high
  14.6 3.7 %inner.1 = (f32[25,16,8,128]{3,2,1,0:T(8,128)S(1)}, f32[25,16,8,128]{3,2,1,0:T(8,128)S(1)}, f32[25,16,8,128]{3,2,1,0:T(8,128)S(1)}, f32[16,16,8,128]{3,2,1,0:T(8,128)S(1)}, f32[4,5,16,8,128]{4,3,2,1,0:T(8,128)S(1)}) custom-call(f32[8,16,8,128]{3,2,1,0:T(8,128)S(1)} %collective-permute-done.1.low, f32[8,16,8,128]{3,2,1,0:T(8,128)S(1)} %get-tuple-element.21.own_a, ...), custom_call_target="tpu_custom_call" | custom-call | flops 100000000 | bytes 10000000 | tf_op jit(solution)/shard_map/inner/pallas_call | solution.py:431
  18.3 3.0 %collective-permute-done.low = f32[8,16,8,128]{3,2,1,0:T(8,128)S(1)} collective-permute-done((f32[8,16,8,128]{3,2,1,0:T(8,128)S(1)}, f32[8,16,8,128]{3,2,1,0:T(8,128)S(1)}, u32[]{:S(2)}, u32[]{:S(2)}) %collective-permute-start) | collective-permute-done | bytes 524320 | tf_op jit(solution)/shard_map/ppermute | solution.py:722
  21.3 0.0 collective-permute-done.3.high
  21.3 6.7 %outer.1 = (f32[16,22,8,128]{3,2,1,0:T(8,128)S(1)}, f32[25,16,8,128]{3,2,1,0:T(8,128)S(1)}, f32[25,16,8,128]{3,2,1,0:T(8,128)S(1)}, f32[25,16,8,128]{3,2,1,0:T(8,128)S(1)}) custom-call(f32[8,16,8,128]{3,2,1,0:T(8,128)S(1)} %collective-permute-done.low, ...), custom_call_target="tpu_custom_call", output_to_operand_aliasing={{1}: (2, {}), {2}: (3, {}), {3}: (4, {})} | custom-call | tf_op jit(solution)/shard_map/outer/pallas_call | solution.py:451
  28.0 27.6 %all_to_all.10.sent = f32[16,22,8,128]{3,2,1,0:T(8,128)S(1)} all-to-all(f32[16,22,8,128]{3,2,1,0:T(8,128)S(1)} %get-tuple-element.27), channel_id=1, replica_groups=mesh['tm'=16,'space'=32] {'tm'}, dimensions={0} | all-to-all | bytes 2883584 | tf_op jit(solution)/shard_map/all_to_all | solution.py:749
  55.6 0.1 pack.1
  55.7 2.6 %collective-permute-start.4 = (f32[84,8,128]{2,1,0:T(8,128)S(1)}, f32[84,8,128]{2,1,0:T(8,128)S(1)}, u32[]{:S(2)}, u32[]{:S(2)}) collective-permute-start(f32[84,8,128]{2,1,0:T(8,128)S(1)} %get-tuple-element.29), channel_id=1, source_target_pairs={{1,2},{3,4},{5,6},{7,8},{9,10},{11,12},{13,14},{15,16},{17,18},{19... | collective-permute-start | bytes 1032200 | tf_op jit(solution)/shard_map/ppermute | solution.py:722
  58.3 2.5 %collective-permute-start.5 = (f32[84,8,128]{2,1,0:T(8,128)S(1)}, f32[84,8,128]{2,1,0:T(8,128)S(1)}, u32[]{:S(2)}, u32[]{:S(2)}) collective-permute-start(f32[84,8,128]{2,1,0:T(8,128)S(1)} %get-tuple-element.30), channel_id=1, source_target_pairs={{0,1},{2,3},{4,5},{6,7},{8,9},{10,11},{12,13},{14,15},{16,17},{18,... | collective-permute-start | bytes 1032200 | tf_op jit(solution)/shard_map/ppermute | solution.py:727
  60.8 0.8 strip.1.eta
  61.6 4.0 %collective-permute-done.4.below = f32[84,8,128]{2,1,0:T(8,128)S(1)} collective-permute-done((f32[84,8,128]{2,1,0:T(8,128)S(1)}, f32[84,8,128]{2,1,0:T(8,128)S(1)}, u32[]{:S(2)}, u32[]{:S(2)}) %collective-permute-start.4) | collective-permute-done | bytes 344096 | tf_op jit(solution)/shard_map/ppermute | solution.py:722
  65.5 0.0 collective-permute-done.5.above
  65.5 2.3 %shard_map.37.done = f32[8,8,8,128]{3,2,1,0:T(8,128)S(1)} custom-call(f32[24,3,8,128]{3,2,1,0:T(8,128)S(1)} %strip.1.eta, f32[16,22,8,128]{3,2,1,0:T(8,128)S(1)} %all_to_all.10.sent, f32[16,2,8,128]{3,2,1,0:T(8,128)S(1)} %get-tuple-element.28.ends, f32[84,8,128]{2,1,0:T(8,128)S(1)} %collective-permute-done.4.below, ...), custom_call_target="tpu_custom_call" | custom-call | tf_op jit(solution)/shard_map/pallas_call | solution.py:680
  67.8 0.7 collective-permute-start.6
  68.5 4.5 %collective-permute-start.7 = (f32[8,8,128]{2,1,0:T(8,128)S(1)}, f32[8,8,128]{2,1,0:T(8,128)S(1)}, u32[]{:S(2)}, u32[]{:S(2)}) collective-permute-start(f32[8,8,128]{2,1,0:T(8,128)S(1)} %slice_bitcast_fusion), channel_id=1, source_target_pairs={{0,32},{64,96},{224,192},{160,128},{256,288},{320,352},{480,448},{... | collective-permute-start | bytes 98312 | tf_op jit(solution)/shard_map/ppermute | solution.py:734
  73.0 0.0 collective-permute-done.6
  73.0 1.3 %collective-permute-done.7 = f32[8,8,128]{2,1,0:T(8,128)S(1)} collective-permute-done((f32[8,8,128]{2,1,0:T(8,128)S(1)}, f32[8,8,128]{2,1,0:T(8,128)S(1)}, u32[]{:S(2)}, u32[]{:S(2)}) %collective-permute-start.7) | collective-permute-done | bytes 32800 | tf_op jit(solution)/shard_map/ppermute | solution.py:734
  74.4 3.2 %collective-permute-start.8 = (f32[8,24,128]{2,1,0:T(8,128)S(1)}, f32[8,24,128]{2,1,0:T(8,128)S(1)}, u32[]{:S(2)}, u32[]{:S(2)}) collective-permute-start(f32[8,24,128]{2,1,0:T(8,128)S(1)} %pad_maximum_fusion.own_u), channel_id=1, source_target_pairs={{1,2},{3,4},{5,6},{7,8},{9,10},{11,12},{13,14},{15,16},{17,18},{19... | collective-permute-start | bytes 294920 | tf_op jit(solution)/shard_map/ppermute | solution.py:722
  77.6 1.9 %collective-permute-start.9 = (f32[8,24,128]{2,1,0:T(8,128)S(1)}, f32[8,24,128]{2,1,0:T(8,128)S(1)}, u32[]{:S(2)}, u32[]{:S(2)}) collective-permute-start(f32[8,24,128]{2,1,0:T(8,128)S(1)} %pad_maximum_fusion.own_u), channel_id=1, source_target_pairs={{0,1},{2,3},{4,5},{6,7},{8,9},{10,11},{12,13},{14,15},{16,17},{18,... | collective-permute-start | bytes 294920 | tf_op jit(solution)/shard_map/ppermute | solution.py:727
  79.5 2.0 %collective-permute-done.8.low_u = f32[8,24,128]{2,1,0:T(8,128)S(1)} collective-permute-done((f32[8,24,128]{2,1,0:T(8,128)S(1)}, f32[8,24,128]{2,1,0:T(8,128)S(1)}, u32[]{:S(2)}, u32[]{:S(2)}) %collective-permute-start.8) | collective-permute-done | bytes 98336 | tf_op jit(solution)/shard_map/ppermute | solution.py:722
  81.5 0.0 collective-permute-done.9.high_u
  81.5 2.8 %shard_map.38 = f32[16,8,8,128]{3,2,1,0:T(8,128)S(1)} custom-call(f32[24,3,8,128]{3,2,1,0:T(8,128)S(1)} %strip.1.eta, f32[16,22,8,128]{3,2,1,0:T(8,128)S(1)} %all_to_all.10.sent, f32[16,2,8,128]{3,2,1,0:T(8,128)S(1)} %get-tuple-element.28.ends, f32[84,8,128]{2,1,0:T(8,128)S(1)} %collective-permute-done.4.below, ...), custom_call_target="tpu_custom_call" | custom-call | tf_op jit(solution)/shard_map/pallas_call | solution.py:680
  84.3 17.2 %all_to_all.11.strips = f32[16,8,8,128]{3,2,1,0:T(8,128)S(1)} all-to-all(f32[16,8,8,128]{3,2,1,0:T(8,128)S(1)} %shard_map.38), channel_id=1, replica_groups=mesh['tm'=16,'space'=32] {'tm'}, dimensions={0} | all-to-all | bytes 1048576 | tf_op jit(solution)/shard_map/all_to_all | solution.py:759
  101.5 0.9 place.1
  (3 shorter events, 0.0 us)
Async XLA Ops:
  1.7 12.9 %collective-permute-start.1 = (f32[8,16,8,128]{3,2,1,0:T(8,128)S(1)}, f32[8,16,8,128]{3,2,1,0:T(8,128)S(1)}, u32[]{:S(2)}, u32[]{:S(2)}) collective-permute-start(f32[8,16,8,128]{3,2,1,0:T(8,128)S(1)} %get-tuple-element.21.own_a), channel_id=1, source_target_pairs={{1,2},{3,4},{5,6},{7,8},{9,10},{11,12},{13,14},{15,16},{17,18},{19... | collective-permute-start | bytes 1572872 | tf_op jit(solution)/shard_map/ppermute | solution.py:722
  7.7 6.9 %collective-permute-start.2 = (f32[8,16,8,128]{3,2,1,0:T(8,128)S(1)}, f32[8,16,8,128]{3,2,1,0:T(8,128)S(1)}, u32[]{:S(2)}, u32[]{:S(2)}) collective-permute-start(f32[8,16,8,128]{3,2,1,0:T(8,128)S(1)} %far.1.own_b), channel_id=1, source_target_pairs={{0,1},{2,3},{4,5},{6,7},{8,9},{10,11},{12,13},{14,15},{16,17},{18,... | collective-permute-start | bytes 1572872 | tf_op jit(solution)/shard_map/ppermute | solution.py:727
  9.6 11.7 %collective-permute-start = (f32[8,16,8,128]{3,2,1,0:T(8,128)S(1)}, f32[8,16,8,128]{3,2,1,0:T(8,128)S(1)}, u32[]{:S(2)}, u32[]{:S(2)}) collective-permute-start(f32[8,16,8,128]{3,2,1,0:T(8,128)S(1)} %far.1.own_b), channel_id=1, source_target_pairs={{1,2},{3,4},{5,6},{7,8},{9,10},{11,12},{13,14},{15,16},{17,18},{19... | collective-permute-start | bytes 1572872 | tf_op jit(solution)/shard_map/ppermute | solution.py:722
  12.6 8.7 %collective-permute-start.3 = (f32[8,16,8,128]{3,2,1,0:T(8,128)S(1)}, f32[8,16,8,128]{3,2,1,0:T(8,128)S(1)}, u32[]{:S(2)}, u32[]{:S(2)}) collective-permute-start(f32[8,16,8,128]{3,2,1,0:T(8,128)S(1)} %get-tuple-element.21.own_a), channel_id=1, source_target_pairs={{0,1},{2,3},{4,5},{6,7},{8,9},{10,11},{12,13},{14,15},{16,17},{18,... | collective-permute-start | bytes 1572872 | tf_op jit(solution)/shard_map/ppermute | solution.py:727
  55.7 9.8 %collective-permute-start.4 = (f32[84,8,128]{2,1,0:T(8,128)S(1)}, f32[84,8,128]{2,1,0:T(8,128)S(1)}, u32[]{:S(2)}, u32[]{:S(2)}) collective-permute-start(f32[84,8,128]{2,1,0:T(8,128)S(1)} %get-tuple-element.29), channel_id=1, source_target_pairs={{1,2},{3,4},{5,6},{7,8},{9,10},{11,12},{13,14},{15,16},{17,18},{19... | collective-permute-start | bytes 1032200 | tf_op jit(solution)/shard_map/ppermute | solution.py:722
  58.3 7.2 %collective-permute-start.5 = (f32[84,8,128]{2,1,0:T(8,128)S(1)}, f32[84,8,128]{2,1,0:T(8,128)S(1)}, u32[]{:S(2)}, u32[]{:S(2)}) collective-permute-start(f32[84,8,128]{2,1,0:T(8,128)S(1)} %get-tuple-element.30), channel_id=1, source_target_pairs={{0,1},{2,3},{4,5},{6,7},{8,9},{10,11},{12,13},{14,15},{16,17},{18,... | collective-permute-start | bytes 1032200 | tf_op jit(solution)/shard_map/ppermute | solution.py:727
  67.8 5.2 %collective-permute-start.6 = (f32[8,8,128]{2,1,0:T(8,128)S(1)}, f32[8,8,128]{2,1,0:T(8,128)S(1)}, u32[]{:S(2)}, u32[]{:S(2)}) collective-permute-start(f32[8,8,128]{2,1,0:T(8,128)S(1)} %slice_bitcast_fusion), channel_id=1, source_target_pairs={{32,64},{96,224},{192,160},{128,256},{288,320},{352,480},{448,416}... | collective-permute-start | bytes 98312 | tf_op jit(solution)/shard_map/ppermute | solution.py:734
  68.5 5.8 %collective-permute-start.7 = (f32[8,8,128]{2,1,0:T(8,128)S(1)}, f32[8,8,128]{2,1,0:T(8,128)S(1)}, u32[]{:S(2)}, u32[]{:S(2)}) collective-permute-start(f32[8,8,128]{2,1,0:T(8,128)S(1)} %slice_bitcast_fusion), channel_id=1, source_target_pairs={{0,32},{64,96},{224,192},{160,128},{256,288},{320,352},{480,448},{... | collective-permute-start | bytes 98312 | tf_op jit(solution)/shard_map/ppermute | solution.py:734
  74.4 7.1 %collective-permute-start.8 = (f32[8,24,128]{2,1,0:T(8,128)S(1)}, f32[8,24,128]{2,1,0:T(8,128)S(1)}, u32[]{:S(2)}, u32[]{:S(2)}) collective-permute-start(f32[8,24,128]{2,1,0:T(8,128)S(1)} %pad_maximum_fusion.own_u), channel_id=1, source_target_pairs={{1,2},{3,4},{5,6},{7,8},{9,10},{11,12},{13,14},{15,16},{17,18},{19... | collective-permute-start | bytes 294920 | tf_op jit(solution)/shard_map/ppermute | solution.py:722
  77.6 4.0 %collective-permute-start.9 = (f32[8,24,128]{2,1,0:T(8,128)S(1)}, f32[8,24,128]{2,1,0:T(8,128)S(1)}, u32[]{:S(2)}, u32[]{:S(2)}) collective-permute-start(f32[8,24,128]{2,1,0:T(8,128)S(1)} %pad_maximum_fusion.own_u), channel_id=1, source_target_pairs={{0,1},{2,3},{4,5},{6,7},{8,9},{10,11},{12,13},{14,15},{16,17},{18,... | collective-permute-start | bytes 294920 | tf_op jit(solution)/shard_map/ppermute | solution.py:727
